TPU v7x, 32 devices: a whole 2x2x4 slice. The times are simulated.
32 devices in a mesh: dp: 8 (over z, y), seq: 4 (over x, core).
Axes of the slice: x: 2, y: 2, z: 4, core: 2. Of those that a mesh axis runs over, the one named last changes fastest.
Arguments:
- tokens: bfloat16 [8192, 768], P(('dp', 'seq')), may hold values from -6 to 6
- ln1_gain: bfloat16 [768], P('dp'), may hold values from 0.25 to 1.75
- w_qkv: bfloat16 [768, 2304], P('dp'), may hold values from -0.21875 to 0.21875
- w_out: bfloat16 [768, 768], P('dp'), may hold values from -1.75 to 1.75
- w_ada: bfloat16 [768, 2304], P('dp'), may hold values from -0.21875 to 0.21875
- w_up: bfloat16 [768, 3072], P('dp'), may hold values from -0.21875 to 0.21875
- w_down: bfloat16 [3072, 768], P('dp'), may hold values from -0.109375 to 0.109375
- out_grad: bfloat16 [8192, 768], P(('dp', 'seq')), may hold values from -6 to 6
- layout: int32 [8, 2], P('dp'), may hold values from 256 to 896, as said below
- timestep: int32 [8], P('dp'), may hold values from 0 to 999
Outputs:
- layer_out: bfloat16 [8192, 768], P(('dp', 'seq'))
- input_grad: bfloat16 [8192, 768], P(('dp', 'seq'))
- gain_grad: float32 [768], P('dp')
- qkv_weight_grad: float32 [768, 2304], P('dp')
- out_weight_grad: float32 [768, 768], P('dp')
- ada_weight_grad: float32 [768, 2304], P('dp')
- up_weight_grad: float32 [768, 3072], P('dp')
- down_weight_grad: float32 [3072, 768], P('dp')
Inputs may be any that keep to these rules, and one draw needn't show every extreme that they name: layout[g] = (P, C): tokens below P are the prompt, the first continuation runs from P to C - 1, the second from C to 1023; P lies between 256 and 512, and each continuation holds at least a quarter of the tokens after the prompt.
All inputs are finite; a program needn't handle non-finite values.
Results may differ from a plain program's by a relative error of at most 0.017.
Values may be sent and summed in bfloat16 or wider, within the bound.
No kernel may reach another device: no remote copies, remote signals or barrier semaphores. Data moves between devices by JAX's collectives and lax.ppermute only.
A program may use at most 128 MiB of HBM per device.

v0:
```python
import functools
import math

import jax
import jax.numpy as jnp
from jax import lax
from jax.experimental import pallas as pl
from jax.experimental.pallas import tpu as pltpu
from jax.sharding import PartitionSpec as P

HEADS = 12
HEAD_DIM = 64

eps = 1e-05

MASKS = (0, 2, 1, 3)


def time_table(time_steps, model_width):
    half_dim = model_width // 2
    frequency = jnp.exp(-math.log(10000.0) * jnp.arange(half_dim, dtype=jnp.float32) / half_dim)
    angles = time_steps[:, None] * frequency[None, :]
    return jnp.concatenate([jnp.cos(angles), jnp.sin(angles)], axis=1)


def low(values_in):
    return values_in.astype(jnp.bfloat16)


def wide(values_in):
    return values_in.astype(jnp.float32)


HEAD_TILE = 128
COST = 1.0
VMEM_GRANT = 16 * 1024 * 1024
MASK_FILL = -1e30
GELU_IN = math.sqrt(2.0 / math.pi)
GELU_CUBE = 0.044715


def rope_tables(positions):
    half_dim = HEAD_DIM // 2
    column = jnp.arange(2 * HEAD_DIM, dtype=jnp.int32)
    frequency = jnp.exp(
        -math.log(10000.0) * 2.0 * (column % half_dim).astype(jnp.float32) / HEAD_DIM
    )
    angles = positions.astype(jnp.float32)[:, None] * frequency[None, :]
    sign = jnp.where(column % HEAD_DIM < half_dim, -1.0, 1.0)
    return (jnp.cos(angles), jnp.sin(angles) * sign[None, :])


def dot_nn(left, right):
    return lax.dot_general(
        left, right, (((1,), (0,)), ((), ())), preferred_element_type=jnp.float32
    )


def dot_nt(left, right):
    return lax.dot_general(
        left, right, (((1,), (1,)), ((), ())), preferred_element_type=jnp.float32
    )


def dot_tn(left, right):
    return lax.dot_general(
        left, right, (((0,), (0,)), ((), ())), preferred_element_type=jnp.float32
    )


def norm_rows(values_in):
    average = jnp.mean(values_in, axis=-1, keepdims=True)
    centred = values_in - average
    variance = jnp.mean(centred * centred, axis=-1, keepdims=True)
    scaling = lax.rsqrt(variance + eps)
    return (centred * scaling, scaling)


def swap_halves(values_in):
    column = lax.broadcasted_iota(jnp.int32, values_in.shape, 1)
    ahead = pltpu.roll(values_in, HEAD_TILE - HEAD_DIM // 2, 1)
    behind = pltpu.roll(values_in, HEAD_DIM // 2, 1)
    return jnp.where(column % HEAD_DIM < HEAD_DIM // 2, ahead, behind)


def whole(count):
    return [pl.BlockSpec(memory_space=pltpu.VMEM)] * count


def scalars():
    return [pl.BlockSpec(memory_space=pltpu.SMEM)]


def run(kernel, out_shapes, args, flops, scratch=(), name=None):
    nbytes = sum(a.size * a.dtype.itemsize for a in args)
    nbytes += sum(math.prod(o.shape) * o.dtype.itemsize for o in out_shapes)
    call = pl.pallas_call(
        kernel,
        out_shape=out_shapes,
        in_specs=scalars() + whole(len(args) - 1),
        out_specs=whole(len(out_shapes)),
        scratch_shapes=list(scratch),
        cost_estimate=pl.CostEstimate(flops=int(flops * COST), bytes_accessed=int(nbytes * COST), transcendentals=0),
        compiler_params=pltpu.CompilerParams(vmem_limit_bytes=VMEM_GRANT),
        name=name,
    )
    return call(*args)


def shaped(shape, kind=jnp.bfloat16):
    return jax.ShapeDtypeStruct(shape, kind)


FIRST, OWNER, PLACE = 2, 6, 10


def block_segment(info, block, rows, axis):
    shape = (rows, 1) if axis == 0 else (1, rows)
    position = info[FIRST + block] + lax.broadcasted_iota(jnp.int32, shape, axis)
    return (position >= info[0]).astype(jnp.int32) + (position >= info[1]).astype(jnp.int32)


def place_rows(info, chunks, first, rows, dest):
    for index, chunk in enumerate(chunks):
        at = pl.multiple_of(info[PLACE + index] * rows, rows)
        dest[pl.ds(at, rows), : chunk.shape[1]] = chunk[first : first + rows, :]


def store_blocks(info, sums_ref, outs):
    if len(outs) == 1:
        outs[0][...] = sums_ref[...]
    else:
        for index, dest in enumerate(outs):
            dest[...] = sums_ref[info[PLACE + index]]


def first_part_kernel(info, qkv_ref, out_ref, dest):
    span = dest.shape[1] // 4
    for part in range(4):

        @pl.when(info[0] == part)
        def _():
            for third in range(3):
                at = (third * 4 + part) * span
                dest[:, third * span : (third + 1) * span] = qkv_ref[:, at : at + span]
            dest[:, 3 * span :] = out_ref[:, part * span : (part + 1) * span]


def modulation_kernel(info, embed_ref, weight_ref, out_ref):
    width = out_ref.shape[2]
    for third in range(3):
        part = dot_nn(embed_ref[...], weight_ref[:, third * width : (third + 1) * width])
        for group in range(out_ref.shape[0]):
            out_ref[group, third : third + 1, :] = part[group : group + 1, :]


def second_part_kernel(count, info, up_ref, down_ref, dest):
    rows = up_ref.shape[0]
    piece = down_ref.shape[0] // 4
    for part in range(4):

        @pl.when(info[0] == part)
        def _():
            for index in range(count):
                at = (index * 4 + part) * piece
                dest[:rows, index * piece : (index + 1) * piece] = up_ref[:, at : at + piece]
            dest[rows:, :] = down_ref[part * piece : (part + 1) * piece, :]


def qkv_kernel(heads, count, info, *refs):
    gain, cos_ref, sin_ref = refs[:3]
    tok_refs = refs[3:7]
    chunks = refs[7 : 7 + count]
    hidden_ref, weight_ref, own_ref, q_ref, k_ref, v_ref, all_ref = refs[7 + count :]
    rows, width = tok_refs[0].shape
    lw = heads * HEAD_DIM
    place_rows(info, chunks, 0, width // count, weight_ref)
    own_ref[...] = weight_ref[:, 3 * lw : 4 * lw]
    gain_row = gain[...]
    for block in range(4):
        all_ref[block] = tok_refs[block][...]

    @pl.loop(0, 4)
    def _(block):
        normed, _ = norm_rows(wide(all_ref[block]))
        hidden = low(normed * gain_row)
        here = pl.ds(pl.multiple_of(block * rows, rows), rows)
        hidden_ref[here, :] = hidden
        both = dot_nn(hidden, weight_ref[:, : 2 * lw])
        last = dot_nn(hidden, weight_ref[:, 2 * lw : 2 * lw + 2 * HEAD_TILE])
        cos_part = cos_ref[here, :]
        sin_part = sin_ref[here, :]
        turned = []
        for tile in range(2 * lw // HEAD_TILE):
            piece = both[:, tile * HEAD_TILE : (tile + 1) * HEAD_TILE]
            turned.append(piece * cos_part + swap_halves(piece) * sin_part)
        column = lax.broadcasted_iota(jnp.int32, (rows, HEAD_TILE), 1)
        segment = block_segment(info, block, rows, 0)
        first_fill = jnp.where(segment == 1, 0.0, MASK_FILL)
        second_fill = jnp.where(segment == 2, 0.0, MASK_FILL)
        q_mark = jnp.where(
            column == HEAD_DIM, first_fill, jnp.where(column == HEAD_DIM + 1, second_fill, 0.0)
        )
        first_mark = jnp.where(segment == 1, 1.0, 0.0)
        second_mark = jnp.where(segment == 2, 1.0, 0.0)
        k_mark = jnp.where(
            column == HEAD_DIM,
            first_mark,
            jnp.where(
                column == HEAD_DIM + 1, second_mark, jnp.where(column < HEAD_DIM + 5, 1.0, 0.0)
            ),
        )
        v_mark = jnp.where(column < HEAD_DIM + 2, 1.0, 0.0)
        for head in range(heads):
            q_at, k_at = head, heads + head
            q_tile = turned[q_at // 2]
            k_tile = turned[k_at // 2]
            v_tile = last[:, HEAD_TILE * (head // 2) : HEAD_TILE * (head // 2 + 1)]
            if q_at % 2:
                q_tile = pltpu.roll(q_tile, HEAD_DIM, 1)
            if k_at % 2:
                k_tile = pltpu.roll(k_tile, HEAD_DIM, 1)
            if head % 2:
                v_tile = pltpu.roll(v_tile, HEAD_DIM, 1)
            there = slice(head * HEAD_TILE, (head + 1) * HEAD_TILE)
            q_ref[here, there] = low(jnp.where(column < HEAD_DIM, q_tile * 0.125, q_mark))
            k_ref[here, there] = low(jnp.where(column < HEAD_DIM, k_tile, k_mark))
            v_ref[here, there] = low(jnp.where(column < HEAD_DIM, v_tile, v_mark))


def attend_kernel(heads, rows, info, q_ref, k_ref, v_ref, *outs):
    att_refs = outs[:4]
    stat_ref, all_ref = outs[4:]
    column = lax.broadcasted_iota(jnp.int32, (rows, HEAD_TILE), 1)

    @pl.loop(0, 4)
    def _(block):
        here = pl.ds(pl.multiple_of(block * rows, rows), rows)
        results = []
        for head in range(heads):
            there = slice(head * HEAD_TILE, (head + 1) * HEAD_TILE)
            queries = q_ref[here, there]
            scores = dot_nt(queries, k_ref[:, there])
            row_max = jnp.max(scores, axis=-1, keepdims=True)
            weights = low(jnp.exp(scores - row_max))
            summed = dot_nn(weights, v_ref[:, there])
            row_sum = summed[:, HEAD_DIM : HEAD_DIM + 1]
            results.append(summed / row_sum)
            minus = -(row_max + jnp.log(row_sum))
            first = low(minus)
            second = low(minus - wide(first))
            third = low(minus - wide(first) - wide(second))
            stat_ref[here, there] = jnp.where(
                column == HEAD_DIM + 2,
                first,
                jnp.where(
                    column == HEAD_DIM + 3, second, jnp.where(column == HEAD_DIM + 4, third, queries)
                ),
            )
        for head in range(0, heads, 2):
            if head + 1 < heads:
                both = jnp.where(
                    column < HEAD_DIM, results[head], pltpu.roll(results[head + 1], HEAD_DIM, 1)
                )
                all_ref[here, head * HEAD_DIM : (head + 2) * HEAD_DIM] = low(both)
            else:
                all_ref[here, head * HEAD_DIM :] = low(results[head][:, :HEAD_DIM])

    for block in range(4):
        att_refs[block][...] = all_ref[block * rows : (block + 1) * rows, :]


def natural(info, blocks, dest):
    for block in range(4):
        dest[info[OWNER + block]] = blocks[block][...]


def middle_kernel(info, tok_ref, mod_ref, *refs):
    middle_ref, hidden_ref, att_ref, weight_ref = refs[8:]
    natural(info, refs[:4], weight_ref)
    natural(info, refs[4:8], att_ref)
    span = weight_ref.shape[2]
    for columns in range(4):
        there = slice(columns * span, (columns + 1) * span)
        total = wide(tok_ref[:, there])
        for part in range(4):
            total = total + dot_nn(
                att_ref[part], weight_ref[columns, part * span : (part + 1) * span, :]
            )
        middle_ref[:, there] = total
    normed, _ = norm_rows(middle_ref[...])
    hidden_ref[...] = low(normed * (1.0 + mod_ref[0:1, :]) + mod_ref[1:2, :])


def act_grad_kernel(count, skip, info, mod_ref, *refs):
    dy_refs = refs[:4]
    chunks = refs[4 : 4 + count]
    mlp_ref, act_ref, weight_ref = refs[4 + count :]
    rows = dy_refs[0].shape[0]
    place_rows(info, chunks, skip, weight_ref.shape[0] // count, weight_ref)
    gate = mod_ref[2:3, :]
    for block in range(4):
        here = slice(block * rows, (block + 1) * rows)
        mlp_ref[here, :] = low(gate * wide(dy_refs[block][...]))

    @pl.loop(0, 2)
    def _(turn):
        here = pl.ds(pl.multiple_of(turn * 2 * rows, 2 * rows), 2 * rows)
        act_ref[here, :] = low(dot_nt(mlp_ref[here, :], weight_ref[...]))


def forward_kernel(count, info, act_grad, *refs):
    hid_refs = refs[:4]
    chunks = refs[4 : 4 + count]
    act_ref, pre_ref, near_ref, far_ref, weight_ref, all_ref = refs[4 + count :]
    rows = hid_refs[0].shape[0]
    place_rows(info, chunks, 0, weight_ref.shape[0] // count, weight_ref)
    for block in range(4):
        all_ref[block] = hid_refs[block][...]

    @pl.loop(0, 2)
    def _(turn):
        there = pl.ds(pl.multiple_of(turn * rows, rows), rows)
        for half, dest in ((1, far_ref), (0, near_ref)):
            here = pl.ds(pl.multiple_of((2 * half + turn) * rows, rows), rows)
            pre = dot_nn(all_ref[2 * half + turn], weight_ref[...])
            square = pre * pre
            inner = jnp.tanh(GELU_IN * (pre + GELU_CUBE * (square * pre)))
            side = 0.5 * (1.0 + inner)
            act_ref[here, :] = low(pre * side)
            slope = side + 0.5 * pre * (1.0 - inner * inner) * (
                GELU_IN * (1.0 + 3.0 * GELU_CUBE * square)
            )
            grad_pre = low(wide(act_grad[here, :]) * slope)
            pre_ref[here, :] = grad_pre
            dest[there, :] = low(dot_nt(grad_pre, weight_ref[...]))


def weight_grad_kernel(count, info, act_ref, mlp_ref, pre_ref, *refs):
    hid_refs = refs[:4]
    outs, sums_ref = refs[4:-1], refs[-1]
    rows = hid_refs[0].shape[0]
    per = act_ref.shape[1] // count
    up = dot_tn(hid_refs[0][...], pre_ref[:rows, :])
    for block in range(1, 4):
        up = up + dot_tn(hid_refs[block][...], pre_ref[block * rows : (block + 1) * rows, :])
    for index in range(count):
        sums_ref[index, :per, :] = low(up[index * per : (index + 1) * per, :])
    down = dot_tn(act_ref[...], mlp_ref[...])
    for index in range(count):
        sums_ref[index, per:, :] = low(down[index * per : (index + 1) * per, :])
    store_blocks(info, sums_ref, outs)


def down_kernel(count, skip, info, act_ref, *refs):
    dy_refs = refs[:4]
    chunks = refs[4 : 4 + count]
    near_ref, far_ref, gate_ref, weight_ref = refs[4 + count :]
    rows = dy_refs[0].shape[0]
    place_rows(info, chunks, skip, weight_ref.shape[0] // count, weight_ref)
    total = jnp.zeros(gate_ref.shape, jnp.float32)
    for block in (2, 3, 1, 0):
        here = slice(block * rows, (block + 1) * rows)
        part = dot_nn(act_ref[here, :], weight_ref[...])
        total = total + jnp.sum(wide(dy_refs[block][...]) * part, axis=0, keepdims=True)
        dest = near_ref if block < 2 else far_ref
        dest[(block % 2) * rows : (block % 2 + 1) * rows, :] = low(part)
    gate_ref[...] = total


def branch_kernel(info, mod_ref, middle_ref, dy_ref, own_ref, core_ref, chip_ref, gate_ref, *refs):
    mid_ref, branch_ref, sums_ref = refs[4:7]
    att_refs = (refs[7], refs[8], None, refs[9])
    weight_ref, parts_ref = refs[10:]
    natural(info, refs[:4], weight_ref)
    rows, width = dy_ref.shape
    grad_hidden = wide(own_ref[:rows, :]) + wide(core_ref[:rows, :]) + wide(chip_ref[...])
    normed, scaling = norm_rows(middle_ref[...])
    sums_ref[0:1, :] = jnp.sum(grad_hidden * normed, axis=0, keepdims=True)
    sums_ref[1:2, :] = jnp.sum(grad_hidden, axis=0, keepdims=True)
    sums_ref[2:3, :] = gate_ref[...]
    grad_normed = grad_hidden * (1.0 + mod_ref[0:1, :])
    first_mean = jnp.mean(grad_normed, axis=-1, keepdims=True)
    second_mean = jnp.mean(grad_normed * normed, axis=-1, keepdims=True)
    mid_ref[...] = wide(dy_ref[...]) + scaling * (grad_normed - first_mean - normed * second_mean)
    span = weight_ref.shape[2]
    branch_ref[:, :width] = low(mid_ref[...])
    branch_ref[:, width + span :] = jnp.zeros(
        (rows, branch_ref.shape[1] - width - span), jnp.bfloat16
    )
    for columns in range(4):
        parts_ref[columns] = low(mid_ref[:, columns * span : (columns + 1) * span])
    for block, dest in enumerate(att_refs):
        at = pl.multiple_of(info[OWNER + block] * span, HEAD_DIM)
        total = dot_nt(parts_ref[0], weight_ref[0, pl.ds(at, span), :])
        for columns in range(1, 4):
            total = total + dot_nt(parts_ref[columns], weight_ref[columns, pl.ds(at, span), :])
        if dest is None:
            branch_ref[:, width : width + span] = low(total)
        else:
            dest[...] = low(total)


def out_grad_kernel(info, att_ref, core_att_ref, branch_ref, core_branch_ref, near_ref, parts_ref):
    span = att_ref.shape[2]
    for columns in range(4):
        here = slice(columns * span, (columns + 1) * span)
        parts_ref[columns] = branch_ref[:, here]
        parts_ref[4 + columns] = core_branch_ref[:, here]
    for block in range(2):
        owner = info[OWNER + block]
        branch, core_branch = parts_ref[owner], parts_ref[4 + owner]
        for part in range(4):
            near_ref[block, part * span : (part + 1) * span, :] = low(
                dot_tn(att_ref[part], branch) + dot_tn(core_att_ref[part], core_branch)
            )


def attend_back_kernel(heads, rows, info, cos_ref, sin_ref, q_ref, k_ref, v_ref, *refs):
    att = refs[:4]
    span = heads * HEAD_DIM
    width = 4 * span
    grads = ((refs[4], 0), (refs[5], 0), (refs[6], width), (refs[7], 0))
    out_ref, gx_ref, turn_ref, dq_ref, dk_ref, dv_ref = refs[8:]
    column = lax.broadcasted_iota(jnp.int32, (rows, HEAD_TILE), 1)

    def tile_of(ref, base, head):
        at = base + HEAD_TILE * (head // 2)
        if base or head % 2 or head + 1 < heads:
            tile = wide(ref[:, at : at + HEAD_TILE])
            return pltpu.roll(tile, HEAD_DIM, 1) if head % 2 else tile
        last = wide(ref[:, at:])
        return jnp.concatenate([last, jnp.zeros_like(last)], axis=1)

    for head in range(heads):
        there = slice(head * HEAD_TILE, (head + 1) * HEAD_TILE)
        for block in range(4):
            here = slice(block * rows, (block + 1) * rows)
            grad = jnp.where(column < HEAD_DIM, tile_of(*grads[block], head), 0.0)
            minus = -jnp.sum(grad * tile_of(att[block], 0, head), axis=-1, keepdims=True)
            first = wide(low(minus))
            gx_ref[here, :] = low(
                jnp.where(
                    column == HEAD_DIM,
                    first,
                    jnp.where(column == HEAD_DIM + 1, minus - first, grad),
                )
            )
        for block in range(4):
            here = slice(block * rows, (block + 1) * rows)
            keys = k_ref[here, there]
            probs = jnp.exp(dot_nt(keys, q_ref[:, there]))
            prob_grad = dot_nt(v_ref[here, there], gx_ref[...])
            score_grad = low(probs * prob_grad)
            dv_ref[here, there] = dot_nn(low(probs), gx_ref[...])
            dk_ref[here, there] = dot_nn(score_grad, q_ref[:, there])
            part = dot_tn(keys, score_grad)
            if block == 0:
                turn_ref[...] = part
            else:
                turn_ref[...] += part
        dq_ref[:, there] = jnp.transpose(turn_ref[...]) * 0.125

    for block in range(4):
        here = slice(block * rows, (block + 1) * rows)
        heads_of = [dq_ref[here, h * HEAD_TILE : (h + 1) * HEAD_TILE] for h in range(heads)]
        heads_of += [dk_ref[here, h * HEAD_TILE : (h + 1) * HEAD_TILE] for h in range(heads)]
        heads_of += [dv_ref[here, h * HEAD_TILE : (h + 1) * HEAD_TILE] for h in range(heads)]
        heads_of.append(jnp.zeros((rows, HEAD_TILE), jnp.float32))
        for tile in range((3 * heads + 1) // 2):
            both = jnp.where(
                column < HEAD_DIM,
                heads_of[2 * tile],
                pltpu.roll(heads_of[2 * tile + 1], HEAD_DIM, 1),
            )
            if tile < heads:
                both = both * cos_ref[here, :] - swap_halves(both) * sin_ref[here, :]
            out_ref[here, tile * HEAD_TILE : (tile + 1) * HEAD_TILE] = low(both)


def hidden_grad_kernel(rows, info, grad_ref, weight_ref, near_ref, far_ref):
    span = grad_ref.shape[1]

    @pl.loop(0, 2)
    def _(turn):
        there = pl.ds(pl.multiple_of(turn * rows, rows), rows)
        for half, dest in ((1, far_ref), (0, near_ref)):
            here = pl.ds(pl.multiple_of((2 * half + turn) * rows, rows), rows)
            dest[there, :] = low(dot_nt(grad_ref[here, :], weight_ref[:, :span]))


def qkv_grad_kernel(count, used, info, hidden_ref, grad_ref, near_ref, chip_ref, *refs):
    outs, sums_ref = refs[:-1], refs[-1]
    total = dot_tn(hidden_ref[...], grad_ref[...])
    out_total = wide(near_ref[0]) + wide(chip_ref[0])
    per = total.shape[0] // count
    for index in range(count):
        here = slice(index * per, (index + 1) * per)
        sums_ref[index, :, :used] = low(total[here, :used])
        sums_ref[index, :, used:] = low(out_total[here, :])
    store_blocks(info, sums_ref, outs)


def input_kernel(info, gain, tok_ref, mid_ref, own_ref, core_ref, chip_ref, out_ref):
    rows = tok_ref.shape[0]
    grad_hidden = wide(own_ref[:rows, :]) + wide(core_ref[:rows, :]) + wide(chip_ref[:rows, :])
    normed, scaling = norm_rows(wide(tok_ref[...]))
    grad_normed = grad_hidden * gain[...]
    first_mean = jnp.mean(grad_normed, axis=-1, keepdims=True)
    second_mean = jnp.mean(grad_normed * normed, axis=-1, keepdims=True)
    out_ref[...] = low(
        mid_ref[...] + scaling * (grad_normed - first_mean - normed * second_mean)
    )


def finish_mlp_kernel(count, info, *refs):
    blocks = refs[:4]
    up_ref, down_ref, all_ref = refs[4:]
    natural(info, blocks, all_ref)
    rows = up_ref.shape[0]
    piece = down_ref.shape[0] // 4
    for part in range(4):
        value = wide(all_ref[part])
        for index in range(count):
            at = (index * 4 + part) * piece
            up_ref[:, at : at + piece] = value[:rows, index * piece : (index + 1) * piece]
        down_ref[part * piece : (part + 1) * piece, :] = value[rows:, :]


def finish_qkv_kernel(info, *refs):
    blocks = refs[:4]
    weight_ref, gain_ref, out_ref, own_ref, sums_ref, all_ref = refs[4:]
    natural(info, blocks, all_ref)
    span = all_ref.shape[2] // 4
    total = jnp.zeros((out_ref.shape[0], 1), jnp.float32)
    for part in range(4):
        value = wide(all_ref[part])
        for third in range(3):
            at = (third * 4 + part) * span
            piece = value[:, third * span : (third + 1) * span]
            total = total + jnp.sum(
                wide(weight_ref[:, at : at + span]) * piece, axis=1, keepdims=True
            )
            out_ref[:, at : at + span] = piece
        own_ref[:, part * span : (part + 1) * span] = value[:, 3 * span :]
    turned = jnp.transpose(jnp.broadcast_to(total, (total.shape[0], HEAD_TILE)))
    sums_ref[...] = turned[0:1, :] / gain_ref[...]


def hop(values_in, mask):
    return lax.ppermute(values_in, "seq", [(i, i ^ mask) for i in range(lax.axis_size("seq"))])


def ring_of(count):
    return [0] + list(range(1, count, 2)) + [i for i in range(count - 1, 0, -1) if i % 2 == 0]


def ring_next(data_count):
    outer = data_count // 2
    ring = ring_of(outer)
    follow = {ring[i]: ring[(i + 1) % outer] for i in range(outer)}
    return [(z * 2 + y, follow[z] * 2 + y) for z in range(outer) for y in range(2)]


def pair(values_in):
    return lax.ppermute(values_in, "dp", [(i, i ^ 1) for i in range(lax.axis_size("dp"))])


def dp_sum_direct(blocks):
    data_count = lax.axis_size("dp")
    if data_count != 8:
        return wide(lax.psum_scatter(blocks, "dp", scatter_dimension=0, tiled=False))
    return jnp.sum(wide(lax.all_to_all(blocks, "dp", 0, 0, tiled=True)), axis=0)


def after(values_in, *earlier):
    return lax.optimization_barrier((values_in,) + earlier)[0]


def onward(values_in):
    return lax.ppermute(values_in, "dp", ring_next(lax.axis_size("dp")))


def kernel_info(layout, rank, index, tok_rows):
    data_count = lax.axis_size("dp")
    column = jnp.arange(PLACE + 8, dtype=jnp.int32)

    def owner(block):
        return rank ^ ((block & 1) * 2 + (block >> 1))

    values = jnp.where(column == 0, layout[0, 0], layout[0, 1])
    values = jnp.where(column >= FIRST, owner(column - FIRST) * tok_rows, values)
    values = jnp.where(column >= OWNER, owner(column - OWNER), values)
    if data_count == 8:
        step = column - PLACE
        at = index >> 1
        at = ((at ^ (at >> 1)) - (step >> 1)) & 3
        place = (at ^ (at >> 1)) * 2 + ((index + step) & 1)
    else:
        place = jnp.zeros_like(column)
    return jnp.where(column >= PLACE, place, values)


def gathered_whole(chunk, sizes):
    gathered = lax.all_gather(chunk, "dp", axis=0)
    parts = []
    at = 0
    for size in sizes:
        parts.append(gathered[:, at : at + size].reshape(-1, chunk.shape[1]))
        at += size
    return [jnp.concatenate(parts, axis=0)]


def four(values_in):
    chip = hop(values_in, 2)
    return [values_in, chip, hop(values_in, 1), hop(chip, 1)]


def beyond(values_in, mask):
    return lax.ppermute(values_in, "dp", [(i, i ^ mask) for i in range(lax.axis_size("dp"))])


def doubled(parts, other, bit):
    return jnp.where(
        bit, jnp.concatenate([other, parts], axis=0), jnp.concatenate([parts, other], axis=0)
    )


def body(tokens, ln1_gain, w_qkv, w_out, w_ada, w_up, w_down, out_grad, layout, timestep):
    seq_count = lax.axis_size("seq")
    data_count = lax.axis_size("dp")
    ringed = data_count == 8
    rank = lax.axis_index("seq")
    index = lax.axis_index("dp")
    high = [(index >> place) & 1 == 1 for place in range(data_count.bit_length() - 1)]
    tokens, rank, index, high = lax.optimization_barrier((tokens, rank, index, high))
    tok_rows, width = tokens.shape
    group_rows = tok_rows * seq_count
    heads_local = HEADS // seq_count
    local_width = heads_local * HEAD_DIM
    head_columns = heads_local * HEAD_TILE
    padded = (3 * heads_local + 1) // 2 * HEAD_TILE
    rows = w_qkv.shape[0]
    hidden = w_up.shape[1] // seq_count
    down_piece = w_down.shape[0] // seq_count
    rank_word = rank.reshape(1).astype(jnp.int32)

    tok_chip = hop(tokens, 2)
    first = run(
        first_part_kernel,
        [shaped((rows, 4 * local_width))],
        [rank_word, w_qkv, w_out],
        0,
        name="first_part",
    )[0]
    if ringed:
        held = [first, onward(first)]
        beside = [pair(first)]
        held[1], beside[0], tokens = lax.optimization_barrier((held[1], beside[0], tokens))
        held.append(onward(held[1]))
        beside.append(pair(held[1]))
        tok_core = hop(tokens, 1)
        held[2], beside[1], tok_chip, tok_core = lax.optimization_barrier(
            (held[2], beside[1], tok_chip, tok_core)
        )
        held.append(onward(held[2]))
        beside.append(pair(held[2]))
        tok_both = hop(tok_chip, 1)
    else:
        tok_core, tok_both = hop(tokens, 1), hop(tok_chip, 1)
    tok_blocks = [tokens, tok_chip, tok_core, tok_both]

    embed = low(time_table(wide(timestep), width))
    sent = jnp.stack(
        [embed.reshape(data_count, rows), jnp.broadcast_to(ln1_gain, (data_count, rows))], axis=1
    )
    if ringed:
        sent = after(sent, held[1])
    taken = lax.all_to_all(sent, "dp", 0, 0, tiled=True)
    embeds = taken[:, 0]
    gain = wide(taken[:, 1].reshape(1, width))
    mod_parts = run(
        modulation_kernel,
        [shaped((data_count, 3, width), jnp.float32)],
        [rank_word, after(embeds, held[2]) if ringed else embeds, w_ada],
        2 * data_count * rows * w_ada.shape[1],
        name="modulation",
    )[0]

    def halves(parts, place):
        half = parts.shape[0] // 2
        kept = jnp.where(high[place], parts[half:], parts[:half])
        given = jnp.where(high[place], parts[:half], parts[half:])
        return kept, beyond(given, 1 << place)

    modulation = mod_parts
    for place in range(len(high) - 1, 2, -1):
        modulation = sum(halves(modulation, place))

    info = kernel_info(layout, rank, index, tok_rows)
    starts = info[FIRST:OWNER]
    if ringed:
        starts = after(starts, held[2])
    positions = (starts[:, None] + jnp.arange(tok_rows, dtype=jnp.int32)[None, :]).reshape(-1)
    cos_table, sin_table = rope_tables(positions)

    second = run(
        functools.partial(second_part_kernel, data_count),
        [shaped((rows + down_piece, width))],
        [rank_word, w_up, w_down],
        0,
        name="second_part",
    )[0]
    if ringed:
        dy_core = hop(after(out_grad, held[2]), 1)
        held[3], beside[2], second, dy_core, *rest = lax.optimization_barrier(
            (
                held[3],
                beside[2],
                second,
                dy_core,
                gain,
                info,
                cos_table,
                sin_table,
                tok_blocks,
            )
        )
        gain, info, cos_table, sin_table, tok_blocks = rest
        beside.append(pair(held[3]))
        first_chunks = [part for both in zip(held, beside) for part in both]
        held = [second, onward(second)]
        beside = [pair(after(second, beside[3]))]
        dy_chip = hop(after(out_grad, held[0]), 2)
    else:
        first_chunks = gathered_whole(first, [rows])
        second_chunks = gathered_whole(second, [rows, down_piece])
        dy_chip, dy_core = hop(out_grad, 2), hop(out_grad, 1)
    kept, sums = halves(modulation, 2)
    if ringed:
        gain, sums = lax.optimization_barrier((gain, sums))
    kept, sums = halves(kept + sums, 1)
    count = len(first_chunks)
    up_rows = rows * (data_count // count)

    hidden_one, qkv_weight, own_out, queries, keys, values = run(
        functools.partial(qkv_kernel, heads_local, count),
        [
            shaped((group_rows, width)),
            shaped((width, 4 * local_width)),
            shaped((width, local_width)),
            shaped((group_rows, head_columns)),
            shaped((group_rows, head_columns)),
            shaped((group_rows, head_columns)),
        ],
        [info, gain, cos_table, sin_table] + tok_blocks + first_chunks,
        2 * group_rows * width * padded,
        scratch=[pltpu.VMEM((seq_count, tok_rows, width), jnp.bfloat16)],
        name="qkv",
    )
    if ringed:
        queries, own_out, held[1], beside[0], sums = lax.optimization_barrier(
            (queries, own_out, held[1], beside[0], sums)
        )
        beside.append(pair(held[1]))
        held.append(onward(held[1]))
    kept, sums = halves(kept + sums, 0)
    chip_out = hop(own_out, 2)
    core_out = hop(own_out, 1)
    *att_parts, marked = run(
        functools.partial(attend_kernel, heads_local, tok_rows),
        [shaped((tok_rows, local_width))] * 4 + [shaped((group_rows, head_columns))],
        [info, queries, keys, values],
        4 * group_rows * group_rows * head_columns,
        scratch=[pltpu.VMEM((group_rows, local_width), jnp.bfloat16)],
        name="attend",
    )
    if ringed:
        att_parts, held[2], beside[1], chip_out, core_out, dy_chip, sums = lax.optimization_barrier(
            (att_parts, held[2], beside[1], chip_out, core_out, dy_chip, sums)
        )
        beside.append(pair(held[2]))
        held.append(onward(held[2]))
    modulation = (kept + sums)[0]
    att_own = [att_parts[0]] + [hop(att_parts[j], MASKS[j]) for j in (1, 2, 3)]
    out_blocks = [own_out, chip_out, core_out, hop(after(chip_out, att_own[2]), 1)]
    if ringed:
        att_own = lax.optimization_barrier(att_own)
    middle, hidden_two, att_ordered = run(
        middle_kernel,
        [
            shaped((tok_rows, width), jnp.float32),
            shaped((tok_rows, width)),
            shaped((seq_count, tok_rows, local_width)),
        ],
        [info, tokens, modulation] + out_blocks + att_own,
        2 * tok_rows * width * width,
        scratch=[pltpu.VMEM((seq_count, width, local_width), jnp.bfloat16)],
        name="middle",
    )

    chip_hidden = hop(hidden_two, 2)
    if ringed:
        beside.append(pair(held[3]))
        second_chunks = [part for both in zip(held, beside) for part in both]
    dy_blocks = [out_grad, dy_chip, dy_core, hop(after(dy_chip, hidden_two), 1)]
    grad_mlp, grad_act = run(
        functools.partial(act_grad_kernel, count, up_rows),
        [shaped((group_rows, width)), shaped((group_rows, hidden))],
        [info, modulation] + dy_blocks + second_chunks,
        2 * group_rows * width * hidden,
        scratch=[pltpu.VMEM((hidden, width), jnp.bfloat16)],
        name="act_grad",
    )
    hid_blocks = [
        hidden_two,
        chip_hidden,
        hop(hidden_two, 1),
        hop(after(chip_hidden, grad_act), 1),
    ]
    half = shaped((group_rows // 2, width))
    activated, grad_pre, gh_near, gh_far = run(
        functools.partial(forward_kernel, count),
        [shaped((group_rows, hidden)), shaped((group_rows, hidden)), half, half],
        [info, grad_act] + hid_blocks + second_chunks,
        4 * group_rows * width * hidden,
        scratch=[
            pltpu.VMEM((width, hidden), jnp.bfloat16),
            pltpu.VMEM((seq_count, tok_rows, width), jnp.bfloat16),
        ],
        name="forward",
    )
    block_shape = (rows + down_piece, width)
    grad_weights = run(
        functools.partial(weight_grad_kernel, data_count),
        [shaped(block_shape)] * count if ringed else [shaped((data_count,) + block_shape)],
        [info, activated, grad_mlp, grad_pre] + hid_blocks,
        4 * group_rows * width * hidden,
        scratch=[pltpu.VMEM((data_count,) + block_shape, jnp.bfloat16)],
        name="weight_grad",
    )
    gh_core = hop(gh_far, 1)
    gh_core, grad_weights = lax.optimization_barrier((gh_core, grad_weights))
    gh_send = low(wide(gh_near[tok_rows:]) + wide(gh_core[tok_rows:]))
    gh_chip = hop(gh_send, 2)
    mlp_near, mlp_far, grad_gate = run(
        functools.partial(down_kernel, count, up_rows),
        [half, half, shaped((1, width), jnp.float32)],
        [info, after(activated, gh_send)] + dy_blocks + second_chunks,
        2 * group_rows * width * hidden,
        scratch=[pltpu.VMEM((hidden, width), jnp.bfloat16)],
        name="down",
    )
    if ringed:
        mlp_keep, mlp_give = list(grad_weights[0::2]), list(grad_weights[1::2])
        mlp_taken = pair(after(mlp_give[1], gh_send))
        gh_chip, mlp_far, mlp_taken = lax.optimization_barrier((gh_chip, mlp_far, mlp_taken))
        mlp_ring = low(wide(mlp_keep[1]) + wide(mlp_taken))
        gh_chip, mlp_ring = lax.optimization_barrier((gh_chip, mlp_ring))
        mlp_carried = onward(mlp_ring)
        mlp_taken = pair(after(mlp_give[2], mlp_ring))
    else:
        gh_chip, mlp_far = lax.optimization_barrier((gh_chip, mlp_far))
    mlp_core = hop(mlp_far, 1)
    core_attended = hop(after(att_ordered, gh_chip), 1)

    branch_columns = -(-(width + local_width) // HEAD_TILE) * HEAD_TILE
    grad_middle, branch, grad_mod, *grad_parts = run(
        branch_kernel,
        [
            shaped((tok_rows, width), jnp.float32),
            shaped((tok_rows, branch_columns)),
            shaped((3, width), jnp.float32),
        ]
        + [shaped((tok_rows, local_width))] * 3,
        [info, modulation, after(middle, mlp_near), out_grad, gh_near, gh_core, gh_chip]
        + [grad_gate]
        + out_blocks,
        2 * tok_rows * width * width,
        scratch=[
            pltpu.VMEM((seq_count, width, local_width), jnp.bfloat16),
            pltpu.VMEM((seq_count, tok_rows, local_width), jnp.bfloat16),
        ],
        name="branch",
    )
    grad_parts, mlp_core = lax.optimization_barrier((grad_parts, mlp_core))
    core_branch = hop(branch, 1)
    grad_att = [grad_parts[0], hop(grad_parts[1], 2), core_branch, hop(grad_parts[2], 3)]
    out_sums = run(
        out_grad_kernel,
        [shaped((2, width, local_width))],
        [info, att_ordered, core_attended, branch, core_branch],
        2 * tok_rows * width * width,
        scratch=[pltpu.VMEM((2 * seq_count, tok_rows, local_width), jnp.bfloat16)],
        name="out_grad",
    )[0]

    if ringed:
        del grad_att[2]
        grad_att, out_sums, mlp_taken, mlp_carried = lax.optimization_barrier(
            (grad_att, out_sums, mlp_taken, mlp_carried)
        )
        grad_att.insert(2, core_branch)
        mlp_ring = low(wide(mlp_keep[2]) + wide(mlp_taken) + wide(mlp_carried))
        mlp_carried = onward(mlp_ring)
        mlp_taken = pair(after(mlp_give[3], mlp_ring))
    out_chip = hop(out_sums[1:], 2)
    mod_core = hop(grad_mod, 1)
    grad_qkv = run(
        functools.partial(attend_back_kernel, heads_local, tok_rows),
        [shaped((group_rows, padded))],
        [info, cos_table, sin_table, marked, keys, values] + att_parts + grad_att,
        10 * group_rows * group_rows * head_columns,
        scratch=[
            pltpu.VMEM((group_rows, HEAD_TILE), jnp.bfloat16),
            pltpu.VMEM((HEAD_TILE, group_rows), jnp.float32),
            pltpu.VMEM((group_rows, head_columns), jnp.float32),
            pltpu.VMEM((group_rows, head_columns), jnp.float32),
            pltpu.VMEM((group_rows, head_columns), jnp.float32),
        ],
        name="attend_back",
    )[0]
    grad_qkv, out_chip, mod_core = lax.optimization_barrier((grad_qkv, out_chip, mod_core))
    grad_mod = grad_mod + mod_core
    mod_chip = hop(grad_mod, 2)
    mlp_send = low(wide(after(mlp_near[tok_rows:], grad_qkv)) + wide(mlp_core[tok_rows:]))
    mlp_chip = hop(mlp_send, 2)
    if ringed:
        grad_qkv, mlp_taken, mlp_carried = lax.optimization_barrier(
            (grad_qkv, mlp_taken, mlp_carried)
        )
    qkv_sums = run(
        functools.partial(qkv_grad_kernel, data_count, 3 * local_width),
        [shaped((rows, 4 * local_width))] * count
        if ringed
        else [shaped((data_count, rows, 4 * local_width))],
        [info, hidden_one, grad_qkv, out_sums, out_chip],
        2 * group_rows * width * padded,
        scratch=[pltpu.VMEM((data_count, rows, 4 * local_width), jnp.bfloat16)],
        name="qkv_grad",
    )
    gq_near, gq_far = run(
        functools.partial(hidden_grad_kernel, tok_rows),
        [half, half],
        [info, after(grad_qkv, qkv_sums[0]), qkv_weight],
        2 * group_rows * width * padded,
        name="hidden_grad",
    )
    if ringed:
        qkv_keep, qkv_give = list(qkv_sums[0::2]), list(qkv_sums[1::2])
        qkv_taken = pair(qkv_give[1])
        mlp_ring = low(wide(after(mlp_keep[3], qkv_sums[0])) + wide(mlp_taken) + wide(mlp_carried))
        mlp_carried = onward(mlp_ring)
        mlp_taken = pair(after(mlp_give[0], mlp_ring))
        gq_far, qkv_taken, mod_chip = lax.optimization_barrier((gq_far, qkv_taken, mod_chip))
        qkv_ring = low(wide(qkv_keep[1]) + wide(qkv_taken))
        qkv_carried = onward(qkv_ring)
        qkv_taken = pair(after(qkv_give[2], qkv_ring))
    grad_mod = (grad_mod + mod_chip)[None]
    mod_other = beyond(grad_mod, 1)
    gq_core = hop(gq_far, 1)
    gq_send = low(wide(gq_near[tok_rows:]) + wide(gq_core[tok_rows:]))
    if ringed:
        qkv_carried, qkv_taken, gq_send, mlp_carried, mlp_taken = lax.optimization_barrier(
            (qkv_carried, qkv_taken, gq_send, mlp_carried, mlp_taken)
        )
        qkv_ring = low(wide(qkv_keep[2]) + wide(qkv_taken) + wide(qkv_carried))
        qkv_carried = onward(qkv_ring)
        qkv_taken = pair(after(qkv_give[3], qkv_ring))
    gq_chip = hop(gq_send, 2)
    if ringed:
        sum_mlp = low(wide(mlp_keep[0]) + wide(mlp_taken) + wide(mlp_carried))
        qkv_carried, qkv_taken, mlp_chip, mod_other = lax.optimization_barrier(
            (qkv_carried, qkv_taken, mlp_chip, mod_other)
        )
        qkv_ring = low(wide(qkv_keep[3]) + wide(qkv_taken) + wide(qkv_carried))
        qkv_carried = onward(qkv_ring)
        qkv_taken = pair(after(qkv_give[0], qkv_ring))
    else:
        sum_mlp = low(dp_sum_direct(grad_weights[0]))
    grad_mod = doubled(grad_mod, mod_other, high[0])
    sum_mlp, gq_chip = lax.optimization_barrier((sum_mlp, gq_chip))
    mlp_blocks = four(sum_mlp)
    grad_inputs = run(
        input_kernel,
        [shaped((tok_rows, width))],
        [info, gain, tokens, grad_middle, gq_near, gq_core, gq_chip],
        20 * tok_rows * width,
        name="input",
    )[0]
    for place in range(1, len(high)):
        grad_mod = doubled(grad_mod, beyond(grad_mod, 1 << place), high[place])
    grad_mods = grad_mod.reshape(data_count, 3 * width)
    if ringed:
        qkv_carried, qkv_taken, grad_inputs = lax.optimization_barrier(
            (qkv_carried, qkv_taken, grad_inputs)
        )
        sum_qkv = low(wide(qkv_keep[0]) + wide(qkv_taken) + wide(qkv_carried))
    else:
        sum_qkv = low(dp_sum_direct(qkv_sums[0]))
    mlp_out = wide(mlp_near[:tok_rows]) + wide(mlp_core[:tok_rows]) + wide(mlp_chip)
    result = low(middle + modulation[2:3] * mlp_out)
    final_ada = lax.dot_general(
        wide(embeds), grad_mods, (((0,), (0,)), ((), ())), precision=lax.Precision.HIGHEST
    )

    final_up, final_down = run(
        functools.partial(finish_mlp_kernel, data_count),
        [shaped(w_up.shape, jnp.float32), shaped(w_down.shape, jnp.float32)],
        [info] + mlp_blocks,
        0,
        scratch=[pltpu.VMEM((seq_count,) + block_shape, jnp.bfloat16)],
        name="finish_mlp",
    )
    final_qkv, final_out, final_gain = run(
        finish_qkv_kernel,
        [
            shaped(w_qkv.shape, jnp.float32),
            shaped(w_out.shape, jnp.float32),
            shaped((1, rows), jnp.float32),
        ],
        [info] + four(sum_qkv) + [w_qkv, wide(ln1_gain).reshape(1, rows)],
        0,
        scratch=[pltpu.VMEM((seq_count, rows, 4 * local_width), jnp.bfloat16)],
        name="finish_qkv",
    )
    return (
        result,
        grad_inputs,
        final_gain.reshape(-1),
        final_qkv,
        final_out,
        final_ada,
        final_up,
        final_down,
    )


def solution(mesh):
    placed = (
        P(("dp", "seq"), None),
        P("dp"),
        P("dp", None),
        P("dp", None),
        P("dp", None),
        P("dp", None),
        P("dp", None),
        P(("dp", "seq"), None),
        P("dp", None),
        P("dp"),
    )
    return jax.shard_map(
        body,
        mesh=mesh,
        in_specs=placed,
        out_specs=(
            P(("dp", "seq"), None),
            P(("dp", "seq"), None),
            P("dp"),
            P("dp", None),
            P("dp", None),
            P("dp", None),
            P("dp", None),
            P("dp", None),
        ),
        check_vma=False,
    )
```

profile of v0, /device:TPU:0, one launch (start us, length us, event | category | flops | bytes accessed | tf_op | source)
XLA Modules:
  0.0 191.8 jit_solution(11650703690904778520)
XLA Ops:
  2.7 3.1 %collective-permute-start = (bf16[96,768]{1,0:T(8,128)(2,1)S(1)}, bf16[96,768]{1,0:T(8,128)(2,1)S(1)}, u32[]{:S(2)}, u32[]{:S(2)}) collective-permute-start(bf16[96,768]{1,0:T(8,128)(2,1)S(1)} %first_part.1.refs_7_), channel_id=1, source_target_pairs={{0,8},{4,12},{8,24},{12,28},{16,0},{20,4},{24,16},{28,20},{1,9},{5... | collective-permute-start | bytes 442376 | tf_op jit(solution)/shard_map/ppermute | solution.py:581
  12.4 2.6 %collective-permute-start.2 = (bf16[96,768]{1,0:T(8,128)(2,1)S(1)}, bf16[96,768]{1,0:T(8,128)(2,1)S(1)}, u32[]{:S(2)}, u32[]{:S(2)}) collective-permute-start(bf16[96,768]{1,0:T(8,128)(2,1)S(1)} %collective-permute-done.refs_9_), channel_id=1, source_target_pairs={{0,8},{4,12},{8,24},{12,28},{16,0},{20,4},{24,16},{28,20},{1,9},{5... | collective-permute-start | bytes 442376 | tf_op jit(solution)/shard_map/ppermute | solution.py:581
  17.1 3.3 %all-to-all-start = ((bf16[8,2,96]{2,1,0:T(2,128)(2,1)}), bf16[8,2,96]{2,1,0:T(2,128)(2,1)S(1)}, u32[]{:S(2)}, u32[]{:S(2)}) async-start(bf16[8,2,96]{2,1,0:T(2,128)(2,1)} %copy.19), calls=%async_computation | async-start | bytes 8192 | tf_op jit(solution)/shard_map/all_to_all | solution.py:679
  24.1 2.6 %all-to-all-done = bf16[8,2,96]{2,1,0:T(2,128)(2,1)S(1)} async-done(((bf16[8,2,96]{2,1,0:T(2,128)(2,1)}), bf16[8,2,96]{2,1,0:T(2,128)(2,1)S(1)}, u32[]{:S(2)}, u32[]{:S(2)}) %all-to-all-start) | async-done | bytes 3104 | tf_op jit(solution)/shard_map/all_to_all | solution.py:679
  28.9 2.4 %collective-permute-start.10 = (f32[4,3,768]{2,1,0:T(4,128)S(1)}, f32[4,3,768]{2,1,0:T(4,128)S(1)}, u32[]{:S(2)}, u32[]{:S(2)}) collective-permute-start(f32[4,3,768]{2,1,0:T(4,128)S(1)} %slice_select_fusion), channel_id=1, source_target_pairs={{0,16},{4,20},{8,24},{12,28},{16,0},{20,4},{24,8},{28,12},{1,17},{... | collective-permute-start | bytes 110600 | tf_op jit(solution)/shard_map/ppermute | solution.py:620
  31.3 1.9 fusion
  36.1 3.6 %collective-permute-done.11.refs_14_ = bf16[96,768]{1,0:T(8,128)(2,1)S(1)} collective-permute-done((bf16[96,768]{1,0:T(8,128)(2,1)S(1)}, bf16[96,768]{1,0:T(8,128)(2,1)S(1)}, u32[]{:S(2)}, u32[]{:S(2)}) %collective-permute-start.11) | collective-permute-done | bytes 147488 | tf_op jit(solution)/shard_map/ppermute | solution.py:566
  43.6 4.6 %qkv.1 = (bf16[1024,768]{1,0:T(8,128)(2,1)S(1)}, bf16[768,768]{1,0:T(8,128)(2,1)S(1)}, bf16[768,192]{1,0:T(8,128)(2,1)S(1)}, bf16[1024,384]{1,0:T(8,128)(2,1)S(1...) custom-call(s32[18]{0:T(128)S(1)} %compare_select_fusion.4.info, f32[1,768]{1,0:T(1,128)S(1)} %reshape.139.refs_0_.gain, ...), custom_call_target="tpu_custom_call" | custom-call | flops 1006632960 | bytes 9210952 | tf_op jit(solution)/shard_map/qkv/pallas_call | solution.py:107
  52.0 2.2 %collective-permute-start.20 = (f32[1,3,768]{2,1,0:T(4,128)S(1)}, f32[1,3,768]{2,1,0:T(4,128)S(1)}, u32[]{:S(2)}, u32[]{:S(2)}) collective-permute-start(f32[1,3,768]{2,1,0:T(4,128)S(1)} %slice_select_fusion.2), channel_id=1, source_target_pairs={{0,4},{4,0},{8,12},{12,8},{16,20},{20,16},{24,28},{28,24},{1,5},{5... | collective-permute-start | bytes 27656 | tf_op jit(solution)/shard_map/ppermute | solution.py:620
  54.1 7.3 %attend.1 = (bf16[256,192]{1,0:T(8,128)(2,1)S(1)}, bf16[256,192]{1,0:T(8,128)(2,1)S(1)}, bf16[256,192]{1,0:T(8,128)(2,1)S(1)}, bf16[256,192]{1,0:T(8,128)(2,1)S(1)}, bf16[1024,384]{1,0:T(8,128)(2,1)S(1)}) custom-call(s32[18]{0:T(128)S(1)} %compare_select_fusion.4.info, bf16[1024,384]{1,0:T(8,128)(2,1)S(1)} %get-tuple-element.209.q_ref, ...), custom_call_target="tpu_custom_call" | custom-call | flops 1610612736 | bytes 3539016 | tf_op jit(solution)/shard_map/attend/pallas_call | solution.py:107
  64.8 4.6 %collective-permute-done.23.refs_5_ = bf16[256,192]{1,0:T(8,128)(2,1)S(1)} collective-permute-done((bf16[256,192]{1,0:T(8,128)(2,1)S(1)}, bf16[256,192]{1,0:T(8,128)(2,1)S(1)}, u32[]{:S(2)}, u32[]{:S(2)}) %collective-permute-start.23) | collective-permute-done | bytes 98336 | tf_op jit(solution)/shard_map/ppermute | solution.py:551
  77.3 6.1 %collective-permute-done.26.refs_9_ = bf16[192,768]{1,0:T(8,128)(2,1)S(1)} collective-permute-done((bf16[192,768]{1,0:T(8,128)(2,1)S(1)}, bf16[192,768]{1,0:T(8,128)(2,1)S(1)}, u32[]{:S(2)}, u32[]{:S(2)}) %collective-permute-start.26) | collective-permute-done | bytes 294944 | tf_op jit(solution)/shard_map/ppermute | solution.py:566
  83.4 5.4 %collective-permute-done.28.refs_11_ = bf16[192,768]{1,0:T(8,128)(2,1)S(1)} collective-permute-done((bf16[192,768]{1,0:T(8,128)(2,1)S(1)}, bf16[192,768]{1,0:T(8,128)(2,1)S(1)}, u32[]{:S(2)}, u32[]{:S(2)}) %collective-permute-start.28) | collective-permute-done | bytes 294944 | tf_op jit(solution)/shard_map/ppermute | solution.py:566
  88.8 2.5 %act_grad.1 = (bf16[1024,768]{1,0:T(8,128)(2,1)S(1)}, bf16[1024,768]{1,0:T(8,128)(2,1)S(1)}) custom-call(s32[18]{0:T(128)S(1)} %compare_select_fusion.4.info, f32[3,768]{1,0:T(4,128)S(1)} %bitcast.30, bf16[256,768]{1,0:T(8,128)(2,1)S(1)} %copy-done.3, bf16[256,768]{1,0:T(8,128)(2,1)S(1)} %collective-permute-done.19.refs_1_, ...), custom_call_target="tpu_custom_call" | custom-call | flops 1207959552 | bytes 7087176 | tf_op jit(solution)/shard_map/act_grad/pallas_call | solution.py:107
  93.1 4.9 %forward.1 = (bf16[1024,768]{1,0:T(8,128)(2,1)S(1)}, bf16[1024,768]{1,0:T(8,128)(2,1)S(1)}, bf16[512,768]{1,0:T(8,128)(2,1)S(1)}, bf16[512,768]{1,0:T(8,128)(2,1)S(1)}) custom-call(s32[18]{0:T(128)S(1)} %compare_select_fusion.4.info, bf16[1024,768]{1,0:T(8,128)(2,1)S(1)} %get-tuple-element.239.act_grad, bf16[256,768]{1,0:T(8,128)(2,1)S(1)} %get-tuple-element.234.refs_0_, ...), custom_call_target="tpu_custom_call" | custom-call | flops 2415919104 | bytes 10223688 | tf_op jit(solution)/shard_map/forward/pallas_call | solution.py:107
  98.2 3.3 %weight_grad.1 = (bf16[192,768]{1,0:T(8,128)(2,1)S(1)}, bf16[192,768]{1,0:T(8,128)(2,1)S(1)}, bf16[192,768]{1,0:T(8,128)(2,1)S(1)}, bf16[192,768]{1,0:T(8,128)(2...) custom-call(s32[18]{0:T(128)S(1)} %compare_select_fusion.4.info, ...), custom_call_target="tpu_custom_call" | custom-call | flops 2415919104 | bytes 8650824 | tf_op jit(solution)/shard_map/weight_grad/pallas_call | solution.py:107
  104.0 2.1 %down.1 = (bf16[512,768]{1,0:T(8,128)(2,1)S(1)}, bf16[512,768]{1,0:T(8,128)(2,1)S(1)}, f32[1,768]{1,0:T(1,128)S(1)}) custom-call(s32[18]{0:T(128)S(1)} %compare_select_fusion.4.info, bf16[1024,768]{1,0:T(8,128)(2,1)S(1)} %get-tuple-element.255.act_ref, bf16[256,768]{1,0:T(8,128)(2,1)S(1)} %copy-done.3, bf16[256,768]{1,0:T(8,128)(2,1)S(1)} %collective-permute-done.19.refs_1_, ...), custom_call_target="tpu_custom_call" | custom-call | flops 1207959552 | bytes 7081032 | tf_op jit(solution)/shard_map/down/pallas_call | solution.py:107
  106.1 6.2 %collective-permute-done.34 = bf16[192,768]{1,0:T(8,128)(2,1)S(1)} collective-permute-done((bf16[192,768]{1,0:T(8,128)(2,1)S(1)}, bf16[192,768]{1,0:T(8,128)(2,1)S(1)}, u32[]{:S(2)}, u32[]{:S(2)}) %collective-permute-start.34) | collective-permute-done | bytes 294944 | tf_op jit(solution)/shard_map/ppermute | solution.py:566
  113.8 2.2 %branch.1 = (f32[256,768]{1,0:T(8,128)S(1)}, bf16[256,1024]{1,0:T(8,128)(2,1)S(1)}, f32[3,768]{1,0:T(4,128)S(1)}, bf16[256,192]{1,0:T(8,128)(2,1)S(1)}, bf16[256...) custom-call(s32[18]{0:T(128)S(1)} %compare_select_fusion.4.info, f32[3,768]{1,0:T(4,128)S(1)} %bitcast.31, ...), custom_call_target="tpu_custom_call" | custom-call | flops 301989888 | bytes 5952584 | tf_op jit(solution)/shard_map/branch/pallas_call | solution.py:107
  120.4 5.1 %collective-permute-done.40 = bf16[192,768]{1,0:T(8,128)(2,1)S(1)} collective-permute-done((bf16[192,768]{1,0:T(8,128)(2,1)S(1)}, bf16[192,768]{1,0:T(8,128)(2,1)S(1)}, u32[]{:S(2)}, u32[]{:S(2)}) %collective-permute-start.40) | collective-permute-done | bytes 294944 | tf_op jit(solution)/shard_map/ppermute | solution.py:566
  126.6 1.8 collective-permute-start.42
  130.2 9.4 %attend_back.1.grad_ref = bf16[1024,640]{1,0:T(8,128)(2,1)S(1)} custom-call(s32[18]{0:T(128)S(1)} %compare_select_fusion.4.info, f32[1024,128]{1,0:T(8,128)S(1)} %get-tuple-element.194.refs_1_.cos_ref, f32[1024,128]{1,0:T(8,128)S(1)} %get-tuple-element.195.refs_2_.sin_ref, bf16[1024,384]{1,0:T(8,128)(2,1)S(1)} %get-tuple-element.272.q_ref, ...), custom_call_target="tpu_custom_call" | custom-call | flops 4026531840 | bytes 5931080 | tf_op jit(solution)/shard_map/attend_back/pallas_call | solution.py:107
  139.6 2.1 %qkv_grad.1 = (bf16[96,768]{1,0:T(8,128)(2,1)S(1)}, bf16[96,768]{1,0:T(8,128)(2,1)S(1)}, bf16[96,768]{1,0:T(8,128)(2,1)S(1)}, bf16[96,768]{1,0:T(8,128)(2,1)S(1)...) custom-call(s32[18]{0:T(128)S(1)} %compare_select_fusion.4.info, ...), custom_call_target="tpu_custom_call" | custom-call | flops 1006632960 | bytes 4948040 | tf_op jit(solution)/shard_map/qkv_grad/pallas_call | solution.py:107
  143.5 2.2 %hidden_grad.1 = (bf16[512,768]{1,0:T(8,128)(2,1)S(1)}, bf16[512,768]{1,0:T(8,128)(2,1)S(1)}) custom-call(s32[18]{0:T(128)S(1)} %compare_select_fusion.4.info, bf16[1024,640]{1,0:T(8,128)(2,1)S(1)} %attend_back.1.grad_ref, bf16[768,768]{1,0:T(8,128)(2,1)S(1)} %get-tuple-element.299.weight_ref), custom_call_target="tpu_custom_call" | custom-call | flops 1006632960 | bytes 4063304 | tf_op jit(solution)/shard_map/hidden_grad/pallas_call | solution.py:107
  147.2 2.4 %collective-permute-start.51 = (bf16[192,768]{1,0:T(8,128)(2,1)S(1)}, bf16[192,768]{1,0:T(8,128)(2,1)S(1)}, u32[]{:S(2)}, u32[]{:S(2)}) collective-permute-start(bf16[192,768]{1,0:T(8,128)(2,1)S(1)} %add_convert_fusion.5), channel_id=1, source_target_pairs={{0,8},{4,12},{8,24},{12,28},{16,0},{20,4},{24,16},{28,20},{1,9},{5... | collective-permute-start | bytes 884744 | tf_op jit(solution)/shard_map/ppermute | solution.py:581
  152.7 8.1 %collective-permute-done.48 = bf16[96,768]{1,0:T(8,128)(2,1)S(1)} collective-permute-done((bf16[96,768]{1,0:T(8,128)(2,1)S(1)}, bf16[96,768]{1,0:T(8,128)(2,1)S(1)}, u32[]{:S(2)}, u32[]{:S(2)}) %collective-permute-start.48) | collective-permute-done | bytes 147488 | tf_op jit(solution)/shard_map/ppermute | solution.py:581
  162.1 1.7 collective-permute-start.53
  165.2 3.2 %collective-permute-done.53 = bf16[96,768]{1,0:T(8,128)(2,1)S(1)} collective-permute-done((bf16[96,768]{1,0:T(8,128)(2,1)S(1)}, bf16[96,768]{1,0:T(8,128)(2,1)S(1)}, u32[]{:S(2)}, u32[]{:S(2)}) %collective-permute-start.53) | collective-permute-done | bytes 147488 | tf_op jit(solution)/shard_map/ppermute | solution.py:581
  177.0 1.9 %input.1 = bf16[256,768]{1,0:T(8,128)(2,1)} custom-call(s32[18]{0:T(128)S(1)} %compare_select_fusion.4.info, f32[1,768]{1,0:T(1,128)S(1)} %reshape.139.refs_0_.gain, bf16[256,768]{1,0:T(8,128)(2,1)S(1)} %copy-done, f32[256,768]{1,0:T(8,128)S(1)} %get-tuple-element.326.mid_ref, bf16[512,768]{1,0:T(8,128)(2,1)S(1)} %get-tuple-element.306.own_ref, ...), custom_call_target="tpu_custom_call" | custom-call | flops 3932160 | bytes 3542088 | tf_op jit(solution)/shard_map/input/pallas_call | solution.py:107
  182.0 3.3 %collective-permute-done.60.refs_1_ = bf16[96,768]{1,0:T(8,128)(2,1)S(1)} collective-permute-done((bf16[96,768]{1,0:T(8,128)(2,1)S(1)}, bf16[96,768]{1,0:T(8,128)(2,1)S(1)}, u32[]{:S(2)}, u32[]{:S(2)}) %collective-permute-start.60) | collective-permute-done | bytes 147488 | tf_op jit(solution)/shard_map/ppermute | solution.py:551
  186.8 2.6 %finish_qkv.1 = (f32[96,2304]{1,0:T(8,128)}, f32[96,768]{1,0:T(8,128)}, f32[1,96]{1,0:T(1,128)}) custom-call(s32[18]{0:T(128)S(1)} %compare_select_fusion.4.info, bf16[96,768]{1,0:T(8,128)(2,1)S(1)} %add_convert_fusion.8.refs_0_, bf16[96,768]{1,0:T(8,128)(2,1)S(1)} %collective-permute-done.60.refs_1_, bf16[96,768]{1,0:T(8,128)(2,1)S(1)} %collective-permute-done.61.refs_2_, ...), custom_call_target="tpu_custom_call" | custom-call | bytes 2212680 | tf_op jit(solution)/shard_map/finish_qkv/pallas_call | solution.py:107
  189.4 2.4 %finish_mlp.1 = (f32[96,3072]{1,0:T(8,128)}, f32[384,768]{1,0:T(8,128)}) custom-call(s32[18]{0:T(128)S(1)} %compare_select_fusion.4.info, bf16[192,768]{1,0:T(8,128)(2,1)S(1)} %add_convert_fusion.4.refs_0_, bf16[192,768]{1,0:T(8,128)(2,1)S(1)} %collective-permute-done.65.refs_1_, bf16[192,768]{1,0:T(8,128)(2,1)S(1)} %collective-permute-done.66.refs_2_, ...), custom_call_target="tpu_custom_call" | custom-call | bytes 3539016 | tf_op jit(solution)/shard_map/finish_mlp/pallas_call | solution.py:107
  (191 shorter events, 72.9 us)
Async XLA Ops:
  7.3 19.6 %collective-permute-start.4 = (bf16[256,768]{1,0:T(8,128)(2,1)}, bf16[256,768]{1,0:T(8,128)(2,1)S(1)}, u32[]{:S(2)}, u32[]{:S(2)}) collective-permute-start(bf16[256,768]{1,0:T(8,128)(2,1)} %tok_ref.1), channel_id=1, source_target_pairs={{0,2},{1,3},{2,0},{3,1},{4,6},{5,7},{6,4},{7,5},{8,10},{9,11},{10,... | collective-permute-start | bytes 1179656 | tf_op jit(solution)/shard_map/ppermute | solution.py:551
  11.1 15.8 %collective-permute-start.5 = (bf16[256,768]{1,0:T(8,128)(2,1)}, bf16[256,768]{1,0:T(8,128)(2,1)S(1)}, u32[]{:S(2)}, u32[]{:S(2)}) collective-permute-start(bf16[256,768]{1,0:T(8,128)(2,1)} %tok_ref.1), channel_id=1, source_target_pairs={{0,1},{1,0},{2,3},{3,2},{4,5},{5,4},{6,7},{7,6},{8,9},{9,8},{10,11... | collective-permute-start | bytes 1179656 | tf_op jit(solution)/shard_map/ppermute | solution.py:551
  12.4 14.5 %collective-permute-start.2 = (bf16[96,768]{1,0:T(8,128)(2,1)S(1)}, bf16[96,768]{1,0:T(8,128)(2,1)S(1)}, u32[]{:S(2)}, u32[]{:S(2)}) collective-permute-start(bf16[96,768]{1,0:T(8,128)(2,1)S(1)} %collective-permute-done.refs_9_), channel_id=1, source_target_pairs={{0,8},{4,12},{8,24},{12,28},{16,0},{20,4},{24,16},{28,20},{1,9},{5... | collective-permute-start | bytes 442376 | tf_op jit(solution)/shard_map/ppermute | solution.py:581
  15.0 11.9 %collective-permute-start.3 = (bf16[96,768]{1,0:T(8,128)(2,1)S(1)}, bf16[96,768]{1,0:T(8,128)(2,1)S(1)}, u32[]{:S(2)}, u32[]{:S(2)}) collective-permute-start(bf16[96,768]{1,0:T(8,128)(2,1)S(1)} %collective-permute-done.refs_9_), channel_id=1, source_target_pairs={{0,4},{4,0},{8,12},{12,8},{16,20},{20,16},{24,28},{28,24},{1,5},{5... | collective-permute-start | bytes 442376 | tf_op jit(solution)/shard_map/ppermute | solution.py:566
  17.1 9.6 %all-to-all-start = ((bf16[8,2,96]{2,1,0:T(2,128)(2,1)}), bf16[8,2,96]{2,1,0:T(2,128)(2,1)S(1)}, u32[]{:S(2)}, u32[]{:S(2)}) async-start(bf16[8,2,96]{2,1,0:T(2,128)(2,1)} %copy.19), calls=%async_computation | async-start | bytes 8192 | tf_op jit(solution)/shard_map/all_to_all | solution.py:679
  33.5 14.7 %collective-permute-start.12 = (bf16[192,768]{1,0:T(8,128)(2,1)S(1)}, bf16[192,768]{1,0:T(8,128)(2,1)S(1)}, u32[]{:S(2)}, u32[]{:S(2)}) collective-permute-start(bf16[192,768]{1,0:T(8,128)(2,1)S(1)} %second_part.1.refs_4_), channel_id=1, source_target_pairs={{0,8},{4,12},{8,24},{12,28},{16,0},{20,4},{24,16},{28,20},{1,9},{5... | collective-permute-start | bytes 884744 | tf_op jit(solution)/shard_map/ppermute | solution.py:581
  42.1 9.8 %collective-permute-start.19 = (bf16[256,768]{1,0:T(8,128)(2,1)S(1)}, bf16[256,768]{1,0:T(8,128)(2,1)S(1)}, u32[]{:S(2)}, u32[]{:S(2)}) collective-permute-start(bf16[256,768]{1,0:T(8,128)(2,1)S(1)} %copy-done.3), channel_id=1, source_target_pairs={{0,2},{1,3},{2,0},{3,1},{4,6},{5,7},{6,4},{7,5},{8,10},{9,11},{10,... | collective-permute-start | bytes 1179656 | tf_op jit(solution)/shard_map/ppermute | solution.py:551
  48.2 13.2 %collective-permute-start.15 = (bf16[192,768]{1,0:T(8,128)(2,1)S(1)}, bf16[192,768]{1,0:T(8,128)(2,1)S(1)}, u32[]{:S(2)}, u32[]{:S(2)}) collective-permute-start(bf16[192,768]{1,0:T(8,128)(2,1)S(1)} %collective-permute-done.12.refs_6_), channel_id=1, source_target_pairs={{0,8},{4,12},{8,24},{12,28},{16,0},{20,4},{24,16},{28,20},{1,9},{5... | collective-permute-start | bytes 884744 | tf_op jit(solution)/shard_map/ppermute | solution.py:581
  49.5 12.0 %collective-permute-start.16 = (bf16[192,768]{1,0:T(8,128)(2,1)S(1)}, bf16[192,768]{1,0:T(8,128)(2,1)S(1)}, u32[]{:S(2)}, u32[]{:S(2)}) collective-permute-start(bf16[192,768]{1,0:T(8,128)(2,1)S(1)} %collective-permute-done.12.refs_6_), channel_id=1, source_target_pairs={{0,4},{4,0},{8,12},{12,8},{16,20},{20,16},{24,28},{28,24},{1,5},{5... | collective-permute-start | bytes 884744 | tf_op jit(solution)/shard_map/ppermute | solution.py:566
  50.0 11.5 %collective-permute-start.17 = (bf16[768,192]{1,0:T(8,128)(2,1)S(1)}, bf16[768,192]{1,0:T(8,128)(2,1)S(1)}, u32[]{:S(2)}, u32[]{:S(2)}) collective-permute-start(bf16[768,192]{1,0:T(8,128)(2,1)S(1)} %get-tuple-element.217.refs_0_), channel_id=1, source_target_pairs={{0,2},{1,3},{2,0},{3,1},{4,6},{5,7},{6,4},{7,5},{8,10},{9,11},{10,... | collective-permute-start | bytes 884744 | tf_op jit(solution)/shard_map/ppermute | solution.py:551
  50.6 10.9 %collective-permute-start.18 = (bf16[768,192]{1,0:T(8,128)(2,1)S(1)}, bf16[768,192]{1,0:T(8,128)(2,1)S(1)}, u32[]{:S(2)}, u32[]{:S(2)}) collective-permute-start(bf16[768,192]{1,0:T(8,128)(2,1)S(1)} %get-tuple-element.217.refs_0_), channel_id=1, source_target_pairs={{0,1},{1,0},{2,3},{3,2},{4,5},{5,4},{6,7},{7,6},{8,9},{9,8},{10,11... | collective-permute-start | bytes 884744 | tf_op jit(solution)/shard_map/ppermute | solution.py:551
  52.0 9.5 %collective-permute-start.20 = (f32[1,3,768]{2,1,0:T(4,128)S(1)}, f32[1,3,768]{2,1,0:T(4,128)S(1)}, u32[]{:S(2)}, u32[]{:S(2)}) collective-permute-start(f32[1,3,768]{2,1,0:T(4,128)S(1)} %slice_select_fusion.2), channel_id=1, source_target_pairs={{0,4},{4,0},{8,12},{12,8},{16,20},{20,16},{24,28},{28,24},{1,5},{5... | collective-permute-start | bytes 27656 | tf_op jit(solution)/shard_map/ppermute | solution.py:620
  64.8 10.3 %collective-permute-start.27 = (bf16[192,768]{1,0:T(8,128)(2,1)S(1)}, bf16[192,768]{1,0:T(8,128)(2,1)S(1)}, u32[]{:S(2)}, u32[]{:S(2)}) collective-permute-start(bf16[192,768]{1,0:T(8,128)(2,1)S(1)} %collective-permute-done.15.refs_8_), channel_id=1, source_target_pairs={{0,8},{4,12},{8,24},{12,28},{16,0},{20,4},{24,16},{28,20},{1,9},{5... | collective-permute-start | bytes 884744 | tf_op jit(solution)/shard_map/ppermute | solution.py:581
  72.8 16.1 %collective-permute-start.25 = (bf16[256,768]{1,0:T(8,128)(2,1)S(1)}, bf16[256,768]{1,0:T(8,128)(2,1)S(1)}, u32[]{:S(2)}, u32[]{:S(2)}) collective-permute-start(bf16[256,768]{1,0:T(8,128)(2,1)S(1)} %collective-permute-done.19.refs_1_), channel_id=1, source_target_pairs={{0,1},{1,0},{2,3},{3,2},{4,5},{5,4},{6,7},{7,6},{8,9},{9,8},{10,11... | collective-permute-start | bytes 1179656 | tf_op jit(solution)/shard_map/ppermute | solution.py:551
  73.5 9.9 %collective-permute-start.26 = (bf16[192,768]{1,0:T(8,128)(2,1)S(1)}, bf16[192,768]{1,0:T(8,128)(2,1)S(1)}, u32[]{:S(2)}, u32[]{:S(2)}) collective-permute-start(bf16[192,768]{1,0:T(8,128)(2,1)S(1)} %collective-permute-done.15.refs_8_), channel_id=1, source_target_pairs={{0,4},{4,0},{8,12},{12,8},{16,20},{20,16},{24,28},{28,24},{1,5},{5... | collective-permute-start | bytes 884744 | tf_op jit(solution)/shard_map/ppermute | solution.py:566
  75.0 13.8 %collective-permute-start.28 = (bf16[192,768]{1,0:T(8,128)(2,1)S(1)}, bf16[192,768]{1,0:T(8,128)(2,1)S(1)}, u32[]{:S(2)}, u32[]{:S(2)}) collective-permute-start(bf16[192,768]{1,0:T(8,128)(2,1)S(1)} %collective-permute-done.27.refs_10_), channel_id=1, source_target_pairs={{0,4},{4,0},{8,12},{12,8},{16,20},{20,16},{24,28},{28,24},{1,5},{5... | collective-permute-start | bytes 884744 | tf_op jit(solution)/shard_map/ppermute | solution.py:566
  75.6 15.8 %collective-permute-start.29 = (bf16[256,768]{1,0:T(8,128)(2,1)S(1)}, bf16[256,768]{1,0:T(8,128)(2,1)S(1)}, u32[]{:S(2)}, u32[]{:S(2)}) collective-permute-start(bf16[256,768]{1,0:T(8,128)(2,1)S(1)} %get-tuple-element.234.refs_0_), channel_id=1, source_target_pairs={{0,2},{1,3},{2,0},{3,1},{4,6},{5,7},{6,4},{7,5},{8,10},{9,11},{10,... | collective-permute-start | bytes 1179656 | tf_op jit(solution)/shard_map/ppermute | solution.py:551
  77.2 14.2 %collective-permute-start.30 = (bf16[256,768]{1,0:T(8,128)(2,1)S(1)}, bf16[256,768]{1,0:T(8,128)(2,1)S(1)}, u32[]{:S(2)}, u32[]{:S(2)}) collective-permute-start(bf16[256,768]{1,0:T(8,128)(2,1)S(1)} %get-tuple-element.234.refs_0_), channel_id=1, source_target_pairs={{0,1},{1,0},{2,3},{3,2},{4,5},{5,4},{6,7},{7,6},{8,9},{9,8},{10,11... | collective-permute-start | bytes 1179656 | tf_op jit(solution)/shard_map/ppermute | solution.py:551
  101.7 11.5 %collective-permute-start.33 = (bf16[256,768]{1,0:T(8,128)(2,1)S(1)}, bf16[256,768]{1,0:T(8,128)(2,1)S(1)}, u32[]{:S(2)}, u32[]{:S(2)}) collective-permute-start(bf16[256,768]{1,0:T(8,128)(2,1)S(1)} %add_convert_fusion.3), channel_id=1, source_target_pairs={{0,2},{1,3},{2,0},{3,1},{4,6},{5,7},{6,4},{7,5},{8,10},{9,11},{10,... | collective-permute-start | bytes 1179656 | tf_op jit(solution)/shard_map/ppermute | solution.py:551
  116.6 10.0 %collective-permute-start.41 = (bf16[192,768]{1,0:T(8,128)(2,1)S(1)}, bf16[192,768]{1,0:T(8,128)(2,1)S(1)}, u32[]{:S(2)}, u32[]{:S(2)}) collective-permute-start(bf16[192,768]{1,0:T(8,128)(2,1)S(1)} %add_convert_fusion.7), channel_id=1, source_target_pairs={{0,8},{4,12},{8,24},{12,28},{16,0},{20,4},{24,16},{28,20},{1,9},{5... | collective-permute-start | bytes 884744 | tf_op jit(solution)/shard_map/ppermute | solution.py:581
  116.7 9.9 %collective-permute-start.36 = (bf16[256,192]{1,0:T(8,128)(2,1)S(1)}, bf16[256,192]{1,0:T(8,128)(2,1)S(1)}, u32[]{:S(2)}, u32[]{:S(2)}) collective-permute-start(bf16[256,192]{1,0:T(8,128)(2,1)S(1)} %get-tuple-element.274), channel_id=1, source_target_pairs={{0,2},{1,3},{2,0},{3,1},{4,6},{5,7},{6,4},{7,5},{8,10},{9,11},{10,... | collective-permute-start | bytes 294920 | tf_op jit(solution)/shard_map/ppermute | solution.py:551
  118.4 21.2 %collective-permute-start.43 = (f32[3,768]{1,0:T(4,128)S(1)}, f32[3,768]{1,0:T(4,128)S(1)}, u32[]{:S(2)}, u32[]{:S(2)}) collective-permute-start(f32[3,768]{1,0:T(4,128)S(1)} %get-tuple-element.286), channel_id=1, source_target_pairs={{0,1},{1,0},{2,3},{3,2},{4,5},{5,4},{6,7},{7,6},{8,9},{9,8},{10,11... | collective-permute-start | bytes 27656 | tf_op jit(solution)/shard_map/ppermute | solution.py:551
  126.6 12.9 %collective-permute-start.42 = (bf16[1,768,192]{2,1,0:T(8,128)(2,1)S(1)}, bf16[1,768,192]{2,1,0:T(8,128)(2,1)S(1)}, u32[]{:S(2)}, u32[]{:S(2)}) collective-permute-start(bf16[1,768,192]{2,1,0:T(8,128)(2,1)S(1)} %slice.86), channel_id=1, source_target_pairs={{0,2},{1,3},{2,0},{3,1},{4,6},{5,7},{6,4},{7,5},{8,10},{9,11},{10,... | collective-permute-start | bytes 884744 | tf_op jit(solution)/shard_map/ppermute | solution.py:551
  128.6 11.0 %collective-permute-start.45 = (bf16[192,768]{1,0:T(8,128)(2,1)S(1)}, bf16[192,768]{1,0:T(8,128)(2,1)S(1)}, u32[]{:S(2)}, u32[]{:S(2)}) collective-permute-start(bf16[192,768]{1,0:T(8,128)(2,1)S(1)} %add_convert_fusion.6), channel_id=1, source_target_pairs={{0,8},{4,12},{8,24},{12,28},{16,0},{20,4},{24,16},{28,20},{1,9},{5... | collective-permute-start | bytes 884744 | tf_op jit(solution)/shard_map/ppermute | solution.py:581
  128.9 10.6 %collective-permute-start.44 = (bf16[192,768]{1,0:T(8,128)(2,1)S(1)}, bf16[192,768]{1,0:T(8,128)(2,1)S(1)}, u32[]{:S(2)}, u32[]{:S(2)}) collective-permute-start(bf16[192,768]{1,0:T(8,128)(2,1)S(1)} %get-tuple-element.292), channel_id=1, source_target_pairs={{0,4},{4,0},{8,12},{12,8},{16,20},{20,16},{24,28},{28,24},{1,5},{5... | collective-permute-start | bytes 884744 | tf_op jit(solution)/shard_map/ppermute | solution.py:566
  147.2 14.8 %collective-permute-start.51 = (bf16[192,768]{1,0:T(8,128)(2,1)S(1)}, bf16[192,768]{1,0:T(8,128)(2,1)S(1)}, u32[]{:S(2)}, u32[]{:S(2)}) collective-permute-start(bf16[192,768]{1,0:T(8,128)(2,1)S(1)} %add_convert_fusion.5), channel_id=1, source_target_pairs={{0,8},{4,12},{8,24},{12,28},{16,0},{20,4},{24,16},{28,20},{1,9},{5... | collective-permute-start | bytes 884744 | tf_op jit(solution)/shard_map/ppermute | solution.py:581
  149.5 12.5 %collective-permute-start.52 = (bf16[192,768]{1,0:T(8,128)(2,1)S(1)}, bf16[192,768]{1,0:T(8,128)(2,1)S(1)}, u32[]{:S(2)}, u32[]{:S(2)}) collective-permute-start(bf16[192,768]{1,0:T(8,128)(2,1)S(1)} %get-tuple-element.313), channel_id=1, source_target_pairs={{0,4},{4,0},{8,12},{12,8},{16,20},{20,16},{24,28},{28,24},{1,5},{5... | collective-permute-start | bytes 884744 | tf_op jit(solution)/shard_map/ppermute | solution.py:566
  150.9 14.3 %collective-permute-start.55 = (bf16[256,768]{1,0:T(8,128)(2,1)S(1)}, bf16[256,768]{1,0:T(8,128)(2,1)S(1)}, u32[]{:S(2)}, u32[]{:S(2)}) collective-permute-start(bf16[256,768]{1,0:T(8,128)(2,1)S(1)} %add_convert_fusion.1), channel_id=1, source_target_pairs={{0,2},{1,3},{2,0},{3,1},{4,6},{5,7},{6,4},{7,5},{8,10},{9,11},{10,... | collective-permute-start | bytes 1179656 | tf_op jit(solution)/shard_map/ppermute | solution.py:551
  151.7 10.3 %collective-permute-start.49 = (bf16[96,768]{1,0:T(8,128)(2,1)S(1)}, bf16[96,768]{1,0:T(8,128)(2,1)S(1)}, u32[]{:S(2)}, u32[]{:S(2)}) collective-permute-start(bf16[96,768]{1,0:T(8,128)(2,1)S(1)} %get-tuple-element.305), channel_id=1, source_target_pairs={{0,4},{4,0},{8,12},{12,8},{16,20},{20,16},{24,28},{28,24},{1,5},{5... | collective-permute-start | bytes 442376 | tf_op jit(solution)/shard_map/ppermute | solution.py:566
  164.5 9.9 %collective-permute-start.59 = (bf16[256,768]{1,0:T(8,128)(2,1)S(1)}, bf16[256,768]{1,0:T(8,128)(2,1)S(1)}, u32[]{:S(2)}, u32[]{:S(2)}) collective-permute-start(bf16[256,768]{1,0:T(8,128)(2,1)S(1)} %add_convert_fusion.2), channel_id=1, source_target_pairs={{0,2},{1,3},{2,0},{3,1},{4,6},{5,7},{6,4},{7,5},{8,10},{9,11},{10,... | collective-permute-start | bytes 1179656 | tf_op jit(solution)/shard_map/ppermute | solution.py:551
  169.0 9.9 %collective-permute-start.57 = (bf16[96,768]{1,0:T(8,128)(2,1)S(1)}, bf16[96,768]{1,0:T(8,128)(2,1)S(1)}, u32[]{:S(2)}, u32[]{:S(2)}) collective-permute-start(bf16[96,768]{1,0:T(8,128)(2,1)S(1)} %add_convert_fusion.9), channel_id=1, source_target_pairs={{0,8},{4,12},{8,24},{12,28},{16,0},{20,4},{24,16},{28,20},{1,9},{5... | collective-permute-start | bytes 442376 | tf_op jit(solution)/shard_map/ppermute | solution.py:581
  176.9 12.4 %collective-permute-start.66 = (bf16[192,768]{1,0:T(8,128)(2,1)S(1)}, bf16[192,768]{1,0:T(8,128)(2,1)S(1)}, u32[]{:S(2)}, u32[]{:S(2)}) collective-permute-start(bf16[192,768]{1,0:T(8,128)(2,1)S(1)} %add_convert_fusion.4.refs_0_), channel_id=1, source_target_pairs={{0,1},{1,0},{2,3},{3,2},{4,5},{5,4},{6,7},{7,6},{8,9},{9,8},{10,11... | collective-permute-start | bytes 884744 | tf_op jit(solution)/shard_map/ppermute | solution.py:551
  (46 other events, 281.0 us)
where the time goes:
time: 192 us
  waiting for transfers between devices  63.6 us (33%)
  starting transfers between devices  61.3 us (32%)
  Pallas kernels  51.1 us (27%)
  local copies, waits for them, and re-layouts  6.99 us (4%)
  other arithmetic  5.49 us (3%)
    pallas_call x18, Pallas kernels, run(): return call(*args)  51.1 us
    ppermute x16, waiting for transfers between devices, pair(): lax.ppermute(values_in, 'dp', [(i, i ^ 1) for i in range(lax.axis_size('d...  28.1 us
    ppermute x34, starting transfers between devices, hop(): lax.ppermute(values_in, 'seq', [(i, i ^ mask) for i in range(lax.axis_siz...  19.6 us
    ppermute x34, waiting for transfers between devices, hop(): lax.ppermute(values_in, 'seq', [(i, i ^ mask) for i in range(lax.axis_siz...  17.6 us
    ppermute x16, starting transfers between devices, pair(): lax.ppermute(values_in, 'dp', [(i, i ^ 1) for i in range(lax.axis_size('d...  15.2 us
    ppermute x12, waiting for transfers between devices, onward(): return lax.ppermute(values_in, 'dp', ring_next(lax.axis_size('dp')))  14.1 us
    ppermute x12, starting transfers between devices, onward(): return lax.ppermute(values_in, 'dp', ring_next(lax.axis_size('dp')))  13.6 us
    ppermute x6, starting transfers between devices, beyond(): lax.ppermute(values_in, 'dp', [(i, i ^ mask) for i in range(lax.axis_size...  9.57 us
  transfers between devices with their start and end apart: 69, of which 27 were waited for; matrix products, arithmetic and copies ran while one was open for 5% of the time, Pallas kernels for 22%

commit v1 on v0

--- a/solution.py
+++ b/solution.py
@@ -785,7 +785,7 @@
     att_own = [att_parts[0]] + [hop(att_parts[j], MASKS[j]) for j in (1, 2, 3)]
     out_blocks = [own_out, chip_out, core_out, hop(after(chip_out, att_own[2]), 1)]
     if ringed:
-        att_own = lax.optimization_barrier(att_own)
+        att_own, held[3], beside[2] = lax.optimization_barrier((att_own, held[3], beside[2]))
     middle, hidden_two, att_ordered = run(
         middle_kernel,
         [
@@ -967,19 +967,18 @@
         qkv_ring = low(wide(qkv_keep[2]) + wide(qkv_taken) + wide(qkv_carried))
         qkv_carried = onward(qkv_ring)
         qkv_taken = pair(after(qkv_give[3], qkv_ring))
-    gq_chip = hop(gq_send, 2)
     if ringed:
         sum_mlp = low(wide(mlp_keep[0]) + wide(mlp_taken) + wide(mlp_carried))
-        qkv_carried, qkv_taken, mlp_chip, mod_other = lax.optimization_barrier(
-            (qkv_carried, qkv_taken, mlp_chip, mod_other)
+        qkv_carried, qkv_taken, mlp_chip, mod_other, gq_send = lax.optimization_barrier(
+            (qkv_carried, qkv_taken, mlp_chip, mod_other, gq_send)
         )
         qkv_ring = low(wide(qkv_keep[3]) + wide(qkv_taken) + wide(qkv_carried))
         qkv_carried = onward(qkv_ring)
         qkv_taken = pair(after(qkv_give[0], qkv_ring))
     else:
         sum_mlp = low(dp_sum_direct(grad_weights[0]))
+    gq_chip = hop(gq_send, 2)
     grad_mod = doubled(grad_mod, mod_other, high[0])
-    sum_mlp, gq_chip = lax.optimization_barrier((sum_mlp, gq_chip))
     mlp_blocks = four(sum_mlp)
     grad_inputs = run(
         input_kernel,
@@ -992,8 +991,8 @@
         grad_mod = doubled(grad_mod, beyond(grad_mod, 1 << place), high[place])
     grad_mods = grad_mod.reshape(data_count, 3 * width)
     if ringed:
-        qkv_carried, qkv_taken, grad_inputs = lax.optimization_barrier(
-            (qkv_carried, qkv_taken, grad_inputs)
+        qkv_carried, qkv_taken, gq_chip = lax.optimization_barrier(
+            (qkv_carried, qkv_taken, gq_chip)
         )
         sum_qkv = low(wide(qkv_keep[0]) + wide(qkv_taken) + wide(qkv_carried))
     else:
@@ -1012,6 +1011,10 @@
         scratch=[pltpu.VMEM((seq_count,) + block_shape, jnp.bfloat16)],
         name="finish_mlp",
     )
+    qkv_far, final_up, grad_inputs = lax.optimization_barrier(
+        (hop(sum_qkv, 2), final_up, grad_inputs)
+    )
+    qkv_blocks = [sum_qkv, qkv_far, hop(after(sum_qkv, qkv_far), 1), hop(qkv_far, 1)]
     final_qkv, final_out, final_gain = run(
         finish_qkv_kernel,
         [
@@ -1019,7 +1022,7 @@
             shaped(w_out.shape, jnp.float32),
             shaped((1, rows), jnp.float32),
         ],
-        [info] + four(sum_qkv) + [w_qkv, wide(ln1_gain).reshape(1, rows)],
+        [info] + qkv_blocks + [w_qkv, wide(ln1_gain).reshape(1, rows)],
         0,
         scratch=[pltpu.VMEM((seq_count, rows, 4 * local_width), jnp.bfloat16)],
         name="finish_qkv",

time: 192 us -> 186 us (0.969)
  waiting for transfers between devices: 63.6 us -> 55 us
  starting transfers between devices: 61.3 us -> 63.8 us
    ppermute x16, waiting for transfers between devices: 28.1 us -> 19.1 us  [pair(): lax.ppermute(values_in, 'dp', [(i, i ^ 1) for i in range(lax.axis_size('d...]
    ppermute x34, waiting for transfers between devices: 17.6 us -> 15.2 us  [hop(): lax.ppermute(values_in, 'seq', [(i, i ^ mask) for i in range(lax.axis_siz...]
    ppermute x16, starting transfers between devices: 15.2 us -> 17.5 us  [pair(): lax.ppermute(values_in, 'dp', [(i, i ^ 1) for i in range(lax.axis_size('d...]
    ppermute x12, starting transfers between devices: 13.6 us -> 15.8 us  [onward(): return lax.ppermute(values_in, 'dp', ring_next(lax.axis_size('dp')))]
  transfers between devices with their start and end apart: 69 -> 69, of which waited for: 27 -> 24; matrix products, arithmetic and copies ran while one was open for 5% -> 5% of each run, Pallas kernels for 22% -> 21%
where the time goes in v1:
time: 186 us
  starting transfers between devices  63.8 us (34%)
  waiting for transfers between devices  55 us (30%)
  Pallas kernels  51.1 us (27%)
  local copies, waits for them, and re-layouts  6.99 us (4%)
  other arithmetic  5.46 us (3%)
  between operations  1.87 us (1%)
    pallas_call x18, Pallas kernels, run(): return call(*args)  51.1 us
    ppermute x16, waiting for transfers between devices, pair(): lax.ppermute(values_in, 'dp', [(i, i ^ 1) for i in range(lax.axis_size('d...  19.1 us
    ppermute x34, starting transfers between devices, hop(): lax.ppermute(values_in, 'seq', [(i, i ^ mask) for i in range(lax.axis_siz...  17.8 us
    ppermute x16, starting transfers between devices, pair(): lax.ppermute(values_in, 'dp', [(i, i ^ 1) for i in range(lax.axis_size('d...  17.5 us
    ppermute x12, starting transfers between devices, onward(): return lax.ppermute(values_in, 'dp', ring_next(lax.axis_size('dp')))  15.8 us
    ppermute x34, waiting for transfers between devices, hop(): lax.ppermute(values_in, 'seq', [(i, i ^ mask) for i in range(lax.axis_siz...  15.2 us
    ppermute x12, waiting for transfers between devices, onward(): return lax.ppermute(values_in, 'dp', ring_next(lax.axis_size('dp')))  15.1 us
    ppermute x6, starting transfers between devices, beyond(): lax.ppermute(values_in, 'dp', [(i, i ^ mask) for i in range(lax.axis_size...  9.32 us
  transfers between devices with their start and end apart: 69, of which 24 were waited for; matrix products, arithmetic and copies ran while one was open for 5% of the time, Pallas kernels for 21%

profile of v1, /device:TPU:0, one launch (start us, length us, event | category | flops | bytes accessed | tf_op | source)
XLA Modules:
  0.0 185.6 jit_solution(4956213289255589944)
XLA Ops:
  2.7 3.1 %collective-permute-start = (bf16[96,768]{1,0:T(8,128)(2,1)S(1)}, bf16[96,768]{1,0:T(8,128)(2,1)S(1)}, u32[]{:S(2)}, u32[]{:S(2)}) collective-permute-start(bf16[96,768]{1,0:T(8,128)(2,1)S(1)} %first_part.1.refs_7_), channel_id=1, source_target_pairs={{0,8},{4,12},{8,24},{12,28},{16,0},{20,4},{24,16},{28,20},{1,9},{5... | collective-permute-start | bytes 442376 | tf_op jit(solution)/shard_map/ppermute | solution.py:581
  12.4 2.6 %collective-permute-start.2 = (bf16[96,768]{1,0:T(8,128)(2,1)S(1)}, bf16[96,768]{1,0:T(8,128)(2,1)S(1)}, u32[]{:S(2)}, u32[]{:S(2)}) collective-permute-start(bf16[96,768]{1,0:T(8,128)(2,1)S(1)} %collective-permute-done.refs_9_), channel_id=1, source_target_pairs={{0,8},{4,12},{8,24},{12,28},{16,0},{20,4},{24,16},{28,20},{1,9},{5... | collective-permute-start | bytes 442376 | tf_op jit(solution)/shard_map/ppermute | solution.py:581
  17.1 3.3 %all-to-all-start = ((bf16[8,2,96]{2,1,0:T(2,128)(2,1)}), bf16[8,2,96]{2,1,0:T(2,128)(2,1)S(1)}, u32[]{:S(2)}, u32[]{:S(2)}) async-start(bf16[8,2,96]{2,1,0:T(2,128)(2,1)} %copy.19), calls=%async_computation | async-start | bytes 8192 | tf_op jit(solution)/shard_map/all_to_all | solution.py:679
  24.1 2.6 %all-to-all-done = bf16[8,2,96]{2,1,0:T(2,128)(2,1)S(1)} async-done(((bf16[8,2,96]{2,1,0:T(2,128)(2,1)}), bf16[8,2,96]{2,1,0:T(2,128)(2,1)S(1)}, u32[]{:S(2)}, u32[]{:S(2)}) %all-to-all-start) | async-done | bytes 3104 | tf_op jit(solution)/shard_map/all_to_all | solution.py:679
  28.9 2.4 %collective-permute-start.10 = (f32[4,3,768]{2,1,0:T(4,128)S(1)}, f32[4,3,768]{2,1,0:T(4,128)S(1)}, u32[]{:S(2)}, u32[]{:S(2)}) collective-permute-start(f32[4,3,768]{2,1,0:T(4,128)S(1)} %slice_select_fusion), channel_id=1, source_target_pairs={{0,16},{4,20},{8,24},{12,28},{16,0},{20,4},{24,8},{28,12},{1,17},{... | collective-permute-start | bytes 110600 | tf_op jit(solution)/shard_map/ppermute | solution.py:620
  31.3 1.9 %fusion = (f32[1024,128]{1,0:T(8,128)S(1)}, f32[1024,128]{1,0:T(8,128)S(1)}) fusion(f32[128]{0:T(128)S(1)} %get-tuple-element.358, f32[128]{0:T(128)S(1)} %get-tuple-element.359, f32[1024]{0:T(1024)S(1)} %bitcast.42), kind=kLoop, calls=%fused_computation.10 | loop fusion | flops 262144 | bytes 1053696 | tf_op jit(solution)/shard_map/mul | solution.py:50
  36.1 3.6 %collective-permute-done.11.refs_14_ = bf16[96,768]{1,0:T(8,128)(2,1)S(1)} collective-permute-done((bf16[96,768]{1,0:T(8,128)(2,1)S(1)}, bf16[96,768]{1,0:T(8,128)(2,1)S(1)}, u32[]{:S(2)}, u32[]{:S(2)}) %collective-permute-start.11) | collective-permute-done | bytes 147488 | tf_op jit(solution)/shard_map/ppermute | solution.py:566
  43.6 4.6 %qkv.1 = (bf16[1024,768]{1,0:T(8,128)(2,1)S(1)}, bf16[768,768]{1,0:T(8,128)(2,1)S(1)}, bf16[768,192]{1,0:T(8,128)(2,1)S(1)}, bf16[1024,384]{1,0:T(8,128)(2,1)S(1...) custom-call(s32[18]{0:T(128)S(1)} %compare_select_fusion.4.info, f32[1,768]{1,0:T(1,128)S(1)} %reshape.139.refs_0_.gain, ...), custom_call_target="tpu_custom_call" | custom-call | flops 1006632960 | bytes 9210952 | tf_op jit(solution)/shard_map/qkv/pallas_call | solution.py:107
  52.0 2.2 %collective-permute-start.20 = (f32[1,3,768]{2,1,0:T(4,128)S(1)}, f32[1,3,768]{2,1,0:T(4,128)S(1)}, u32[]{:S(2)}, u32[]{:S(2)}) collective-permute-start(f32[1,3,768]{2,1,0:T(4,128)S(1)} %slice_select_fusion.2), channel_id=1, source_target_pairs={{0,4},{4,0},{8,12},{12,8},{16,20},{20,16},{24,28},{28,24},{1,5},{5... | collective-permute-start | bytes 27656 | tf_op jit(solution)/shard_map/ppermute | solution.py:620
  54.1 7.3 %attend.1 = (bf16[256,192]{1,0:T(8,128)(2,1)S(1)}, bf16[256,192]{1,0:T(8,128)(2,1)S(1)}, bf16[256,192]{1,0:T(8,128)(2,1)S(1)}, bf16[256,192]{1,0:T(8,128)(2,1)S(1)}, bf16[1024,384]{1,0:T(8,128)(2,1)S(1)}) custom-call(s32[18]{0:T(128)S(1)} %compare_select_fusion.4.info, bf16[1024,384]{1,0:T(8,128)(2,1)S(1)} %get-tuple-element.213.q_ref, ...), custom_call_target="tpu_custom_call" | custom-call | flops 1610612736 | bytes 3539016 | tf_op jit(solution)/shard_map/attend/pallas_call | solution.py:107
  64.8 4.6 %collective-permute-done.23.refs_5_ = bf16[256,192]{1,0:T(8,128)(2,1)S(1)} collective-permute-done((bf16[256,192]{1,0:T(8,128)(2,1)S(1)}, bf16[256,192]{1,0:T(8,128)(2,1)S(1)}, u32[]{:S(2)}, u32[]{:S(2)}) %collective-permute-start.23) | collective-permute-done | bytes 98336 | tf_op jit(solution)/shard_map/ppermute | solution.py:551
  76.0 7.1 %collective-permute-done.28.refs_11_ = bf16[192,768]{1,0:T(8,128)(2,1)S(1)} collective-permute-done((bf16[192,768]{1,0:T(8,128)(2,1)S(1)}, bf16[192,768]{1,0:T(8,128)(2,1)S(1)}, u32[]{:S(2)}, u32[]{:S(2)}) %collective-permute-start.28) | collective-permute-done | bytes 294944 | tf_op jit(solution)/shard_map/ppermute | solution.py:566
  83.1 2.5 %act_grad.1 = (bf16[1024,768]{1,0:T(8,128)(2,1)S(1)}, bf16[1024,768]{1,0:T(8,128)(2,1)S(1)}) custom-call(s32[18]{0:T(128)S(1)} %compare_select_fusion.4.info, f32[3,768]{1,0:T(4,128)S(1)} %bitcast.30, bf16[256,768]{1,0:T(8,128)(2,1)S(1)} %copy-done.3, bf16[256,768]{1,0:T(8,128)(2,1)S(1)} %collective-permute-done.19.refs_1_, ...), custom_call_target="tpu_custom_call" | custom-call | flops 1207959552 | bytes 7087176 | tf_op jit(solution)/shard_map/act_grad/pallas_call | solution.py:107
  87.4 4.9 %forward.1 = (bf16[1024,768]{1,0:T(8,128)(2,1)S(1)}, bf16[1024,768]{1,0:T(8,128)(2,1)S(1)}, bf16[512,768]{1,0:T(8,128)(2,1)S(1)}, bf16[512,768]{1,0:T(8,128)(2,1)S(1)}) custom-call(s32[18]{0:T(128)S(1)} %compare_select_fusion.4.info, bf16[1024,768]{1,0:T(8,128)(2,1)S(1)} %get-tuple-element.245.act_grad, bf16[256,768]{1,0:T(8,128)(2,1)S(1)} %get-tuple-element.239.refs_0_, ...), custom_call_target="tpu_custom_call" | custom-call | flops 2415919104 | bytes 10223688 | tf_op jit(solution)/shard_map/forward/pallas_call | solution.py:107
  92.5 3.3 %weight_grad.1 = (bf16[192,768]{1,0:T(8,128)(2,1)S(1)}, bf16[192,768]{1,0:T(8,128)(2,1)S(1)}, bf16[192,768]{1,0:T(8,128)(2,1)S(1)}, bf16[192,768]{1,0:T(8,128)(2...) custom-call(s32[18]{0:T(128)S(1)} %compare_select_fusion.4.info, ...), custom_call_target="tpu_custom_call" | custom-call | flops 2415919104 | bytes 8650824 | tf_op jit(solution)/shard_map/weight_grad/pallas_call | solution.py:107
  98.8 2.1 %down.1 = (bf16[512,768]{1,0:T(8,128)(2,1)S(1)}, bf16[512,768]{1,0:T(8,128)(2,1)S(1)}, f32[1,768]{1,0:T(1,128)S(1)}) custom-call(s32[18]{0:T(128)S(1)} %compare_select_fusion.4.info, bf16[1024,768]{1,0:T(8,128)(2,1)S(1)} %get-tuple-element.261.act_ref, bf16[256,768]{1,0:T(8,128)(2,1)S(1)} %copy-done.3, bf16[256,768]{1,0:T(8,128)(2,1)S(1)} %collective-permute-done.19.refs_1_, ...), custom_call_target="tpu_custom_call" | custom-call | flops 1207959552 | bytes 7081032 | tf_op jit(solution)/shard_map/down/pallas_call | solution.py:107
  100.9 5.6 %collective-permute-done.34 = bf16[192,768]{1,0:T(8,128)(2,1)S(1)} collective-permute-done((bf16[192,768]{1,0:T(8,128)(2,1)S(1)}, bf16[192,768]{1,0:T(8,128)(2,1)S(1)}, u32[]{:S(2)}, u32[]{:S(2)}) %collective-permute-start.34) | collective-permute-done | bytes 294944 | tf_op jit(solution)/shard_map/ppermute | solution.py:566
  108.1 2.2 %branch.1 = (f32[256,768]{1,0:T(8,128)S(1)}, bf16[256,1024]{1,0:T(8,128)(2,1)S(1)}, f32[3,768]{1,0:T(4,128)S(1)}, bf16[256,192]{1,0:T(8,128)(2,1)S(1)}, bf16[256...) custom-call(s32[18]{0:T(128)S(1)} %compare_select_fusion.4.info, f32[3,768]{1,0:T(4,128)S(1)} %bitcast.31, ...), custom_call_target="tpu_custom_call" | custom-call | flops 301989888 | bytes 5952584 | tf_op jit(solution)/shard_map/branch/pallas_call | solution.py:107
  111.7 2.1 %collective-permute-start.41 = (bf16[192,768]{1,0:T(8,128)(2,1)S(1)}, bf16[192,768]{1,0:T(8,128)(2,1)S(1)}, u32[]{:S(2)}, u32[]{:S(2)}) collective-permute-start(bf16[192,768]{1,0:T(8,128)(2,1)S(1)} %add_convert_fusion.7), channel_id=1, source_target_pairs={{0,8},{4,12},{8,24},{12,28},{16,0},{20,4},{24,16},{28,20},{1,9},{5... | collective-permute-start | bytes 884744 | tf_op jit(solution)/shard_map/ppermute | solution.py:581
  117.6 2.2 %collective-permute-done.40 = bf16[192,768]{1,0:T(8,128)(2,1)S(1)} collective-permute-done((bf16[192,768]{1,0:T(8,128)(2,1)S(1)}, bf16[192,768]{1,0:T(8,128)(2,1)S(1)}, u32[]{:S(2)}, u32[]{:S(2)}) %collective-permute-start.40) | collective-permute-done | bytes 294944 | tf_op jit(solution)/shard_map/ppermute | solution.py:566
  119.8 1.9 %collective-permute-done.41 = bf16[192,768]{1,0:T(8,128)(2,1)S(1)} collective-permute-done((bf16[192,768]{1,0:T(8,128)(2,1)S(1)}, bf16[192,768]{1,0:T(8,128)(2,1)S(1)}, u32[]{:S(2)}, u32[]{:S(2)}) %collective-permute-start.41) | collective-permute-done | bytes 294944 | tf_op jit(solution)/shard_map/ppermute | solution.py:581
  125.6 9.4 %attend_back.1.grad_ref = bf16[1024,640]{1,0:T(8,128)(2,1)S(1)} custom-call(s32[18]{0:T(128)S(1)} %compare_select_fusion.4.info, f32[1024,128]{1,0:T(8,128)S(1)} %get-tuple-element.198.refs_1_.cos_ref, f32[1024,128]{1,0:T(8,128)S(1)} %get-tuple-element.199.refs_2_.sin_ref, bf16[1024,384]{1,0:T(8,128)(2,1)S(1)} %get-tuple-element.278.q_ref, ...), custom_call_target="tpu_custom_call" | custom-call | flops 4026531840 | bytes 5931080 | tf_op jit(solution)/shard_map/attend_back/pallas_call | solution.py:107
  135.0 2.1 %qkv_grad.1 = (bf16[96,768]{1,0:T(8,128)(2,1)S(1)}, bf16[96,768]{1,0:T(8,128)(2,1)S(1)}, bf16[96,768]{1,0:T(8,128)(2,1)S(1)}, bf16[96,768]{1,0:T(8,128)(2,1)S(1)...) custom-call(s32[18]{0:T(128)S(1)} %compare_select_fusion.4.info, ...), custom_call_target="tpu_custom_call" | custom-call | flops 1006632960 | bytes 4948040 | tf_op jit(solution)/shard_map/qkv_grad/pallas_call | solution.py:107
  139.1 2.2 %hidden_grad.1 = (bf16[512,768]{1,0:T(8,128)(2,1)S(1)}, bf16[512,768]{1,0:T(8,128)(2,1)S(1)}) custom-call(s32[18]{0:T(128)S(1)} %compare_select_fusion.4.info, bf16[1024,640]{1,0:T(8,128)(2,1)S(1)} %attend_back.1.grad_ref, bf16[768,768]{1,0:T(8,128)(2,1)S(1)} %get-tuple-element.305.weight_ref), custom_call_target="tpu_custom_call" | custom-call | flops 1006632960 | bytes 4063304 | tf_op jit(solution)/shard_map/hidden_grad/pallas_call | solution.py:107
  142.4 1.9 %collective-permute-start.51 = (bf16[192,768]{1,0:T(8,128)(2,1)S(1)}, bf16[192,768]{1,0:T(8,128)(2,1)S(1)}, u32[]{:S(2)}, u32[]{:S(2)}) collective-permute-start(bf16[192,768]{1,0:T(8,128)(2,1)S(1)} %add_convert_fusion.5), channel_id=1, source_target_pairs={{0,8},{4,12},{8,24},{12,28},{16,0},{20,4},{24,16},{28,20},{1,9},{5... | collective-permute-start | bytes 884744 | tf_op jit(solution)/shard_map/ppermute | solution.py:581
  147.9 8.1 %collective-permute-done.48 = bf16[96,768]{1,0:T(8,128)(2,1)S(1)} collective-permute-done((bf16[96,768]{1,0:T(8,128)(2,1)S(1)}, bf16[96,768]{1,0:T(8,128)(2,1)S(1)}, u32[]{:S(2)}, u32[]{:S(2)}) %collective-permute-start.48) | collective-permute-done | bytes 147488 | tf_op jit(solution)/shard_map/ppermute | solution.py:581
  160.1 3.6 %collective-permute-done.53 = bf16[96,768]{1,0:T(8,128)(2,1)S(1)} collective-permute-done((bf16[96,768]{1,0:T(8,128)(2,1)S(1)}, bf16[96,768]{1,0:T(8,128)(2,1)S(1)}, u32[]{:S(2)}, u32[]{:S(2)}) %collective-permute-start.53) | collective-permute-done | bytes 147488 | tf_op jit(solution)/shard_map/ppermute | solution.py:581
  168.6 1.9 %collective-permute-done.66 = f32[2,3,768]{2,1,0:T(4,128)S(1)} collective-permute-done((f32[2,3,768]{2,1,0:T(4,128)S(1)}, f32[2,3,768]{2,1,0:T(4,128)S(1)}, u32[]{:S(2)}, u32[]{:S(2)}) %collective-permute-start.66) | collective-permute-done | bytes 18464 | tf_op jit(solution)/shard_map/ppermute | solution.py:620
  172.3 3.4 %collective-permute-done.59.chip_ref = bf16[256,768]{1,0:T(8,128)(2,1)S(1)} collective-permute-done((bf16[256,768]{1,0:T(8,128)(2,1)S(1)}, bf16[256,768]{1,0:T(8,128)(2,1)S(1)}, u32[]{:S(2)}, u32[]{:S(2)}) %collective-permute-start.59) | collective-permute-done | bytes 393248 | tf_op jit(solution)/shard_map/ppermute | solution.py:551
  176.7 1.9 %input.1 = bf16[256,768]{1,0:T(8,128)(2,1)} custom-call(s32[18]{0:T(128)S(1)} %compare_select_fusion.4.info, f32[1,768]{1,0:T(1,128)S(1)} %reshape.139.refs_0_.gain, bf16[256,768]{1,0:T(8,128)(2,1)S(1)} %copy-done, f32[256,768]{1,0:T(8,128)S(1)} %get-tuple-element.340.mid_ref, bf16[512,768]{1,0:T(8,128)(2,1)S(1)} %get-tuple-element.312.own_ref, ...), custom_call_target="tpu_custom_call" | custom-call | flops 3932160 | bytes 3542088 | tf_op jit(solution)/shard_map/input/pallas_call | solution.py:107
  178.7 2.4 %finish_mlp.1 = (f32[96,3072]{1,0:T(8,128)}, f32[384,768]{1,0:T(8,128)}) custom-call(s32[18]{0:T(128)S(1)} %compare_select_fusion.4.info, bf16[192,768]{1,0:T(8,128)(2,1)S(1)} %add_convert_fusion.4.refs_0_, bf16[192,768]{1,0:T(8,128)(2,1)S(1)} %collective-permute-done.61.refs_1_, bf16[192,768]{1,0:T(8,128)(2,1)S(1)} %collective-permute-done.62.refs_2_, ...), custom_call_target="tpu_custom_call" | custom-call | bytes 3539016 | tf_op jit(solution)/shard_map/finish_mlp/pallas_call | solution.py:107
  183.0 2.6 %finish_qkv.1 = (f32[96,2304]{1,0:T(8,128)}, f32[96,768]{1,0:T(8,128)}, f32[1,96]{1,0:T(1,128)}) custom-call(s32[18]{0:T(128)S(1)} %compare_select_fusion.4.info, bf16[96,768]{1,0:T(8,128)(2,1)S(1)} %add_convert_fusion.8.refs_0_, bf16[96,768]{1,0:T(8,128)(2,1)S(1)} %collective-permute-done.60.refs_1_, bf16[96,768]{1,0:T(8,128)(2,1)S(1)} %collective-permute-done.64.refs_2_, ...), custom_call_target="tpu_custom_call" | custom-call | bytes 2212680 | tf_op jit(solution)/shard_map/finish_qkv/pallas_call | solution.py:107
  (191 shorter events, 72.2 us)
Async XLA Ops:
  7.3 19.6 %collective-permute-start.4 = (bf16[256,768]{1,0:T(8,128)(2,1)}, bf16[256,768]{1,0:T(8,128)(2,1)S(1)}, u32[]{:S(2)}, u32[]{:S(2)}) collective-permute-start(bf16[256,768]{1,0:T(8,128)(2,1)} %tok_ref.1), channel_id=1, source_target_pairs={{0,2},{1,3},{2,0},{3,1},{4,6},{5,7},{6,4},{7,5},{8,10},{9,11},{10,... | collective-permute-start | bytes 1179656 | tf_op jit(solution)/shard_map/ppermute | solution.py:551
  11.1 15.8 %collective-permute-start.5 = (bf16[256,768]{1,0:T(8,128)(2,1)}, bf16[256,768]{1,0:T(8,128)(2,1)S(1)}, u32[]{:S(2)}, u32[]{:S(2)}) collective-permute-start(bf16[256,768]{1,0:T(8,128)(2,1)} %tok_ref.1), channel_id=1, source_target_pairs={{0,1},{1,0},{2,3},{3,2},{4,5},{5,4},{6,7},{7,6},{8,9},{9,8},{10,11... | collective-permute-start | bytes 1179656 | tf_op jit(solution)/shard_map/ppermute | solution.py:551
  12.4 14.5 %collective-permute-start.2 = (bf16[96,768]{1,0:T(8,128)(2,1)S(1)}, bf16[96,768]{1,0:T(8,128)(2,1)S(1)}, u32[]{:S(2)}, u32[]{:S(2)}) collective-permute-start(bf16[96,768]{1,0:T(8,128)(2,1)S(1)} %collective-permute-done.refs_9_), channel_id=1, source_target_pairs={{0,8},{4,12},{8,24},{12,28},{16,0},{20,4},{24,16},{28,20},{1,9},{5... | collective-permute-start | bytes 442376 | tf_op jit(solution)/shard_map/ppermute | solution.py:581
  15.0 11.9 %collective-permute-start.3 = (bf16[96,768]{1,0:T(8,128)(2,1)S(1)}, bf16[96,768]{1,0:T(8,128)(2,1)S(1)}, u32[]{:S(2)}, u32[]{:S(2)}) collective-permute-start(bf16[96,768]{1,0:T(8,128)(2,1)S(1)} %collective-permute-done.refs_9_), channel_id=1, source_target_pairs={{0,4},{4,0},{8,12},{12,8},{16,20},{20,16},{24,28},{28,24},{1,5},{5... | collective-permute-start | bytes 442376 | tf_op jit(solution)/shard_map/ppermute | solution.py:566
  17.1 9.6 %all-to-all-start = ((bf16[8,2,96]{2,1,0:T(2,128)(2,1)}), bf16[8,2,96]{2,1,0:T(2,128)(2,1)S(1)}, u32[]{:S(2)}, u32[]{:S(2)}) async-start(bf16[8,2,96]{2,1,0:T(2,128)(2,1)} %copy.19), calls=%async_computation | async-start | bytes 8192 | tf_op jit(solution)/shard_map/all_to_all | solution.py:679
  33.5 14.7 %collective-permute-start.12 = (bf16[192,768]{1,0:T(8,128)(2,1)S(1)}, bf16[192,768]{1,0:T(8,128)(2,1)S(1)}, u32[]{:S(2)}, u32[]{:S(2)}) collective-permute-start(bf16[192,768]{1,0:T(8,128)(2,1)S(1)} %second_part.1.refs_4_), channel_id=1, source_target_pairs={{0,8},{4,12},{8,24},{12,28},{16,0},{20,4},{24,16},{28,20},{1,9},{5... | collective-permute-start | bytes 884744 | tf_op jit(solution)/shard_map/ppermute | solution.py:581
  42.1 9.8 %collective-permute-start.19 = (bf16[256,768]{1,0:T(8,128)(2,1)S(1)}, bf16[256,768]{1,0:T(8,128)(2,1)S(1)}, u32[]{:S(2)}, u32[]{:S(2)}) collective-permute-start(bf16[256,768]{1,0:T(8,128)(2,1)S(1)} %copy-done.3), channel_id=1, source_target_pairs={{0,2},{1,3},{2,0},{3,1},{4,6},{5,7},{6,4},{7,5},{8,10},{9,11},{10,... | collective-permute-start | bytes 1179656 | tf_op jit(solution)/shard_map/ppermute | solution.py:551
  48.2 13.2 %collective-permute-start.15 = (bf16[192,768]{1,0:T(8,128)(2,1)S(1)}, bf16[192,768]{1,0:T(8,128)(2,1)S(1)}, u32[]{:S(2)}, u32[]{:S(2)}) collective-permute-start(bf16[192,768]{1,0:T(8,128)(2,1)S(1)} %collective-permute-done.12.refs_6_), channel_id=1, source_target_pairs={{0,8},{4,12},{8,24},{12,28},{16,0},{20,4},{24,16},{28,20},{1,9},{5... | collective-permute-start | bytes 884744 | tf_op jit(solution)/shard_map/ppermute | solution.py:581
  49.5 12.0 %collective-permute-start.16 = (bf16[192,768]{1,0:T(8,128)(2,1)S(1)}, bf16[192,768]{1,0:T(8,128)(2,1)S(1)}, u32[]{:S(2)}, u32[]{:S(2)}) collective-permute-start(bf16[192,768]{1,0:T(8,128)(2,1)S(1)} %collective-permute-done.12.refs_6_), channel_id=1, source_target_pairs={{0,4},{4,0},{8,12},{12,8},{16,20},{20,16},{24,28},{28,24},{1,5},{5... | collective-permute-start | bytes 884744 | tf_op jit(solution)/shard_map/ppermute | solution.py:566
  50.0 11.5 %collective-permute-start.17 = (bf16[768,192]{1,0:T(8,128)(2,1)S(1)}, bf16[768,192]{1,0:T(8,128)(2,1)S(1)}, u32[]{:S(2)}, u32[]{:S(2)}) collective-permute-start(bf16[768,192]{1,0:T(8,128)(2,1)S(1)} %get-tuple-element.221.refs_0_), channel_id=1, source_target_pairs={{0,2},{1,3},{2,0},{3,1},{4,6},{5,7},{6,4},{7,5},{8,10},{9,11},{10,... | collective-permute-start | bytes 884744 | tf_op jit(solution)/shard_map/ppermute | solution.py:551
  50.6 10.9 %collective-permute-start.18 = (bf16[768,192]{1,0:T(8,128)(2,1)S(1)}, bf16[768,192]{1,0:T(8,128)(2,1)S(1)}, u32[]{:S(2)}, u32[]{:S(2)}) collective-permute-start(bf16[768,192]{1,0:T(8,128)(2,1)S(1)} %get-tuple-element.221.refs_0_), channel_id=1, source_target_pairs={{0,1},{1,0},{2,3},{3,2},{4,5},{5,4},{6,7},{7,6},{8,9},{9,8},{10,11... | collective-permute-start | bytes 884744 | tf_op jit(solution)/shard_map/ppermute | solution.py:551
  52.0 9.5 %collective-permute-start.20 = (f32[1,3,768]{2,1,0:T(4,128)S(1)}, f32[1,3,768]{2,1,0:T(4,128)S(1)}, u32[]{:S(2)}, u32[]{:S(2)}) collective-permute-start(f32[1,3,768]{2,1,0:T(4,128)S(1)} %slice_select_fusion.2), channel_id=1, source_target_pairs={{0,4},{4,0},{8,12},{12,8},{16,20},{20,16},{24,28},{28,24},{1,5},{5... | collective-permute-start | bytes 27656 | tf_op jit(solution)/shard_map/ppermute | solution.py:620
  61.6 10.3 %collective-permute-start.25 = (bf16[192,768]{1,0:T(8,128)(2,1)S(1)}, bf16[192,768]{1,0:T(8,128)(2,1)S(1)}, u32[]{:S(2)}, u32[]{:S(2)}) collective-permute-start(bf16[192,768]{1,0:T(8,128)(2,1)S(1)} %collective-permute-done.15.refs_8_), channel_id=1, source_target_pairs={{0,8},{4,12},{8,24},{12,28},{16,0},{20,4},{24,16},{28,20},{1,9},{5... | collective-permute-start | bytes 884744 | tf_op jit(solution)/shard_map/ppermute | solution.py:581
  61.8 10.1 %collective-permute-start.26 = (bf16[192,768]{1,0:T(8,128)(2,1)S(1)}, bf16[192,768]{1,0:T(8,128)(2,1)S(1)}, u32[]{:S(2)}, u32[]{:S(2)}) collective-permute-start(bf16[192,768]{1,0:T(8,128)(2,1)S(1)} %collective-permute-done.15.refs_8_), channel_id=1, source_target_pairs={{0,4},{4,0},{8,12},{12,8},{16,20},{20,16},{24,28},{28,24},{1,5},{5... | collective-permute-start | bytes 884744 | tf_op jit(solution)/shard_map/ppermute | solution.py:566
  73.6 9.5 %collective-permute-start.27 = (bf16[256,768]{1,0:T(8,128)(2,1)S(1)}, bf16[256,768]{1,0:T(8,128)(2,1)S(1)}, u32[]{:S(2)}, u32[]{:S(2)}) collective-permute-start(bf16[256,768]{1,0:T(8,128)(2,1)S(1)} %collective-permute-done.19.refs_1_), channel_id=1, source_target_pairs={{0,1},{1,0},{2,3},{3,2},{4,5},{5,4},{6,7},{7,6},{8,9},{9,8},{10,11... | collective-permute-start | bytes 1179656 | tf_op jit(solution)/shard_map/ppermute | solution.py:551
  73.7 9.4 %collective-permute-start.28 = (bf16[192,768]{1,0:T(8,128)(2,1)S(1)}, bf16[192,768]{1,0:T(8,128)(2,1)S(1)}, u32[]{:S(2)}, u32[]{:S(2)}) collective-permute-start(bf16[192,768]{1,0:T(8,128)(2,1)S(1)} %collective-permute-done.25.refs_10_), channel_id=1, source_target_pairs={{0,4},{4,0},{8,12},{12,8},{16,20},{20,16},{24,28},{28,24},{1,5},{5... | collective-permute-start | bytes 884744 | tf_op jit(solution)/shard_map/ppermute | solution.py:566
  74.3 11.4 %collective-permute-start.29 = (bf16[256,768]{1,0:T(8,128)(2,1)S(1)}, bf16[256,768]{1,0:T(8,128)(2,1)S(1)}, u32[]{:S(2)}, u32[]{:S(2)}) collective-permute-start(bf16[256,768]{1,0:T(8,128)(2,1)S(1)} %get-tuple-element.239.refs_0_), channel_id=1, source_target_pairs={{0,2},{1,3},{2,0},{3,1},{4,6},{5,7},{6,4},{7,5},{8,10},{9,11},{10,... | collective-permute-start | bytes 1179656 | tf_op jit(solution)/shard_map/ppermute | solution.py:551
  76.0 9.7 %collective-permute-start.30 = (bf16[256,768]{1,0:T(8,128)(2,1)S(1)}, bf16[256,768]{1,0:T(8,128)(2,1)S(1)}, u32[]{:S(2)}, u32[]{:S(2)}) collective-permute-start(bf16[256,768]{1,0:T(8,128)(2,1)S(1)} %get-tuple-element.239.refs_0_), channel_id=1, source_target_pairs={{0,1},{1,0},{2,3},{3,2},{4,5},{5,4},{6,7},{7,6},{8,9},{9,8},{10,11... | collective-permute-start | bytes 1179656 | tf_op jit(solution)/shard_map/ppermute | solution.py:551
  95.9 11.5 %collective-permute-start.33 = (bf16[256,768]{1,0:T(8,128)(2,1)S(1)}, bf16[256,768]{1,0:T(8,128)(2,1)S(1)}, u32[]{:S(2)}, u32[]{:S(2)}) collective-permute-start(bf16[256,768]{1,0:T(8,128)(2,1)S(1)} %add_convert_fusion.3), channel_id=1, source_target_pairs={{0,2},{1,3},{2,0},{3,1},{4,6},{5,7},{6,4},{7,5},{8,10},{9,11},{10,... | collective-permute-start | bytes 1179656 | tf_op jit(solution)/shard_map/ppermute | solution.py:551
  110.4 9.4 %collective-permute-start.40 = (bf16[192,768]{1,0:T(8,128)(2,1)S(1)}, bf16[192,768]{1,0:T(8,128)(2,1)S(1)}, u32[]{:S(2)}, u32[]{:S(2)}) collective-permute-start(bf16[192,768]{1,0:T(8,128)(2,1)S(1)} %get-tuple-element.287), channel_id=1, source_target_pairs={{0,4},{4,0},{8,12},{12,8},{16,20},{20,16},{24,28},{28,24},{1,5},{5... | collective-permute-start | bytes 884744 | tf_op jit(solution)/shard_map/ppermute | solution.py:566
  111.7 10.0 %collective-permute-start.41 = (bf16[192,768]{1,0:T(8,128)(2,1)S(1)}, bf16[192,768]{1,0:T(8,128)(2,1)S(1)}, u32[]{:S(2)}, u32[]{:S(2)}) collective-permute-start(bf16[192,768]{1,0:T(8,128)(2,1)S(1)} %add_convert_fusion.7), channel_id=1, source_target_pairs={{0,8},{4,12},{8,24},{12,28},{16,0},{20,4},{24,16},{28,20},{1,9},{5... | collective-permute-start | bytes 884744 | tf_op jit(solution)/shard_map/ppermute | solution.py:581
  115.3 19.7 %collective-permute-start.43 = (f32[3,768]{1,0:T(4,128)S(1)}, f32[3,768]{1,0:T(4,128)S(1)}, u32[]{:S(2)}, u32[]{:S(2)}) collective-permute-start(f32[3,768]{1,0:T(4,128)S(1)} %get-tuple-element.292), channel_id=1, source_target_pairs={{0,1},{1,0},{2,3},{3,2},{4,5},{5,4},{6,7},{7,6},{8,9},{9,8},{10,11... | collective-permute-start | bytes 27656 | tf_op jit(solution)/shard_map/ppermute | solution.py:551
  121.7 13.3 %collective-permute-start.42 = (bf16[1,768,192]{2,1,0:T(8,128)(2,1)S(1)}, bf16[1,768,192]{2,1,0:T(8,128)(2,1)S(1)}, u32[]{:S(2)}, u32[]{:S(2)}) collective-permute-start(bf16[1,768,192]{2,1,0:T(8,128)(2,1)S(1)} %slice.86), channel_id=1, source_target_pairs={{0,2},{1,3},{2,0},{3,1},{4,6},{5,7},{6,4},{7,5},{8,10},{9,11},{10,... | collective-permute-start | bytes 884744 | tf_op jit(solution)/shard_map/ppermute | solution.py:551
  123.4 11.7 %collective-permute-start.45 = (bf16[192,768]{1,0:T(8,128)(2,1)S(1)}, bf16[192,768]{1,0:T(8,128)(2,1)S(1)}, u32[]{:S(2)}, u32[]{:S(2)}) collective-permute-start(bf16[192,768]{1,0:T(8,128)(2,1)S(1)} %add_convert_fusion.6), channel_id=1, source_target_pairs={{0,8},{4,12},{8,24},{12,28},{16,0},{20,4},{24,16},{28,20},{1,9},{5... | collective-permute-start | bytes 884744 | tf_op jit(solution)/shard_map/ppermute | solution.py:581
  124.8 10.2 %collective-permute-start.44 = (bf16[192,768]{1,0:T(8,128)(2,1)S(1)}, bf16[192,768]{1,0:T(8,128)(2,1)S(1)}, u32[]{:S(2)}, u32[]{:S(2)}) collective-permute-start(bf16[192,768]{1,0:T(8,128)(2,1)S(1)} %get-tuple-element.298), channel_id=1, source_target_pairs={{0,4},{4,0},{8,12},{12,8},{16,20},{20,16},{24,28},{28,24},{1,5},{5... | collective-permute-start | bytes 884744 | tf_op jit(solution)/shard_map/ppermute | solution.py:566
  142.4 14.8 %collective-permute-start.51 = (bf16[192,768]{1,0:T(8,128)(2,1)S(1)}, bf16[192,768]{1,0:T(8,128)(2,1)S(1)}, u32[]{:S(2)}, u32[]{:S(2)}) collective-permute-start(bf16[192,768]{1,0:T(8,128)(2,1)S(1)} %add_convert_fusion.5), channel_id=1, source_target_pairs={{0,8},{4,12},{8,24},{12,28},{16,0},{20,4},{24,16},{28,20},{1,9},{5... | collective-permute-start | bytes 884744 | tf_op jit(solution)/shard_map/ppermute | solution.py:581
  144.3 12.9 %collective-permute-start.52 = (bf16[192,768]{1,0:T(8,128)(2,1)S(1)}, bf16[192,768]{1,0:T(8,128)(2,1)S(1)}, u32[]{:S(2)}, u32[]{:S(2)}) collective-permute-start(bf16[192,768]{1,0:T(8,128)(2,1)S(1)} %get-tuple-element.319), channel_id=1, source_target_pairs={{0,4},{4,0},{8,12},{12,8},{16,20},{20,16},{24,28},{28,24},{1,5},{5... | collective-permute-start | bytes 884744 | tf_op jit(solution)/shard_map/ppermute | solution.py:566
  145.2 14.9 %collective-permute-start.55 = (bf16[256,768]{1,0:T(8,128)(2,1)S(1)}, bf16[256,768]{1,0:T(8,128)(2,1)S(1)}, u32[]{:S(2)}, u32[]{:S(2)}) collective-permute-start(bf16[256,768]{1,0:T(8,128)(2,1)S(1)} %add_convert_fusion.1), channel_id=1, source_target_pairs={{0,2},{1,3},{2,0},{3,1},{4,6},{5,7},{6,4},{7,5},{8,10},{9,11},{10,... | collective-permute-start | bytes 1179656 | tf_op jit(solution)/shard_map/ppermute | solution.py:551
  145.9 10.1 %collective-permute-start.48 = (bf16[96,768]{1,0:T(8,128)(2,1)S(1)}, bf16[96,768]{1,0:T(8,128)(2,1)S(1)}, u32[]{:S(2)}, u32[]{:S(2)}) collective-permute-start(bf16[96,768]{1,0:T(8,128)(2,1)S(1)} %add_convert_fusion.11), channel_id=1, source_target_pairs={{0,8},{4,12},{8,24},{12,28},{16,0},{20,4},{24,16},{28,20},{1,9},{5... | collective-permute-start | bytes 442376 | tf_op jit(solution)/shard_map/ppermute | solution.py:581
  146.4 10.7 %collective-permute-start.49 = (bf16[96,768]{1,0:T(8,128)(2,1)S(1)}, bf16[96,768]{1,0:T(8,128)(2,1)S(1)}, u32[]{:S(2)}, u32[]{:S(2)}) collective-permute-start(bf16[96,768]{1,0:T(8,128)(2,1)S(1)} %get-tuple-element.311), channel_id=1, source_target_pairs={{0,4},{4,0},{8,12},{12,8},{16,20},{20,16},{24,28},{28,24},{1,5},{5... | collective-permute-start | bytes 442376 | tf_op jit(solution)/shard_map/ppermute | solution.py:566
  159.4 12.7 %collective-permute-start.61 = (bf16[192,768]{1,0:T(8,128)(2,1)S(1)}, bf16[192,768]{1,0:T(8,128)(2,1)S(1)}, u32[]{:S(2)}, u32[]{:S(2)}) collective-permute-start(bf16[192,768]{1,0:T(8,128)(2,1)S(1)} %add_convert_fusion.4.refs_0_), channel_id=1, source_target_pairs={{0,2},{1,3},{2,0},{3,1},{4,6},{5,7},{6,4},{7,5},{8,10},{9,11},{10,... | collective-permute-start | bytes 884744 | tf_op jit(solution)/shard_map/ppermute | solution.py:551
  166.0 9.8 %collective-permute-start.59 = (bf16[256,768]{1,0:T(8,128)(2,1)S(1)}, bf16[256,768]{1,0:T(8,128)(2,1)S(1)}, u32[]{:S(2)}, u32[]{:S(2)}) collective-permute-start(bf16[256,768]{1,0:T(8,128)(2,1)S(1)} %add_convert_fusion.2), channel_id=1, source_target_pairs={{0,2},{1,3},{2,0},{3,1},{4,6},{5,7},{6,4},{7,5},{8,10},{9,11},{10,... | collective-permute-start | bytes 1179656 | tf_op jit(solution)/shard_map/ppermute | solution.py:551
  (46 other events, 277.1 us)

commit v2 on v1

--- a/solution.py
+++ b/solution.py
@@ -674,8 +674,6 @@
     sent = jnp.stack(
         [embed.reshape(data_count, rows), jnp.broadcast_to(ln1_gain, (data_count, rows))], axis=1
     )
-    if ringed:
-        sent = after(sent, held[1])
     taken = lax.all_to_all(sent, "dp", 0, 0, tiled=True)
     embeds = taken[:, 0]
     gain = wide(taken[:, 1].reshape(1, width))
@@ -699,10 +697,6 @@
 
     info = kernel_info(layout, rank, index, tok_rows)
     starts = info[FIRST:OWNER]
-    if ringed:
-        starts = after(starts, held[2])
-    positions = (starts[:, None] + jnp.arange(tok_rows, dtype=jnp.int32)[None, :]).reshape(-1)
-    cos_table, sin_table = rope_tables(positions)
 
     second = run(
         functools.partial(second_part_kernel, data_count),
@@ -721,21 +715,25 @@
                 dy_core,
                 gain,
                 info,
-                cos_table,
-                sin_table,
                 tok_blocks,
             )
         )
-        gain, info, cos_table, sin_table, tok_blocks = rest
+        gain, info, tok_blocks = rest
+        modulation = after(modulation, held[3])
         beside.append(pair(held[3]))
         first_chunks = [part for both in zip(held, beside) for part in both]
+        second = after(second, beside[3])
         held = [second, onward(second)]
-        beside = [pair(after(second, beside[3]))]
+        beside = [pair(second)]
         dy_chip = hop(after(out_grad, held[0]), 2)
     else:
         first_chunks = gathered_whole(first, [rows])
         second_chunks = gathered_whole(second, [rows, down_piece])
         dy_chip, dy_core = hop(out_grad, 2), hop(out_grad, 1)
+    if ringed:
+        starts = after(starts, first_chunks[6])
+    positions = (starts[:, None] + jnp.arange(tok_rows, dtype=jnp.int32)[None, :]).reshape(-1)
+    cos_table, sin_table = rope_tables(positions)
     kept, sums = halves(modulation, 2)
     if ringed:
         gain, sums = lax.optimization_barrier((gain, sums))
@@ -969,8 +967,8 @@
         qkv_taken = pair(after(qkv_give[3], qkv_ring))
     if ringed:
         sum_mlp = low(wide(mlp_keep[0]) + wide(mlp_taken) + wide(mlp_carried))
-        qkv_carried, qkv_taken, mlp_chip, mod_other, gq_send = lax.optimization_barrier(
-            (qkv_carried, qkv_taken, mlp_chip, mod_other, gq_send)
+        qkv_carried, qkv_taken, mlp_chip, mod_other = lax.optimization_barrier(
+            (qkv_carried, qkv_taken, mlp_chip, mod_other)
         )
         qkv_ring = low(wide(qkv_keep[3]) + wide(qkv_taken) + wide(qkv_carried))
         qkv_carried = onward(qkv_ring)
@@ -979,7 +977,7 @@
         sum_mlp = low(dp_sum_direct(grad_weights[0]))
     gq_chip = hop(gq_send, 2)
     grad_mod = doubled(grad_mod, mod_other, high[0])
-    mlp_blocks = four(sum_mlp)
+    mlp_far = hop(sum_mlp, 2)
     grad_inputs = run(
         input_kernel,
         [shaped((tok_rows, width))],
@@ -1003,6 +1001,7 @@
         wide(embeds), grad_mods, (((0,), (0,)), ((), ())), precision=lax.Precision.HIGHEST
     )
 
+    mlp_blocks = [sum_mlp, mlp_far, hop(sum_mlp, 1), hop(after(mlp_far, sum_qkv, grad_inputs), 1)]
     final_up, final_down = run(
         functools.partial(finish_mlp_kernel, data_count),
         [shaped(w_up.shape, jnp.float32), shaped(w_down.shape, jnp.float32)],

time: 186 us -> 184 us (0.989)
  waiting for transfers between devices: 55 us -> 48.1 us
  starting transfers between devices: 63.8 us -> 65.7 us
    ppermute x12, starting transfers between devices: 15.8 us -> 18.6 us  [onward(): return lax.ppermute(values_in, 'dp', ring_next(lax.axis_size('dp')))]
    all_to_all x1, waiting for transfers between devices: 2.64 us -> 0.01 us  [body(): taken = lax.all_to_all(sent, 'dp', 0, 0, tiled=True)]
    unnamed x24 -> x28, local copies, waits for them, and re-layouts: 4.11 us -> 4.77 us
  transfers between devices with their start and end apart: 69 -> 69, of which waited for: 24 -> 23; matrix products, arithmetic and copies ran while one was open for 5% -> 7% of each run, Pallas kernels for 21% -> 22%
where the time goes in v2:
time: 184 us
  starting transfers between devices  65.7 us (36%)
  Pallas kernels  51.2 us (28%)
  waiting for transfers between devices  48.1 us (26%)
  local copies, waits for them, and re-layouts  8.16 us (4%)
  other arithmetic  7.29 us (4%)
  between operations  1.9 us (1%)
    pallas_call x18, Pallas kernels, run(): return call(*args)  51.2 us
    ppermute x34, starting transfers between devices, hop(): lax.ppermute(values_in, 'seq', [(i, i ^ mask) for i in range(lax.axis_siz...  18.7 us
    ppermute x16, waiting for transfers between devices, pair(): lax.ppermute(values_in, 'dp', [(i, i ^ 1) for i in range(lax.axis_size('d...  18.6 us
    ppermute x12, starting transfers between devices, onward(): return lax.ppermute(values_in, 'dp', ring_next(lax.axis_size('dp')))  18.6 us
    ppermute x16, starting transfers between devices, pair(): lax.ppermute(values_in, 'dp', [(i, i ^ 1) for i in range(lax.axis_size('d...  17 us
    ppermute x34, waiting for transfers between devices, hop(): lax.ppermute(values_in, 'seq', [(i, i ^ mask) for i in range(lax.axis_siz...  13.8 us
    ppermute x12, waiting for transfers between devices, onward(): return lax.ppermute(values_in, 'dp', ring_next(lax.axis_size('dp')))  13.4 us
    ppermute x6, starting transfers between devices, beyond(): lax.ppermute(values_in, 'dp', [(i, i ^ mask) for i in range(lax.axis_size...  8.12 us
  transfers between devices with their start and end apart: 69, of which 23 were waited for; matrix products, arithmetic and copies ran while one was open for 7% of the time, Pallas kernels for 22%

profile of v2, /device:TPU:0, one launch (start us, length us, event | category | flops | bytes accessed | tf_op | source)
XLA Modules:
  0.0 183.9 jit_solution(17260168254381773116)
XLA Ops:
  2.7 3.1 %collective-permute-start = (bf16[96,768]{1,0:T(8,128)(2,1)S(1)}, bf16[96,768]{1,0:T(8,128)(2,1)S(1)}, u32[]{:S(2)}, u32[]{:S(2)}) collective-permute-start(bf16[96,768]{1,0:T(8,128)(2,1)S(1)} %first_part.1.refs_7_), channel_id=1, source_target_pairs={{0,8},{4,12},{8,24},{12,28},{16,0},{20,4},{24,16},{28,20},{1,9},{5... | collective-permute-start | bytes 442376 | tf_op jit(solution)/shard_map/ppermute | solution.py:581
  8.8 1.9 %collective-permute-done.refs_9_ = bf16[96,768]{1,0:T(8,128)(2,1)S(1)} collective-permute-done((bf16[96,768]{1,0:T(8,128)(2,1)S(1)}, bf16[96,768]{1,0:T(8,128)(2,1)S(1)}, u32[]{:S(2)}, u32[]{:S(2)}) %collective-permute-start) | collective-permute-done | bytes 147488 | tf_op jit(solution)/shard_map/ppermute | solution.py:581
  11.7 2.6 %collective-permute-start.2 = (bf16[96,768]{1,0:T(8,128)(2,1)S(1)}, bf16[96,768]{1,0:T(8,128)(2,1)}, u32[]{:S(2)}, u32[]{:S(2)}) collective-permute-start(bf16[96,768]{1,0:T(8,128)(2,1)S(1)} %collective-permute-done.refs_9_), channel_id=1, source_target_pairs={{0,8},{4,12},{8,24},{12,28},{16,0},{20,4},{24,16},{28,20},{1,9},{5... | collective-permute-start | bytes 442376 | tf_op jit(solution)/shard_map/ppermute | solution.py:581
  17.3 3.3 %all-to-all-start = ((bf16[8,2,96]{2,1,0:T(2,128)(2,1)}), bf16[8,2,96]{2,1,0:T(2,128)(2,1)S(1)}, u32[]{:S(2)}, u32[]{:S(2)}) async-start(bf16[8,2,96]{2,1,0:T(2,128)(2,1)} %copy.19), calls=%async_computation | async-start | bytes 8192 | tf_op jit(solution)/shard_map/all_to_all | solution.py:677
  23.7 1.9 %collective-permute-start.6 = (bf16[96,768]{1,0:T(8,128)(2,1)}, bf16[96,768]{1,0:T(8,128)(2,1)}, u32[]{:S(2)}, u32[]{:S(2)}) collective-permute-start(bf16[96,768]{1,0:T(8,128)(2,1)} %collective-permute-done.2.refs_11_), channel_id=1, source_target_pairs={{0,8},{4,12},{8,24},{12,28},{16,0},{20,4},{24,16},{28,20},{1,9},{5... | collective-permute-start | bytes 442376 | tf_op jit(solution)/shard_map/ppermute | solution.py:581
  35.2 2.6 %fusion = (f32[1024,128]{1,0:T(8,128)S(1)}, f32[1024,128]{1,0:T(8,128)S(1)}) fusion(f32[128]{0:T(128)} %get-tuple-element.354, f32[128]{0:T(128)} %get-tuple-element.355, f32[1024]{0:T(1024)S(1)} %bitcast.42), kind=kLoop, calls=%fused_computation.10 | loop fusion | flops 262144 | bytes 1053696 | tf_op jit(solution)/shard_map/mul | solution.py:50
  38.1 2.4 %collective-permute-start.12 = (bf16[192,768]{1,0:T(8,128)(2,1)S(1)}, bf16[192,768]{1,0:T(8,128)(2,1)S(1)}, u32[]{:S(2)}, u32[]{:S(2)}) collective-permute-start(bf16[192,768]{1,0:T(8,128)(2,1)S(1)} %second_part.1.refs_4_), channel_id=1, source_target_pairs={{0,8},{4,12},{8,24},{12,28},{16,0},{20,4},{24,16},{28,20},{1,9},{5... | collective-permute-start | bytes 884744 | tf_op jit(solution)/shard_map/ppermute | solution.py:581
  44.1 5.1 %qkv.1 = (bf16[1024,768]{1,0:T(8,128)(2,1)S(1)}, bf16[768,768]{1,0:T(8,128)(2,1)S(1)}, bf16[768,192]{1,0:T(8,128)(2,1)S(1)}, bf16[1024,384]{1,0:T(8,128)(2,1)S(1...) custom-call(s32[18]{0:T(128)S(1)} %compare_select_fusion.4.info, f32[1,768]{1,0:T(1,128)S(1)} %reshape.139.refs_0_.gain, ...), custom_call_target="tpu_custom_call" | custom-call | flops 1006632960 | bytes 9210952 | tf_op jit(solution)/shard_map/qkv/pallas_call | solution.py:107
  53.2 7.2 %attend.1 = (bf16[256,192]{1,0:T(8,128)(2,1)S(1)}, bf16[256,192]{1,0:T(8,128)(2,1)S(1)}, bf16[256,192]{1,0:T(8,128)(2,1)S(1)}, bf16[256,192]{1,0:T(8,128)(2,1)S(1)}, bf16[1024,384]{1,0:T(8,128)(2,1)S(1)}) custom-call(s32[18]{0:T(128)S(1)} %compare_select_fusion.4.info, bf16[1024,384]{1,0:T(8,128)(2,1)S(1)} %get-tuple-element.209.q_ref, ...), custom_call_target="tpu_custom_call" | custom-call | flops 1610612736 | bytes 3539016 | tf_op jit(solution)/shard_map/attend/pallas_call | solution.py:107
  61.1 1.7 collective-permute-start.25
  65.0 4.4 %collective-permute-done.23.refs_5_ = bf16[256,192]{1,0:T(8,128)(2,1)S(1)} collective-permute-done((bf16[256,192]{1,0:T(8,128)(2,1)S(1)}, bf16[256,192]{1,0:T(8,128)(2,1)S(1)}, u32[]{:S(2)}, u32[]{:S(2)}) %collective-permute-start.23) | collective-permute-done | bytes 98336 | tf_op jit(solution)/shard_map/ppermute | solution.py:551
  69.4 2.0 %collective-permute-done.24.refs_7_ = bf16[256,192]{1,0:T(8,128)(2,1)S(1)} collective-permute-done((bf16[256,192]{1,0:T(8,128)(2,1)S(1)}, bf16[256,192]{1,0:T(8,128)(2,1)S(1)}, u32[]{:S(2)}, u32[]{:S(2)}) %collective-permute-start.24) | collective-permute-done | bytes 98336 | tf_op jit(solution)/shard_map/ppermute | solution.py:551
  71.9 1.7 middle.1
  76.7 6.5 %collective-permute-done.28.refs_11_ = bf16[192,768]{1,0:T(8,128)(2,1)S(1)} collective-permute-done((bf16[192,768]{1,0:T(8,128)(2,1)S(1)}, bf16[192,768]{1,0:T(8,128)(2,1)S(1)}, u32[]{:S(2)}, u32[]{:S(2)}) %collective-permute-start.28) | collective-permute-done | bytes 294944 | tf_op jit(solution)/shard_map/ppermute | solution.py:566
  83.2 2.5 %act_grad.1 = (bf16[1024,768]{1,0:T(8,128)(2,1)S(1)}, bf16[1024,768]{1,0:T(8,128)(2,1)S(1)}) custom-call(s32[18]{0:T(128)S(1)} %compare_select_fusion.4.info, f32[3,768]{1,0:T(4,128)S(1)} %bitcast.30, bf16[256,768]{1,0:T(8,128)(2,1)S(1)} %copy-done.3, bf16[256,768]{1,0:T(8,128)(2,1)S(1)} %collective-permute-done.19.refs_1_, ...), custom_call_target="tpu_custom_call" | custom-call | flops 1207959552 | bytes 7087176 | tf_op jit(solution)/shard_map/act_grad/pallas_call | solution.py:107
  86.2 1.7 collective-permute-done.31.refs_3_
  87.9 4.9 %forward.1 = (bf16[1024,768]{1,0:T(8,128)(2,1)S(1)}, bf16[1024,768]{1,0:T(8,128)(2,1)S(1)}, bf16[512,768]{1,0:T(8,128)(2,1)S(1)}, bf16[512,768]{1,0:T(8,128)(2,1)S(1)}) custom-call(s32[18]{0:T(128)S(1)} %compare_select_fusion.4.info, bf16[1024,768]{1,0:T(8,128)(2,1)S(1)} %get-tuple-element.241.act_grad, bf16[256,768]{1,0:T(8,128)(2,1)S(1)} %get-tuple-element.235.refs_0_, ...), custom_call_target="tpu_custom_call" | custom-call | flops 2415919104 | bytes 10223688 | tf_op jit(solution)/shard_map/forward/pallas_call | solution.py:107
  93.0 3.4 %weight_grad.1 = (bf16[192,768]{1,0:T(8,128)(2,1)S(1)}, bf16[192,768]{1,0:T(8,128)(2,1)S(1)}, bf16[192,768]{1,0:T(8,128)(2,1)S(1)}, bf16[192,768]{1,0:T(8,128)(2...) custom-call(s32[18]{0:T(128)S(1)} %compare_select_fusion.4.info, ...), custom_call_target="tpu_custom_call" | custom-call | flops 2415919104 | bytes 8650824 | tf_op jit(solution)/shard_map/weight_grad/pallas_call | solution.py:107
  98.9 2.1 %down.1 = (bf16[512,768]{1,0:T(8,128)(2,1)S(1)}, bf16[512,768]{1,0:T(8,128)(2,1)S(1)}, f32[1,768]{1,0:T(1,128)S(1)}) custom-call(s32[18]{0:T(128)S(1)} %compare_select_fusion.4.info, bf16[1024,768]{1,0:T(8,128)(2,1)S(1)} %get-tuple-element.257.act_ref, bf16[256,768]{1,0:T(8,128)(2,1)S(1)} %copy-done.3, bf16[256,768]{1,0:T(8,128)(2,1)S(1)} %collective-permute-done.19.refs_1_, ...), custom_call_target="tpu_custom_call" | custom-call | flops 1207959552 | bytes 7081032 | tf_op jit(solution)/shard_map/down/pallas_call | solution.py:107
  100.9 6.1 %collective-permute-done.34 = bf16[192,768]{1,0:T(8,128)(2,1)S(1)} collective-permute-done((bf16[192,768]{1,0:T(8,128)(2,1)S(1)}, bf16[192,768]{1,0:T(8,128)(2,1)S(1)}, u32[]{:S(2)}, u32[]{:S(2)}) %collective-permute-start.34) | collective-permute-done | bytes 294944 | tf_op jit(solution)/shard_map/ppermute | solution.py:566
  108.6 2.2 %branch.1 = (f32[256,768]{1,0:T(8,128)S(1)}, bf16[256,1024]{1,0:T(8,128)(2,1)S(1)}, f32[3,768]{1,0:T(4,128)S(1)}, bf16[256,192]{1,0:T(8,128)(2,1)S(1)}, bf16[256...) custom-call(s32[18]{0:T(128)S(1)} %compare_select_fusion.4.info, f32[3,768]{1,0:T(4,128)S(1)} %bitcast.31, ...), custom_call_target="tpu_custom_call" | custom-call | flops 301989888 | bytes 5952584 | tf_op jit(solution)/shard_map/branch/pallas_call | solution.py:107
  115.9 4.4 %collective-permute-done.40 = bf16[192,768]{1,0:T(8,128)(2,1)S(1)} collective-permute-done((bf16[192,768]{1,0:T(8,128)(2,1)S(1)}, bf16[192,768]{1,0:T(8,128)(2,1)S(1)}, u32[]{:S(2)}, u32[]{:S(2)}) %collective-permute-start.40) | collective-permute-done | bytes 294944 | tf_op jit(solution)/shard_map/ppermute | solution.py:566
  125.0 9.1 %attend_back.1.grad_ref = bf16[1024,640]{1,0:T(8,128)(2,1)S(1)} custom-call(s32[18]{0:T(128)S(1)} %compare_select_fusion.4.info, f32[1024,128]{1,0:T(8,128)S(1)} %get-tuple-element.349.refs_1_.cos_ref, f32[1024,128]{1,0:T(8,128)S(1)} %get-tuple-element.348.refs_2_.sin_ref, bf16[1024,384]{1,0:T(8,128)(2,1)S(1)} %get-tuple-element.274.q_ref, ...), custom_call_target="tpu_custom_call" | custom-call | flops 4026531840 | bytes 5931080 | tf_op jit(solution)/shard_map/attend_back/pallas_call | solution.py:107
  134.2 2.1 %qkv_grad.1 = (bf16[96,768]{1,0:T(8,128)(2,1)S(1)}, bf16[96,768]{1,0:T(8,128)(2,1)S(1)}, bf16[96,768]{1,0:T(8,128)(2,1)S(1)}, bf16[96,768]{1,0:T(8,128)(2,1)S(1)...) custom-call(s32[18]{0:T(128)S(1)} %compare_select_fusion.4.info, ...), custom_call_target="tpu_custom_call" | custom-call | flops 1006632960 | bytes 4948040 | tf_op jit(solution)/shard_map/qkv_grad/pallas_call | solution.py:107
  137.8 2.2 %hidden_grad.1 = (bf16[512,768]{1,0:T(8,128)(2,1)S(1)}, bf16[512,768]{1,0:T(8,128)(2,1)S(1)}) custom-call(s32[18]{0:T(128)S(1)} %compare_select_fusion.4.info, bf16[1024,640]{1,0:T(8,128)(2,1)S(1)} %attend_back.1.grad_ref, bf16[768,768]{1,0:T(8,128)(2,1)S(1)} %get-tuple-element.301.weight_ref), custom_call_target="tpu_custom_call" | custom-call | flops 1006632960 | bytes 4063304 | tf_op jit(solution)/shard_map/hidden_grad/pallas_call | solution.py:107
  141.6 1.9 %collective-permute-start.51 = (bf16[192,768]{1,0:T(8,128)(2,1)S(1)}, bf16[192,768]{1,0:T(8,128)(2,1)S(1)}, u32[]{:S(2)}, u32[]{:S(2)}) collective-permute-start(bf16[192,768]{1,0:T(8,128)(2,1)S(1)} %add_convert_fusion.5), channel_id=1, source_target_pairs={{0,8},{4,12},{8,24},{12,28},{16,0},{20,4},{24,16},{28,20},{1,9},{5... | collective-permute-start | bytes 884744 | tf_op jit(solution)/shard_map/ppermute | solution.py:581
  147.3 8.1 %collective-permute-done.48 = bf16[96,768]{1,0:T(8,128)(2,1)S(1)} collective-permute-done((bf16[96,768]{1,0:T(8,128)(2,1)S(1)}, bf16[96,768]{1,0:T(8,128)(2,1)S(1)}, u32[]{:S(2)}, u32[]{:S(2)}) %collective-permute-start.48) | collective-permute-done | bytes 147488 | tf_op jit(solution)/shard_map/ppermute | solution.py:581
  160.7 2.1 %collective-permute-done.53 = bf16[96,768]{1,0:T(8,128)(2,1)S(1)} collective-permute-done((bf16[96,768]{1,0:T(8,128)(2,1)S(1)}, bf16[96,768]{1,0:T(8,128)(2,1)S(1)}, u32[]{:S(2)}, u32[]{:S(2)}) %collective-permute-start.53) | collective-permute-done | bytes 147488 | tf_op jit(solution)/shard_map/ppermute | solution.py:581
  169.4 1.7 collective-permute-start.67
  171.8 1.9 %input.1 = bf16[256,768]{1,0:T(8,128)(2,1)} custom-call(s32[18]{0:T(128)S(1)} %compare_select_fusion.4.info, f32[1,768]{1,0:T(1,128)S(1)} %reshape.139.refs_0_.gain, bf16[256,768]{1,0:T(8,128)(2,1)S(1)} %copy-done, f32[256,768]{1,0:T(8,128)S(1)} %get-tuple-element.334.mid_ref, bf16[512,768]{1,0:T(8,128)(2,1)S(1)} %get-tuple-element.308.own_ref, ...), custom_call_target="tpu_custom_call" | custom-call | flops 3932160 | bytes 3542088 | tf_op jit(solution)/shard_map/input/pallas_call | solution.py:107
  176.9 2.4 %finish_mlp.1 = (f32[96,3072]{1,0:T(8,128)}, f32[384,768]{1,0:T(8,128)}) custom-call(s32[18]{0:T(128)S(1)} %compare_select_fusion.4.info, bf16[192,768]{1,0:T(8,128)(2,1)S(1)} %add_convert_fusion.4.refs_0_, bf16[192,768]{1,0:T(8,128)(2,1)S(1)} %collective-permute-done.61.refs_1_, bf16[192,768]{1,0:T(8,128)(2,1)S(1)} %collective-permute-done.62.refs_2_, ...), custom_call_target="tpu_custom_call" | custom-call | bytes 3539016 | tf_op jit(solution)/shard_map/finish_mlp/pallas_call | solution.py:107
  181.3 2.6 %finish_qkv.1 = (f32[96,2304]{1,0:T(8,128)}, f32[96,768]{1,0:T(8,128)}, f32[1,96]{1,0:T(1,128)}) custom-call(s32[18]{0:T(128)S(1)} %compare_select_fusion.4.info, bf16[96,768]{1,0:T(8,128)(2,1)S(1)} %add_convert_fusion.8.refs_0_, bf16[96,768]{1,0:T(8,128)(2,1)S(1)} %collective-permute-done.60.refs_1_, bf16[96,768]{1,0:T(8,128)(2,1)S(1)} %collective-permute-done.64.refs_2_, ...), custom_call_target="tpu_custom_call" | custom-call | bytes 2212680 | tf_op jit(solution)/shard_map/finish_qkv/pallas_call | solution.py:107
  (195 shorter events, 74.3 us)
Async XLA Ops:
  7.3 14.1 %collective-permute-start.4 = (bf16[256,768]{1,0:T(8,128)(2,1)}, bf16[256,768]{1,0:T(8,128)(2,1)S(1)}, u32[]{:S(2)}, u32[]{:S(2)}) collective-permute-start(bf16[256,768]{1,0:T(8,128)(2,1)} %tok_ref.1), channel_id=1, source_target_pairs={{0,2},{1,3},{2,0},{3,1},{4,6},{5,7},{6,4},{7,5},{8,10},{9,11},{10,... | collective-permute-start | bytes 1179656 | tf_op jit(solution)/shard_map/ppermute | solution.py:551
  11.1 10.3 %collective-permute-start.5 = (bf16[256,768]{1,0:T(8,128)(2,1)}, bf16[256,768]{1,0:T(8,128)(2,1)S(1)}, u32[]{:S(2)}, u32[]{:S(2)}) collective-permute-start(bf16[256,768]{1,0:T(8,128)(2,1)} %tok_ref.1), channel_id=1, source_target_pairs={{0,1},{1,0},{2,3},{3,2},{4,5},{5,4},{6,7},{7,6},{8,9},{9,8},{10,11... | collective-permute-start | bytes 1179656 | tf_op jit(solution)/shard_map/ppermute | solution.py:551
  11.7 8.9 %collective-permute-start.2 = (bf16[96,768]{1,0:T(8,128)(2,1)S(1)}, bf16[96,768]{1,0:T(8,128)(2,1)}, u32[]{:S(2)}, u32[]{:S(2)}) collective-permute-start(bf16[96,768]{1,0:T(8,128)(2,1)S(1)} %collective-permute-done.refs_9_), channel_id=1, source_target_pairs={{0,8},{4,12},{8,24},{12,28},{16,0},{20,4},{24,16},{28,20},{1,9},{5... | collective-permute-start | bytes 442376 | tf_op jit(solution)/shard_map/ppermute | solution.py:581
  17.3 13.9 %all-to-all-start = ((bf16[8,2,96]{2,1,0:T(2,128)(2,1)}), bf16[8,2,96]{2,1,0:T(2,128)(2,1)S(1)}, u32[]{:S(2)}, u32[]{:S(2)}) async-start(bf16[8,2,96]{2,1,0:T(2,128)(2,1)} %copy.19), calls=%async_computation | async-start | bytes 8192 | tf_op jit(solution)/shard_map/all_to_all | solution.py:677
  21.4 10.3 %collective-permute-start.8 = (bf16[256,768]{1,0:T(8,128)(2,1)}, bf16[256,768]{1,0:T(8,128)(2,1)S(1)}, u32[]{:S(2)}, u32[]{:S(2)}) collective-permute-start(bf16[256,768]{1,0:T(8,128)(2,1)} %dy_ref.1), channel_id=1, source_target_pairs={{0,1},{1,0},{2,3},{3,2},{4,5},{5,4},{6,7},{7,6},{8,9},{9,8},{10,11... | collective-permute-start | bytes 1179656 | tf_op jit(solution)/shard_map/ppermute | solution.py:551
  21.4 10.3 %collective-permute-start.9 = (bf16[256,768]{1,0:T(8,128)(2,1)S(1)}, bf16[256,768]{1,0:T(8,128)(2,1)S(1)}, u32[]{:S(2)}, u32[]{:S(2)}) collective-permute-start(bf16[256,768]{1,0:T(8,128)(2,1)S(1)} %collective-permute-done.4.refs_4_), channel_id=1, source_target_pairs={{0,1},{1,0},{2,3},{3,2},{4,5},{5,4},{6,7},{7,6},{8,9},{9,8},{10,11... | collective-permute-start | bytes 1179656 | tf_op jit(solution)/shard_map/ppermute | solution.py:551
  38.1 11.1 %collective-permute-start.12 = (bf16[192,768]{1,0:T(8,128)(2,1)S(1)}, bf16[192,768]{1,0:T(8,128)(2,1)S(1)}, u32[]{:S(2)}, u32[]{:S(2)}) collective-permute-start(bf16[192,768]{1,0:T(8,128)(2,1)S(1)} %second_part.1.refs_4_), channel_id=1, source_target_pairs={{0,8},{4,12},{8,24},{12,28},{16,0},{20,4},{24,16},{28,20},{1,9},{5... | collective-permute-start | bytes 884744 | tf_op jit(solution)/shard_map/ppermute | solution.py:581
  42.6 17.8 %collective-permute-start.19 = (bf16[256,768]{1,0:T(8,128)(2,1)S(1)}, bf16[256,768]{1,0:T(8,128)(2,1)S(1)}, u32[]{:S(2)}, u32[]{:S(2)}) collective-permute-start(bf16[256,768]{1,0:T(8,128)(2,1)S(1)} %copy-done.3), channel_id=1, source_target_pairs={{0,2},{1,3},{2,0},{3,1},{4,6},{5,7},{6,4},{7,5},{8,10},{9,11},{10,... | collective-permute-start | bytes 1179656 | tf_op jit(solution)/shard_map/ppermute | solution.py:551
  50.6 9.9 %collective-permute-start.15 = (bf16[192,768]{1,0:T(8,128)(2,1)S(1)}, bf16[192,768]{1,0:T(8,128)(2,1)S(1)}, u32[]{:S(2)}, u32[]{:S(2)}) collective-permute-start(bf16[192,768]{1,0:T(8,128)(2,1)S(1)} %collective-permute-done.12.refs_6_), channel_id=1, source_target_pairs={{0,8},{4,12},{8,24},{12,28},{16,0},{20,4},{24,16},{28,20},{1,9},{5... | collective-permute-start | bytes 884744 | tf_op jit(solution)/shard_map/ppermute | solution.py:581
  51.4 9.1 %collective-permute-start.16 = (bf16[192,768]{1,0:T(8,128)(2,1)S(1)}, bf16[192,768]{1,0:T(8,128)(2,1)S(1)}, u32[]{:S(2)}, u32[]{:S(2)}) collective-permute-start(bf16[192,768]{1,0:T(8,128)(2,1)S(1)} %collective-permute-done.12.refs_6_), channel_id=1, source_target_pairs={{0,4},{4,0},{8,12},{12,8},{16,20},{20,16},{24,28},{28,24},{1,5},{5... | collective-permute-start | bytes 884744 | tf_op jit(solution)/shard_map/ppermute | solution.py:566
  61.1 10.4 %collective-permute-start.25 = (bf16[192,768]{1,0:T(8,128)(2,1)S(1)}, bf16[192,768]{1,0:T(8,128)(2,1)S(1)}, u32[]{:S(2)}, u32[]{:S(2)}) collective-permute-start(bf16[192,768]{1,0:T(8,128)(2,1)S(1)} %collective-permute-done.15.refs_8_), channel_id=1, source_target_pairs={{0,8},{4,12},{8,24},{12,28},{16,0},{20,4},{24,16},{28,20},{1,9},{5... | collective-permute-start | bytes 884744 | tf_op jit(solution)/shard_map/ppermute | solution.py:581
  62.8 9.1 %collective-permute-start.26 = (bf16[192,768]{1,0:T(8,128)(2,1)S(1)}, bf16[192,768]{1,0:T(8,128)(2,1)S(1)}, u32[]{:S(2)}, u32[]{:S(2)}) collective-permute-start(bf16[192,768]{1,0:T(8,128)(2,1)S(1)} %collective-permute-done.15.refs_8_), channel_id=1, source_target_pairs={{0,4},{4,0},{8,12},{12,8},{16,20},{20,16},{24,28},{28,24},{1,5},{5... | collective-permute-start | bytes 884744 | tf_op jit(solution)/shard_map/ppermute | solution.py:566
  73.7 9.5 %collective-permute-start.27 = (bf16[256,768]{1,0:T(8,128)(2,1)S(1)}, bf16[256,768]{1,0:T(8,128)(2,1)S(1)}, u32[]{:S(2)}, u32[]{:S(2)}) collective-permute-start(bf16[256,768]{1,0:T(8,128)(2,1)S(1)} %collective-permute-done.19.refs_1_), channel_id=1, source_target_pairs={{0,1},{1,0},{2,3},{3,2},{4,5},{5,4},{6,7},{7,6},{8,9},{9,8},{10,11... | collective-permute-start | bytes 1179656 | tf_op jit(solution)/shard_map/ppermute | solution.py:551
  73.8 9.4 %collective-permute-start.28 = (bf16[192,768]{1,0:T(8,128)(2,1)S(1)}, bf16[192,768]{1,0:T(8,128)(2,1)S(1)}, u32[]{:S(2)}, u32[]{:S(2)}) collective-permute-start(bf16[192,768]{1,0:T(8,128)(2,1)S(1)} %collective-permute-done.25.refs_10_), channel_id=1, source_target_pairs={{0,4},{4,0},{8,12},{12,8},{16,20},{20,16},{24,28},{28,24},{1,5},{5... | collective-permute-start | bytes 884744 | tf_op jit(solution)/shard_map/ppermute | solution.py:566
  75.2 11.0 %collective-permute-start.29 = (bf16[256,768]{1,0:T(8,128)(2,1)S(1)}, bf16[256,768]{1,0:T(8,128)(2,1)S(1)}, u32[]{:S(2)}, u32[]{:S(2)}) collective-permute-start(bf16[256,768]{1,0:T(8,128)(2,1)S(1)} %get-tuple-element.235.refs_0_), channel_id=1, source_target_pairs={{0,2},{1,3},{2,0},{3,1},{4,6},{5,7},{6,4},{7,5},{8,10},{9,11},{10,... | collective-permute-start | bytes 1179656 | tf_op jit(solution)/shard_map/ppermute | solution.py:551
  76.6 9.6 %collective-permute-start.30 = (bf16[256,768]{1,0:T(8,128)(2,1)S(1)}, bf16[256,768]{1,0:T(8,128)(2,1)S(1)}, u32[]{:S(2)}, u32[]{:S(2)}) collective-permute-start(bf16[256,768]{1,0:T(8,128)(2,1)S(1)} %get-tuple-element.235.refs_0_), channel_id=1, source_target_pairs={{0,1},{1,0},{2,3},{3,2},{4,5},{5,4},{6,7},{7,6},{8,9},{9,8},{10,11... | collective-permute-start | bytes 1179656 | tf_op jit(solution)/shard_map/ppermute | solution.py:551
  96.5 11.5 %collective-permute-start.33 = (bf16[256,768]{1,0:T(8,128)(2,1)S(1)}, bf16[256,768]{1,0:T(8,128)(2,1)S(1)}, u32[]{:S(2)}, u32[]{:S(2)}) collective-permute-start(bf16[256,768]{1,0:T(8,128)(2,1)S(1)} %add_convert_fusion.3), channel_id=1, source_target_pairs={{0,2},{1,3},{2,0},{3,1},{4,6},{5,7},{6,4},{7,5},{8,10},{9,11},{10,... | collective-permute-start | bytes 1179656 | tf_op jit(solution)/shard_map/ppermute | solution.py:551
  98.1 9.0 %collective-permute-start.34 = (bf16[192,768]{1,0:T(8,128)(2,1)S(1)}, bf16[192,768]{1,0:T(8,128)(2,1)S(1)}, u32[]{:S(2)}, u32[]{:S(2)}) collective-permute-start(bf16[192,768]{1,0:T(8,128)(2,1)S(1)} %get-tuple-element.262), channel_id=1, source_target_pairs={{0,4},{4,0},{8,12},{12,8},{16,20},{20,16},{24,28},{28,24},{1,5},{5... | collective-permute-start | bytes 884744 | tf_op jit(solution)/shard_map/ppermute | solution.py:566
  110.9 9.4 %collective-permute-start.40 = (bf16[192,768]{1,0:T(8,128)(2,1)S(1)}, bf16[192,768]{1,0:T(8,128)(2,1)S(1)}, u32[]{:S(2)}, u32[]{:S(2)}) collective-permute-start(bf16[192,768]{1,0:T(8,128)(2,1)S(1)} %get-tuple-element.283), channel_id=1, source_target_pairs={{0,4},{4,0},{8,12},{12,8},{16,20},{20,16},{24,28},{28,24},{1,5},{5... | collective-permute-start | bytes 884744 | tf_op jit(solution)/shard_map/ppermute | solution.py:566
  111.8 10.0 %collective-permute-start.41 = (bf16[192,768]{1,0:T(8,128)(2,1)S(1)}, bf16[192,768]{1,0:T(8,128)(2,1)S(1)}, u32[]{:S(2)}, u32[]{:S(2)}) collective-permute-start(bf16[192,768]{1,0:T(8,128)(2,1)S(1)} %add_convert_fusion.7), channel_id=1, source_target_pairs={{0,8},{4,12},{8,24},{12,28},{16,0},{20,4},{24,16},{28,20},{1,9},{5... | collective-permute-start | bytes 884744 | tf_op jit(solution)/shard_map/ppermute | solution.py:581
  112.2 9.6 %collective-permute-start.36 = (bf16[256,192]{1,0:T(8,128)(2,1)S(1)}, bf16[256,192]{1,0:T(8,128)(2,1)S(1)}, u32[]{:S(2)}, u32[]{:S(2)}) collective-permute-start(bf16[256,192]{1,0:T(8,128)(2,1)S(1)} %get-tuple-element.276), channel_id=1, source_target_pairs={{0,2},{1,3},{2,0},{3,1},{4,6},{5,7},{6,4},{7,5},{8,10},{9,11},{10,... | collective-permute-start | bytes 294920 | tf_op jit(solution)/shard_map/ppermute | solution.py:551
  113.7 20.5 %collective-permute-start.43 = (f32[3,768]{1,0:T(4,128)S(1)}, f32[3,768]{1,0:T(4,128)S(1)}, u32[]{:S(2)}, u32[]{:S(2)}) collective-permute-start(f32[3,768]{1,0:T(4,128)S(1)} %get-tuple-element.288), channel_id=1, source_target_pairs={{0,1},{1,0},{2,3},{3,2},{4,5},{5,4},{6,7},{7,6},{8,9},{9,8},{10,11... | collective-permute-start | bytes 27656 | tf_op jit(solution)/shard_map/ppermute | solution.py:551
  121.8 12.4 %collective-permute-start.42 = (bf16[1,768,192]{2,1,0:T(8,128)(2,1)S(1)}, bf16[1,768,192]{2,1,0:T(8,128)(2,1)S(1)}, u32[]{:S(2)}, u32[]{:S(2)}) collective-permute-start(bf16[1,768,192]{2,1,0:T(8,128)(2,1)S(1)} %slice.86), channel_id=1, source_target_pairs={{0,2},{1,3},{2,0},{3,1},{4,6},{5,7},{6,4},{7,5},{8,10},{9,11},{10,... | collective-permute-start | bytes 884744 | tf_op jit(solution)/shard_map/ppermute | solution.py:551
  123.5 10.7 %collective-permute-start.45 = (bf16[192,768]{1,0:T(8,128)(2,1)S(1)}, bf16[192,768]{1,0:T(8,128)(2,1)S(1)}, u32[]{:S(2)}, u32[]{:S(2)}) collective-permute-start(bf16[192,768]{1,0:T(8,128)(2,1)S(1)} %add_convert_fusion.6), channel_id=1, source_target_pairs={{0,8},{4,12},{8,24},{12,28},{16,0},{20,4},{24,16},{28,20},{1,9},{5... | collective-permute-start | bytes 884744 | tf_op jit(solution)/shard_map/ppermute | solution.py:581
  123.8 10.4 %collective-permute-start.44 = (bf16[192,768]{1,0:T(8,128)(2,1)S(1)}, bf16[192,768]{1,0:T(8,128)(2,1)S(1)}, u32[]{:S(2)}, u32[]{:S(2)}) collective-permute-start(bf16[192,768]{1,0:T(8,128)(2,1)S(1)} %get-tuple-element.294), channel_id=1, source_target_pairs={{0,4},{4,0},{8,12},{12,8},{16,20},{20,16},{24,28},{28,24},{1,5},{5... | collective-permute-start | bytes 884744 | tf_op jit(solution)/shard_map/ppermute | solution.py:566
  141.6 14.6 %collective-permute-start.51 = (bf16[192,768]{1,0:T(8,128)(2,1)S(1)}, bf16[192,768]{1,0:T(8,128)(2,1)S(1)}, u32[]{:S(2)}, u32[]{:S(2)}) collective-permute-start(bf16[192,768]{1,0:T(8,128)(2,1)S(1)} %add_convert_fusion.5), channel_id=1, source_target_pairs={{0,8},{4,12},{8,24},{12,28},{16,0},{20,4},{24,16},{28,20},{1,9},{5... | collective-permute-start | bytes 884744 | tf_op jit(solution)/shard_map/ppermute | solution.py:581
  143.5 12.7 %collective-permute-start.52 = (bf16[192,768]{1,0:T(8,128)(2,1)S(1)}, bf16[192,768]{1,0:T(8,128)(2,1)S(1)}, u32[]{:S(2)}, u32[]{:S(2)}) collective-permute-start(bf16[192,768]{1,0:T(8,128)(2,1)S(1)} %get-tuple-element.315), channel_id=1, source_target_pairs={{0,4},{4,0},{8,12},{12,8},{16,20},{20,16},{24,28},{28,24},{1,5},{5... | collective-permute-start | bytes 884744 | tf_op jit(solution)/shard_map/ppermute | solution.py:566
  144.8 15.9 %collective-permute-start.55 = (bf16[256,768]{1,0:T(8,128)(2,1)S(1)}, bf16[256,768]{1,0:T(8,128)(2,1)S(1)}, u32[]{:S(2)}, u32[]{:S(2)}) collective-permute-start(bf16[256,768]{1,0:T(8,128)(2,1)S(1)} %add_convert_fusion.1), channel_id=1, source_target_pairs={{0,2},{1,3},{2,0},{3,1},{4,6},{5,7},{6,4},{7,5},{8,10},{9,11},{10,... | collective-permute-start | bytes 1179656 | tf_op jit(solution)/shard_map/ppermute | solution.py:551
  145.5 9.8 %collective-permute-start.48 = (bf16[96,768]{1,0:T(8,128)(2,1)S(1)}, bf16[96,768]{1,0:T(8,128)(2,1)S(1)}, u32[]{:S(2)}, u32[]{:S(2)}) collective-permute-start(bf16[96,768]{1,0:T(8,128)(2,1)S(1)} %add_convert_fusion.11), channel_id=1, source_target_pairs={{0,8},{4,12},{8,24},{12,28},{16,0},{20,4},{24,16},{28,20},{1,9},{5... | collective-permute-start | bytes 442376 | tf_op jit(solution)/shard_map/ppermute | solution.py:581
  146.0 10.2 %collective-permute-start.49 = (bf16[96,768]{1,0:T(8,128)(2,1)S(1)}, bf16[96,768]{1,0:T(8,128)(2,1)S(1)}, u32[]{:S(2)}, u32[]{:S(2)}) collective-permute-start(bf16[96,768]{1,0:T(8,128)(2,1)S(1)} %get-tuple-element.307), channel_id=1, source_target_pairs={{0,4},{4,0},{8,12},{12,8},{16,20},{20,16},{24,28},{28,24},{1,5},{5... | collective-permute-start | bytes 442376 | tf_op jit(solution)/shard_map/ppermute | solution.py:566
  158.5 12.6 %collective-permute-start.59 = (bf16[256,768]{1,0:T(8,128)(2,1)S(1)}, bf16[256,768]{1,0:T(8,128)(2,1)S(1)}, u32[]{:S(2)}, u32[]{:S(2)}) collective-permute-start(bf16[256,768]{1,0:T(8,128)(2,1)S(1)} %add_convert_fusion.2), channel_id=1, source_target_pairs={{0,2},{1,3},{2,0},{3,1},{4,6},{5,7},{6,4},{7,5},{8,10},{9,11},{10,... | collective-permute-start | bytes 1179656 | tf_op jit(solution)/shard_map/ppermute | solution.py:551
  159.2 16.2 %collective-permute-start.61 = (bf16[192,768]{1,0:T(8,128)(2,1)S(1)}, bf16[192,768]{1,0:T(8,128)(2,1)S(1)}, u32[]{:S(2)}, u32[]{:S(2)}) collective-permute-start(bf16[192,768]{1,0:T(8,128)(2,1)S(1)} %add_convert_fusion.4.refs_0_), channel_id=1, source_target_pairs={{0,2},{1,3},{2,0},{3,1},{4,6},{5,7},{6,4},{7,5},{8,10},{9,11},{10,... | collective-permute-start | bytes 884744 | tf_op jit(solution)/shard_map/ppermute | solution.py:551
  (48 other events, 286.9 us)

commit v3 on v2

--- a/solution.py
+++ b/solution.py
@@ -947,9 +947,6 @@
     if ringed:
         qkv_keep, qkv_give = list(qkv_sums[0::2]), list(qkv_sums[1::2])
         qkv_taken = pair(qkv_give[1])
-        mlp_ring = low(wide(after(mlp_keep[3], qkv_sums[0])) + wide(mlp_taken) + wide(mlp_carried))
-        mlp_carried = onward(mlp_ring)
-        mlp_taken = pair(after(mlp_give[0], mlp_ring))
         gq_far, qkv_taken, mod_chip = lax.optimization_barrier((gq_far, qkv_taken, mod_chip))
         qkv_ring = low(wide(qkv_keep[1]) + wide(qkv_taken))
         qkv_carried = onward(qkv_ring)
@@ -957,19 +954,26 @@
     grad_mod = (grad_mod + mod_chip)[None]
     mod_other = beyond(grad_mod, 1)
     gq_core = hop(gq_far, 1)
+    if ringed:
+        mlp_ring = low(wide(after(mlp_keep[3], gq_core)) + wide(mlp_taken) + wide(mlp_carried))
+        mlp_carried = onward(mlp_ring)
+        mlp_taken = pair(after(mlp_give[0], mlp_ring))
     gq_send = low(wide(gq_near[tok_rows:]) + wide(gq_core[tok_rows:]))
     if ringed:
-        qkv_carried, qkv_taken, gq_send, mlp_carried, mlp_taken = lax.optimization_barrier(
-            (qkv_carried, qkv_taken, gq_send, mlp_carried, mlp_taken)
+        qkv_carried, qkv_taken, gq_send = lax.optimization_barrier(
+            (qkv_carried, qkv_taken, gq_send)
         )
         qkv_ring = low(wide(qkv_keep[2]) + wide(qkv_taken) + wide(qkv_carried))
         qkv_carried = onward(qkv_ring)
         qkv_taken = pair(after(qkv_give[3], qkv_ring))
     if ringed:
-        sum_mlp = low(wide(mlp_keep[0]) + wide(mlp_taken) + wide(mlp_carried))
         qkv_carried, qkv_taken, mlp_chip, mod_other = lax.optimization_barrier(
             (qkv_carried, qkv_taken, mlp_chip, mod_other)
         )
+        mlp_carried, mlp_taken, qkv_carried = lax.optimization_barrier(
+            (mlp_carried, mlp_taken, qkv_carried)
+        )
+        sum_mlp = low(wide(mlp_keep[0]) + wide(mlp_taken) + wide(mlp_carried))
         qkv_ring = low(wide(qkv_keep[3]) + wide(qkv_taken) + wide(qkv_carried))
         qkv_carried = onward(qkv_ring)
         qkv_taken = pair(after(qkv_give[0], qkv_ring))

time: 184 us -> 182 us (0.989)
  waiting for transfers between devices: 48.1 us -> 41.9 us
  starting transfers between devices: 65.7 us -> 69 us
    ppermute x12, waiting for transfers between devices: 13.4 us -> 8.49 us  [onward(): return lax.ppermute(values_in, 'dp', ring_next(lax.axis_size('dp')))]
where the time goes in v3:
time: 182 us
  starting transfers between devices  69 us (38%)
  Pallas kernels  51.8 us (28%)
  waiting for transfers between devices  41.9 us (23%)
  local copies, waits for them, and re-layouts  8.17 us (4%)
  other arithmetic  7.28 us (4%)
  between operations  1.89 us (1%)
    pallas_call x18, Pallas kernels, run(): return call(*args)  51.8 us
    ppermute x34, starting transfers between devices, hop(): lax.ppermute(values_in, 'seq', [(i, i ^ mask) for i in range(lax.axis_siz...  20.1 us
    ppermute x12, starting transfers between devices, onward(): return lax.ppermute(values_in, 'dp', ring_next(lax.axis_size('dp')))  19.6 us
    ppermute x16, waiting for transfers between devices, pair(): lax.ppermute(values_in, 'dp', [(i, i ^ 1) for i in range(lax.axis_size('d...  18.8 us
    ppermute x16, starting transfers between devices, pair(): lax.ppermute(values_in, 'dp', [(i, i ^ 1) for i in range(lax.axis_size('d...  17.4 us
    ppermute x34, waiting for transfers between devices, hop(): lax.ppermute(values_in, 'seq', [(i, i ^ mask) for i in range(lax.axis_siz...  13.9 us
    ppermute x6, starting transfers between devices, beyond(): lax.ppermute(values_in, 'dp', [(i, i ^ mask) for i in range(lax.axis_size...  8.61 us
    ppermute x12, waiting for transfers between devices, onward(): return lax.ppermute(values_in, 'dp', ring_next(lax.axis_size('dp')))  8.49 us
  transfers between devices with their start and end apart: 69, of which 23 were waited for; matrix products, arithmetic and copies ran while one was open for 7% of the time, Pallas kernels for 22%

profile of v3, /device:TPU:0, one launch (start us, length us, event | category | flops | bytes accessed | tf_op | source)
XLA Modules:
  0.0 181.5 jit_solution(5662317961477284486)
XLA Ops:
  2.7 3.1 %collective-permute-start = (bf16[96,768]{1,0:T(8,128)(2,1)S(1)}, bf16[96,768]{1,0:T(8,128)(2,1)S(1)}, u32[]{:S(2)}, u32[]{:S(2)}) collective-permute-start(bf16[96,768]{1,0:T(8,128)(2,1)S(1)} %first_part.1.refs_7_), channel_id=1, source_target_pairs={{0,8},{4,12},{8,24},{12,28},{16,0},{20,4},{24,16},{28,20},{1,9},{5... | collective-permute-start | bytes 442376 | tf_op jit(solution)/shard_map/ppermute | solution.py:581
  8.8 1.9 %collective-permute-done.refs_9_ = bf16[96,768]{1,0:T(8,128)(2,1)S(1)} collective-permute-done((bf16[96,768]{1,0:T(8,128)(2,1)S(1)}, bf16[96,768]{1,0:T(8,128)(2,1)S(1)}, u32[]{:S(2)}, u32[]{:S(2)}) %collective-permute-start) | collective-permute-done | bytes 147488 | tf_op jit(solution)/shard_map/ppermute | solution.py:581
  11.7 2.6 %collective-permute-start.2 = (bf16[96,768]{1,0:T(8,128)(2,1)S(1)}, bf16[96,768]{1,0:T(8,128)(2,1)}, u32[]{:S(2)}, u32[]{:S(2)}) collective-permute-start(bf16[96,768]{1,0:T(8,128)(2,1)S(1)} %collective-permute-done.refs_9_), channel_id=1, source_target_pairs={{0,8},{4,12},{8,24},{12,28},{16,0},{20,4},{24,16},{28,20},{1,9},{5... | collective-permute-start | bytes 442376 | tf_op jit(solution)/shard_map/ppermute | solution.py:581
  17.3 3.3 %all-to-all-start = ((bf16[8,2,96]{2,1,0:T(2,128)(2,1)}), bf16[8,2,96]{2,1,0:T(2,128)(2,1)S(1)}, u32[]{:S(2)}, u32[]{:S(2)}) async-start(bf16[8,2,96]{2,1,0:T(2,128)(2,1)} %copy.19), calls=%async_computation | async-start | bytes 8192 | tf_op jit(solution)/shard_map/all_to_all | solution.py:677
  23.7 1.9 %collective-permute-start.6 = (bf16[96,768]{1,0:T(8,128)(2,1)}, bf16[96,768]{1,0:T(8,128)(2,1)}, u32[]{:S(2)}, u32[]{:S(2)}) collective-permute-start(bf16[96,768]{1,0:T(8,128)(2,1)} %collective-permute-done.2.refs_11_), channel_id=1, source_target_pairs={{0,8},{4,12},{8,24},{12,28},{16,0},{20,4},{24,16},{28,20},{1,9},{5... | collective-permute-start | bytes 442376 | tf_op jit(solution)/shard_map/ppermute | solution.py:581
  35.2 2.6 %fusion = (f32[1024,128]{1,0:T(8,128)S(1)}, f32[1024,128]{1,0:T(8,128)S(1)}) fusion(f32[128]{0:T(128)} %get-tuple-element.356, f32[128]{0:T(128)} %get-tuple-element.357, f32[1024]{0:T(1024)S(1)} %bitcast.42), kind=kLoop, calls=%fused_computation.10 | loop fusion | flops 262144 | bytes 1053696 | tf_op jit(solution)/shard_map/mul | solution.py:50
  38.1 2.4 %collective-permute-start.12 = (bf16[192,768]{1,0:T(8,128)(2,1)S(1)}, bf16[192,768]{1,0:T(8,128)(2,1)S(1)}, u32[]{:S(2)}, u32[]{:S(2)}) collective-permute-start(bf16[192,768]{1,0:T(8,128)(2,1)S(1)} %second_part.1.refs_4_), channel_id=1, source_target_pairs={{0,8},{4,12},{8,24},{12,28},{16,0},{20,4},{24,16},{28,20},{1,9},{5... | collective-permute-start | bytes 884744 | tf_op jit(solution)/shard_map/ppermute | solution.py:581
  44.1 5.1 %qkv.1 = (bf16[1024,768]{1,0:T(8,128)(2,1)S(1)}, bf16[768,768]{1,0:T(8,128)(2,1)S(1)}, bf16[768,192]{1,0:T(8,128)(2,1)S(1)}, bf16[1024,384]{1,0:T(8,128)(2,1)S(1...) custom-call(s32[18]{0:T(128)S(1)} %compare_select_fusion.4.info, f32[1,768]{1,0:T(1,128)S(1)} %reshape.139.refs_0_.gain, ...), custom_call_target="tpu_custom_call" | custom-call | flops 1006632960 | bytes 9210952 | tf_op jit(solution)/shard_map/qkv/pallas_call | solution.py:107
  53.2 7.3 %attend.1 = (bf16[256,192]{1,0:T(8,128)(2,1)S(1)}, bf16[256,192]{1,0:T(8,128)(2,1)S(1)}, bf16[256,192]{1,0:T(8,128)(2,1)S(1)}, bf16[256,192]{1,0:T(8,128)(2,1)S(1)}, bf16[1024,384]{1,0:T(8,128)(2,1)S(1)}) custom-call(s32[18]{0:T(128)S(1)} %compare_select_fusion.4.info, bf16[1024,384]{1,0:T(8,128)(2,1)S(1)} %get-tuple-element.210.q_ref, ...), custom_call_target="tpu_custom_call" | custom-call | flops 1610612736 | bytes 3539016 | tf_op jit(solution)/shard_map/attend/pallas_call | solution.py:107
  65.0 4.4 %collective-permute-done.23.refs_5_ = bf16[256,192]{1,0:T(8,128)(2,1)S(1)} collective-permute-done((bf16[256,192]{1,0:T(8,128)(2,1)S(1)}, bf16[256,192]{1,0:T(8,128)(2,1)S(1)}, u32[]{:S(2)}, u32[]{:S(2)}) %collective-permute-start.23) | collective-permute-done | bytes 98336 | tf_op jit(solution)/shard_map/ppermute | solution.py:551
  69.5 2.0 %collective-permute-done.24.refs_7_ = bf16[256,192]{1,0:T(8,128)(2,1)S(1)} collective-permute-done((bf16[256,192]{1,0:T(8,128)(2,1)S(1)}, bf16[256,192]{1,0:T(8,128)(2,1)S(1)}, u32[]{:S(2)}, u32[]{:S(2)}) %collective-permute-start.24) | collective-permute-done | bytes 98336 | tf_op jit(solution)/shard_map/ppermute | solution.py:551
  71.9 1.7 middle.1
  76.7 6.5 %collective-permute-done.28.refs_11_ = bf16[192,768]{1,0:T(8,128)(2,1)S(1)} collective-permute-done((bf16[192,768]{1,0:T(8,128)(2,1)S(1)}, bf16[192,768]{1,0:T(8,128)(2,1)S(1)}, u32[]{:S(2)}, u32[]{:S(2)}) %collective-permute-start.28) | collective-permute-done | bytes 294944 | tf_op jit(solution)/shard_map/ppermute | solution.py:566
  83.2 2.5 %act_grad.1 = (bf16[1024,768]{1,0:T(8,128)(2,1)S(1)}, bf16[1024,768]{1,0:T(8,128)(2,1)S(1)}) custom-call(s32[18]{0:T(128)S(1)} %compare_select_fusion.4.info, f32[3,768]{1,0:T(4,128)S(1)} %bitcast.30, bf16[256,768]{1,0:T(8,128)(2,1)S(1)} %copy-done.3, bf16[256,768]{1,0:T(8,128)(2,1)S(1)} %collective-permute-done.19.refs_1_, ...), custom_call_target="tpu_custom_call" | custom-call | flops 1207959552 | bytes 7087176 | tf_op jit(solution)/shard_map/act_grad/pallas_call | solution.py:107
  86.2 1.7 collective-permute-done.31.refs_3_
  87.9 4.9 %forward.1 = (bf16[1024,768]{1,0:T(8,128)(2,1)S(1)}, bf16[1024,768]{1,0:T(8,128)(2,1)S(1)}, bf16[512,768]{1,0:T(8,128)(2,1)S(1)}, bf16[512,768]{1,0:T(8,128)(2,1)S(1)}) custom-call(s32[18]{0:T(128)S(1)} %compare_select_fusion.4.info, bf16[1024,768]{1,0:T(8,128)(2,1)S(1)} %get-tuple-element.242.act_grad, bf16[256,768]{1,0:T(8,128)(2,1)S(1)} %get-tuple-element.236.refs_0_, ...), custom_call_target="tpu_custom_call" | custom-call | flops 2415919104 | bytes 10223688 | tf_op jit(solution)/shard_map/forward/pallas_call | solution.py:107
  93.1 3.4 %weight_grad.1 = (bf16[192,768]{1,0:T(8,128)(2,1)S(1)}, bf16[192,768]{1,0:T(8,128)(2,1)S(1)}, bf16[192,768]{1,0:T(8,128)(2,1)S(1)}, bf16[192,768]{1,0:T(8,128)(2...) custom-call(s32[18]{0:T(128)S(1)} %compare_select_fusion.4.info, ...), custom_call_target="tpu_custom_call" | custom-call | flops 2415919104 | bytes 8650824 | tf_op jit(solution)/shard_map/weight_grad/pallas_call | solution.py:107
  98.9 2.1 %down.1 = (bf16[512,768]{1,0:T(8,128)(2,1)S(1)}, bf16[512,768]{1,0:T(8,128)(2,1)S(1)}, f32[1,768]{1,0:T(1,128)S(1)}) custom-call(s32[18]{0:T(128)S(1)} %compare_select_fusion.4.info, bf16[1024,768]{1,0:T(8,128)(2,1)S(1)} %get-tuple-element.258.act_ref, bf16[256,768]{1,0:T(8,128)(2,1)S(1)} %copy-done.3, bf16[256,768]{1,0:T(8,128)(2,1)S(1)} %collective-permute-done.19.refs_1_, ...), custom_call_target="tpu_custom_call" | custom-call | flops 1207959552 | bytes 7081032 | tf_op jit(solution)/shard_map/down/pallas_call | solution.py:107
  101.0 6.1 %collective-permute-done.34 = bf16[192,768]{1,0:T(8,128)(2,1)S(1)} collective-permute-done((bf16[192,768]{1,0:T(8,128)(2,1)S(1)}, bf16[192,768]{1,0:T(8,128)(2,1)S(1)}, u32[]{:S(2)}, u32[]{:S(2)}) %collective-permute-start.34) | collective-permute-done | bytes 294944 | tf_op jit(solution)/shard_map/ppermute | solution.py:566
  108.1 2.2 %branch.1 = (f32[256,768]{1,0:T(8,128)S(1)}, bf16[256,1024]{1,0:T(8,128)(2,1)S(1)}, f32[3,768]{1,0:T(4,128)S(1)}, bf16[256,192]{1,0:T(8,128)(2,1)S(1)}, bf16[256...) custom-call(s32[18]{0:T(128)S(1)} %compare_select_fusion.4.info, f32[3,768]{1,0:T(4,128)S(1)} %bitcast.31, ...), custom_call_target="tpu_custom_call" | custom-call | flops 301989888 | bytes 5952584 | tf_op jit(solution)/shard_map/branch/pallas_call | solution.py:107
  116.3 4.0 %collective-permute-done.40 = bf16[192,768]{1,0:T(8,128)(2,1)S(1)} collective-permute-done((bf16[192,768]{1,0:T(8,128)(2,1)S(1)}, bf16[192,768]{1,0:T(8,128)(2,1)S(1)}, u32[]{:S(2)}, u32[]{:S(2)}) %collective-permute-start.40) | collective-permute-done | bytes 294944 | tf_op jit(solution)/shard_map/ppermute | solution.py:566
  125.0 9.4 %attend_back.1.grad_ref = bf16[1024,640]{1,0:T(8,128)(2,1)S(1)} custom-call(s32[18]{0:T(128)S(1)} %compare_select_fusion.4.info, f32[1024,128]{1,0:T(8,128)S(1)} %get-tuple-element.351.refs_1_.cos_ref, f32[1024,128]{1,0:T(8,128)S(1)} %get-tuple-element.350.refs_2_.sin_ref, bf16[1024,384]{1,0:T(8,128)(2,1)S(1)} %get-tuple-element.275.q_ref, ...), custom_call_target="tpu_custom_call" | custom-call | flops 4026531840 | bytes 5931080 | tf_op jit(solution)/shard_map/attend_back/pallas_call | solution.py:107
  134.4 2.1 %qkv_grad.1 = (bf16[96,768]{1,0:T(8,128)(2,1)S(1)}, bf16[96,768]{1,0:T(8,128)(2,1)S(1)}, bf16[96,768]{1,0:T(8,128)(2,1)S(1)}, bf16[96,768]{1,0:T(8,128)(2,1)S(1)...) custom-call(s32[18]{0:T(128)S(1)} %compare_select_fusion.4.info, ...), custom_call_target="tpu_custom_call" | custom-call | flops 1006632960 | bytes 4948040 | tf_op jit(solution)/shard_map/qkv_grad/pallas_call | solution.py:107
  138.0 2.2 %hidden_grad.1 = (bf16[512,768]{1,0:T(8,128)(2,1)S(1)}, bf16[512,768]{1,0:T(8,128)(2,1)S(1)}) custom-call(s32[18]{0:T(128)S(1)} %compare_select_fusion.4.info, bf16[1024,640]{1,0:T(8,128)(2,1)S(1)} %attend_back.1.grad_ref, bf16[768,768]{1,0:T(8,128)(2,1)S(1)} %get-tuple-element.302.weight_ref), custom_call_target="tpu_custom_call" | custom-call | flops 1006632960 | bytes 4063304 | tf_op jit(solution)/shard_map/hidden_grad/pallas_call | solution.py:107
  142.5 2.0 %collective-permute-start.48 = (bf16[96,768]{1,0:T(8,128)(2,1)S(1)}, bf16[96,768]{1,0:T(8,128)(2,1)S(1)}, u32[]{:S(2)}, u32[]{:S(2)}) collective-permute-start(bf16[96,768]{1,0:T(8,128)(2,1)S(1)} %add_convert_fusion.11), channel_id=1, source_target_pairs={{0,8},{4,12},{8,24},{12,28},{16,0},{20,4},{24,16},{28,20},{1,9},{5... | collective-permute-start | bytes 442376 | tf_op jit(solution)/shard_map/ppermute | solution.py:581
  146.7 3.0 %collective-permute-done.48 = bf16[96,768]{1,0:T(8,128)(2,1)S(1)} collective-permute-done((bf16[96,768]{1,0:T(8,128)(2,1)S(1)}, bf16[96,768]{1,0:T(8,128)(2,1)S(1)}, u32[]{:S(2)}, u32[]{:S(2)}) %collective-permute-start.48) | collective-permute-done | bytes 147488 | tf_op jit(solution)/shard_map/ppermute | solution.py:581
  152.3 2.4 %collective-permute-start.55 = (bf16[192,768]{1,0:T(8,128)(2,1)S(1)}, bf16[192,768]{1,0:T(8,128)(2,1)S(1)}, u32[]{:S(2)}, u32[]{:S(2)}) collective-permute-start(bf16[192,768]{1,0:T(8,128)(2,1)S(1)} %add_convert_fusion.5), channel_id=1, source_target_pairs={{0,8},{4,12},{8,24},{12,28},{16,0},{20,4},{24,16},{28,20},{1,9},{5... | collective-permute-start | bytes 884744 | tf_op jit(solution)/shard_map/ppermute | solution.py:581
  158.2 2.1 %collective-permute-start.66 = (f32[2,3,768]{2,1,0:T(4,128)S(1)}, f32[2,3,768]{2,1,0:T(4,128)S(1)}, u32[]{:S(2)}, u32[]{:S(2)}) collective-permute-start(f32[2,3,768]{2,1,0:T(4,128)S(1)} %maximum_select_fusion.4), channel_id=1, source_target_pairs={{0,8},{4,12},{8,0},{12,4},{16,24},{20,28},{24,16},{28,20},{1,9},{5... | collective-permute-start | bytes 55304 | tf_op jit(solution)/shard_map/ppermute | solution.py:620
  167.0 1.6 collective-permute-start.67
  168.6 2.0 %input.1 = bf16[256,768]{1,0:T(8,128)(2,1)} custom-call(s32[18]{0:T(128)S(1)} %compare_select_fusion.4.info, f32[1,768]{1,0:T(1,128)S(1)} %reshape.139.refs_0_.gain, bf16[256,768]{1,0:T(8,128)(2,1)S(1)} %copy-done, f32[256,768]{1,0:T(8,128)S(1)} %get-tuple-element.336.mid_ref, bf16[512,768]{1,0:T(8,128)(2,1)S(1)} %get-tuple-element.309.own_ref, ...), custom_call_target="tpu_custom_call" | custom-call | flops 3932160 | bytes 3542088 | tf_op jit(solution)/shard_map/input/pallas_call | solution.py:107
  173.7 2.4 %finish_mlp.1 = (f32[96,3072]{1,0:T(8,128)}, f32[384,768]{1,0:T(8,128)}) custom-call(s32[18]{0:T(128)S(1)} %compare_select_fusion.4.info, bf16[192,768]{1,0:T(8,128)(2,1)S(1)} %add_convert_fusion.4.refs_0_, bf16[192,768]{1,0:T(8,128)(2,1)S(1)} %collective-permute-done.61.refs_1_, bf16[192,768]{1,0:T(8,128)(2,1)S(1)} %collective-permute-done.62.refs_2_, ...), custom_call_target="tpu_custom_call" | custom-call | bytes 3539016 | tf_op jit(solution)/shard_map/finish_mlp/pallas_call | solution.py:107
  178.9 2.6 %finish_qkv.1 = (f32[96,2304]{1,0:T(8,128)}, f32[96,768]{1,0:T(8,128)}, f32[1,96]{1,0:T(1,128)}) custom-call(s32[18]{0:T(128)S(1)} %compare_select_fusion.4.info, bf16[96,768]{1,0:T(8,128)(2,1)S(1)} %add_convert_fusion.8.refs_0_, bf16[96,768]{1,0:T(8,128)(2,1)S(1)} %collective-permute-done.60.refs_1_, bf16[96,768]{1,0:T(8,128)(2,1)S(1)} %collective-permute-done.64.refs_2_, ...), custom_call_target="tpu_custom_call" | custom-call | bytes 2212680 | tf_op jit(solution)/shard_map/finish_qkv/pallas_call | solution.py:107
  (195 shorter events, 76.3 us)
Async XLA Ops:
  7.3 14.1 %collective-permute-start.4 = (bf16[256,768]{1,0:T(8,128)(2,1)}, bf16[256,768]{1,0:T(8,128)(2,1)S(1)}, u32[]{:S(2)}, u32[]{:S(2)}) collective-permute-start(bf16[256,768]{1,0:T(8,128)(2,1)} %tok_ref.1), channel_id=1, source_target_pairs={{0,2},{1,3},{2,0},{3,1},{4,6},{5,7},{6,4},{7,5},{8,10},{9,11},{10,... | collective-permute-start | bytes 1179656 | tf_op jit(solution)/shard_map/ppermute | solution.py:551
  11.1 10.3 %collective-permute-start.5 = (bf16[256,768]{1,0:T(8,128)(2,1)}, bf16[256,768]{1,0:T(8,128)(2,1)S(1)}, u32[]{:S(2)}, u32[]{:S(2)}) collective-permute-start(bf16[256,768]{1,0:T(8,128)(2,1)} %tok_ref.1), channel_id=1, source_target_pairs={{0,1},{1,0},{2,3},{3,2},{4,5},{5,4},{6,7},{7,6},{8,9},{9,8},{10,11... | collective-permute-start | bytes 1179656 | tf_op jit(solution)/shard_map/ppermute | solution.py:551
  11.7 8.9 %collective-permute-start.2 = (bf16[96,768]{1,0:T(8,128)(2,1)S(1)}, bf16[96,768]{1,0:T(8,128)(2,1)}, u32[]{:S(2)}, u32[]{:S(2)}) collective-permute-start(bf16[96,768]{1,0:T(8,128)(2,1)S(1)} %collective-permute-done.refs_9_), channel_id=1, source_target_pairs={{0,8},{4,12},{8,24},{12,28},{16,0},{20,4},{24,16},{28,20},{1,9},{5... | collective-permute-start | bytes 442376 | tf_op jit(solution)/shard_map/ppermute | solution.py:581
  17.3 13.9 %all-to-all-start = ((bf16[8,2,96]{2,1,0:T(2,128)(2,1)}), bf16[8,2,96]{2,1,0:T(2,128)(2,1)S(1)}, u32[]{:S(2)}, u32[]{:S(2)}) async-start(bf16[8,2,96]{2,1,0:T(2,128)(2,1)} %copy.19), calls=%async_computation | async-start | bytes 8192 | tf_op jit(solution)/shard_map/all_to_all | solution.py:677
  21.4 10.3 %collective-permute-start.8 = (bf16[256,768]{1,0:T(8,128)(2,1)}, bf16[256,768]{1,0:T(8,128)(2,1)S(1)}, u32[]{:S(2)}, u32[]{:S(2)}) collective-permute-start(bf16[256,768]{1,0:T(8,128)(2,1)} %dy_ref.1), channel_id=1, source_target_pairs={{0,1},{1,0},{2,3},{3,2},{4,5},{5,4},{6,7},{7,6},{8,9},{9,8},{10,11... | collective-permute-start | bytes 1179656 | tf_op jit(solution)/shard_map/ppermute | solution.py:551
  21.4 10.3 %collective-permute-start.9 = (bf16[256,768]{1,0:T(8,128)(2,1)S(1)}, bf16[256,768]{1,0:T(8,128)(2,1)S(1)}, u32[]{:S(2)}, u32[]{:S(2)}) collective-permute-start(bf16[256,768]{1,0:T(8,128)(2,1)S(1)} %collective-permute-done.4.refs_4_), channel_id=1, source_target_pairs={{0,1},{1,0},{2,3},{3,2},{4,5},{5,4},{6,7},{7,6},{8,9},{9,8},{10,11... | collective-permute-start | bytes 1179656 | tf_op jit(solution)/shard_map/ppermute | solution.py:551
  38.1 11.1 %collective-permute-start.12 = (bf16[192,768]{1,0:T(8,128)(2,1)S(1)}, bf16[192,768]{1,0:T(8,128)(2,1)S(1)}, u32[]{:S(2)}, u32[]{:S(2)}) collective-permute-start(bf16[192,768]{1,0:T(8,128)(2,1)S(1)} %second_part.1.refs_4_), channel_id=1, source_target_pairs={{0,8},{4,12},{8,24},{12,28},{16,0},{20,4},{24,16},{28,20},{1,9},{5... | collective-permute-start | bytes 884744 | tf_op jit(solution)/shard_map/ppermute | solution.py:581
  40.5 8.7 %collective-permute-start.13 = (bf16[192,768]{1,0:T(8,128)(2,1)S(1)}, bf16[192,768]{1,0:T(8,128)(2,1)S(1)}, u32[]{:S(2)}, u32[]{:S(2)}) collective-permute-start(bf16[192,768]{1,0:T(8,128)(2,1)S(1)} %second_part.1.refs_4_), channel_id=1, source_target_pairs={{0,4},{4,0},{8,12},{12,8},{16,20},{20,16},{24,28},{28,24},{1,5},{5... | collective-permute-start | bytes 884744 | tf_op jit(solution)/shard_map/ppermute | solution.py:566
  42.6 17.9 %collective-permute-start.19 = (bf16[256,768]{1,0:T(8,128)(2,1)S(1)}, bf16[256,768]{1,0:T(8,128)(2,1)S(1)}, u32[]{:S(2)}, u32[]{:S(2)}) collective-permute-start(bf16[256,768]{1,0:T(8,128)(2,1)S(1)} %copy-done.3), channel_id=1, source_target_pairs={{0,2},{1,3},{2,0},{3,1},{4,6},{5,7},{6,4},{7,5},{8,10},{9,11},{10,... | collective-permute-start | bytes 1179656 | tf_op jit(solution)/shard_map/ppermute | solution.py:551
  50.6 10.0 %collective-permute-start.15 = (bf16[192,768]{1,0:T(8,128)(2,1)S(1)}, bf16[192,768]{1,0:T(8,128)(2,1)S(1)}, u32[]{:S(2)}, u32[]{:S(2)}) collective-permute-start(bf16[192,768]{1,0:T(8,128)(2,1)S(1)} %collective-permute-done.12.refs_6_), channel_id=1, source_target_pairs={{0,8},{4,12},{8,24},{12,28},{16,0},{20,4},{24,16},{28,20},{1,9},{5... | collective-permute-start | bytes 884744 | tf_op jit(solution)/shard_map/ppermute | solution.py:581
  51.4 9.2 %collective-permute-start.16 = (bf16[192,768]{1,0:T(8,128)(2,1)S(1)}, bf16[192,768]{1,0:T(8,128)(2,1)S(1)}, u32[]{:S(2)}, u32[]{:S(2)}) collective-permute-start(bf16[192,768]{1,0:T(8,128)(2,1)S(1)} %collective-permute-done.12.refs_6_), channel_id=1, source_target_pairs={{0,4},{4,0},{8,12},{12,8},{16,20},{20,16},{24,28},{28,24},{1,5},{5... | collective-permute-start | bytes 884744 | tf_op jit(solution)/shard_map/ppermute | solution.py:566
  61.2 10.3 %collective-permute-start.25 = (bf16[192,768]{1,0:T(8,128)(2,1)S(1)}, bf16[192,768]{1,0:T(8,128)(2,1)S(1)}, u32[]{:S(2)}, u32[]{:S(2)}) collective-permute-start(bf16[192,768]{1,0:T(8,128)(2,1)S(1)} %collective-permute-done.15.refs_8_), channel_id=1, source_target_pairs={{0,8},{4,12},{8,24},{12,28},{16,0},{20,4},{24,16},{28,20},{1,9},{5... | collective-permute-start | bytes 884744 | tf_op jit(solution)/shard_map/ppermute | solution.py:581
  62.8 9.1 %collective-permute-start.26 = (bf16[192,768]{1,0:T(8,128)(2,1)S(1)}, bf16[192,768]{1,0:T(8,128)(2,1)S(1)}, u32[]{:S(2)}, u32[]{:S(2)}) collective-permute-start(bf16[192,768]{1,0:T(8,128)(2,1)S(1)} %collective-permute-done.15.refs_8_), channel_id=1, source_target_pairs={{0,4},{4,0},{8,12},{12,8},{16,20},{20,16},{24,28},{28,24},{1,5},{5... | collective-permute-start | bytes 884744 | tf_op jit(solution)/shard_map/ppermute | solution.py:566
  63.2 8.8 %collective-permute-start.22 = (bf16[768,192]{1,0:T(8,128)(2,1)S(1)}, bf16[768,192]{1,0:T(8,128)(2,1)S(1)}, u32[]{:S(2)}, u32[]{:S(2)}) collective-permute-start(bf16[768,192]{1,0:T(8,128)(2,1)S(1)} %collective-permute-done.17.refs_1_), channel_id=1, source_target_pairs={{0,1},{1,0},{2,3},{3,2},{4,5},{5,4},{6,7},{7,6},{8,9},{9,8},{10,11... | collective-permute-start | bytes 884744 | tf_op jit(solution)/shard_map/ppermute | solution.py:551
  73.7 9.5 %collective-permute-start.27 = (bf16[256,768]{1,0:T(8,128)(2,1)S(1)}, bf16[256,768]{1,0:T(8,128)(2,1)S(1)}, u32[]{:S(2)}, u32[]{:S(2)}) collective-permute-start(bf16[256,768]{1,0:T(8,128)(2,1)S(1)} %collective-permute-done.19.refs_1_), channel_id=1, source_target_pairs={{0,1},{1,0},{2,3},{3,2},{4,5},{5,4},{6,7},{7,6},{8,9},{9,8},{10,11... | collective-permute-start | bytes 1179656 | tf_op jit(solution)/shard_map/ppermute | solution.py:551
  73.8 9.4 %collective-permute-start.28 = (bf16[192,768]{1,0:T(8,128)(2,1)S(1)}, bf16[192,768]{1,0:T(8,128)(2,1)S(1)}, u32[]{:S(2)}, u32[]{:S(2)}) collective-permute-start(bf16[192,768]{1,0:T(8,128)(2,1)S(1)} %collective-permute-done.25.refs_10_), channel_id=1, source_target_pairs={{0,4},{4,0},{8,12},{12,8},{16,20},{20,16},{24,28},{28,24},{1,5},{5... | collective-permute-start | bytes 884744 | tf_op jit(solution)/shard_map/ppermute | solution.py:566
  75.2 11.0 %collective-permute-start.29 = (bf16[256,768]{1,0:T(8,128)(2,1)S(1)}, bf16[256,768]{1,0:T(8,128)(2,1)S(1)}, u32[]{:S(2)}, u32[]{:S(2)}) collective-permute-start(bf16[256,768]{1,0:T(8,128)(2,1)S(1)} %get-tuple-element.236.refs_0_), channel_id=1, source_target_pairs={{0,2},{1,3},{2,0},{3,1},{4,6},{5,7},{6,4},{7,5},{8,10},{9,11},{10,... | collective-permute-start | bytes 1179656 | tf_op jit(solution)/shard_map/ppermute | solution.py:551
  76.6 9.6 %collective-permute-start.30 = (bf16[256,768]{1,0:T(8,128)(2,1)S(1)}, bf16[256,768]{1,0:T(8,128)(2,1)S(1)}, u32[]{:S(2)}, u32[]{:S(2)}) collective-permute-start(bf16[256,768]{1,0:T(8,128)(2,1)S(1)} %get-tuple-element.236.refs_0_), channel_id=1, source_target_pairs={{0,1},{1,0},{2,3},{3,2},{4,5},{5,4},{6,7},{7,6},{8,9},{9,8},{10,11... | collective-permute-start | bytes 1179656 | tf_op jit(solution)/shard_map/ppermute | solution.py:551
  96.6 11.5 %collective-permute-start.33 = (bf16[256,768]{1,0:T(8,128)(2,1)S(1)}, bf16[256,768]{1,0:T(8,128)(2,1)S(1)}, u32[]{:S(2)}, u32[]{:S(2)}) collective-permute-start(bf16[256,768]{1,0:T(8,128)(2,1)S(1)} %add_convert_fusion.3), channel_id=1, source_target_pairs={{0,2},{1,3},{2,0},{3,1},{4,6},{5,7},{6,4},{7,5},{8,10},{9,11},{10,... | collective-permute-start | bytes 1179656 | tf_op jit(solution)/shard_map/ppermute | solution.py:551
  98.1 9.0 %collective-permute-start.34 = (bf16[192,768]{1,0:T(8,128)(2,1)S(1)}, bf16[192,768]{1,0:T(8,128)(2,1)S(1)}, u32[]{:S(2)}, u32[]{:S(2)}) collective-permute-start(bf16[192,768]{1,0:T(8,128)(2,1)S(1)} %get-tuple-element.263), channel_id=1, source_target_pairs={{0,4},{4,0},{8,12},{12,8},{16,20},{20,16},{24,28},{28,24},{1,5},{5... | collective-permute-start | bytes 884744 | tf_op jit(solution)/shard_map/ppermute | solution.py:566
  111.0 9.4 %collective-permute-start.40 = (bf16[192,768]{1,0:T(8,128)(2,1)S(1)}, bf16[192,768]{1,0:T(8,128)(2,1)S(1)}, u32[]{:S(2)}, u32[]{:S(2)}) collective-permute-start(bf16[192,768]{1,0:T(8,128)(2,1)S(1)} %get-tuple-element.284), channel_id=1, source_target_pairs={{0,4},{4,0},{8,12},{12,8},{16,20},{20,16},{24,28},{28,24},{1,5},{5... | collective-permute-start | bytes 884744 | tf_op jit(solution)/shard_map/ppermute | solution.py:566
  111.8 10.0 %collective-permute-start.41 = (bf16[192,768]{1,0:T(8,128)(2,1)S(1)}, bf16[192,768]{1,0:T(8,128)(2,1)S(1)}, u32[]{:S(2)}, u32[]{:S(2)}) collective-permute-start(bf16[192,768]{1,0:T(8,128)(2,1)S(1)} %add_convert_fusion.7), channel_id=1, source_target_pairs={{0,8},{4,12},{8,24},{12,28},{16,0},{20,4},{24,16},{28,20},{1,9},{5... | collective-permute-start | bytes 884744 | tf_op jit(solution)/shard_map/ppermute | solution.py:581
  112.1 9.6 %collective-permute-start.36 = (bf16[256,192]{1,0:T(8,128)(2,1)S(1)}, bf16[256,192]{1,0:T(8,128)(2,1)S(1)}, u32[]{:S(2)}, u32[]{:S(2)}) collective-permute-start(bf16[256,192]{1,0:T(8,128)(2,1)S(1)} %get-tuple-element.277), channel_id=1, source_target_pairs={{0,2},{1,3},{2,0},{3,1},{4,6},{5,7},{6,4},{7,5},{8,10},{9,11},{10,... | collective-permute-start | bytes 294920 | tf_op jit(solution)/shard_map/ppermute | solution.py:551
  114.6 19.8 %collective-permute-start.43 = (f32[3,768]{1,0:T(4,128)S(1)}, f32[3,768]{1,0:T(4,128)S(1)}, u32[]{:S(2)}, u32[]{:S(2)}) collective-permute-start(f32[3,768]{1,0:T(4,128)S(1)} %get-tuple-element.289), channel_id=1, source_target_pairs={{0,1},{1,0},{2,3},{3,2},{4,5},{5,4},{6,7},{7,6},{8,9},{9,8},{10,11... | collective-permute-start | bytes 27656 | tf_op jit(solution)/shard_map/ppermute | solution.py:551
  121.8 12.6 %collective-permute-start.42 = (bf16[1,768,192]{2,1,0:T(8,128)(2,1)S(1)}, bf16[1,768,192]{2,1,0:T(8,128)(2,1)S(1)}, u32[]{:S(2)}, u32[]{:S(2)}) collective-permute-start(bf16[1,768,192]{2,1,0:T(8,128)(2,1)S(1)} %slice.86), channel_id=1, source_target_pairs={{0,2},{1,3},{2,0},{3,1},{4,6},{5,7},{6,4},{7,5},{8,10},{9,11},{10,... | collective-permute-start | bytes 884744 | tf_op jit(solution)/shard_map/ppermute | solution.py:551
  123.4 11.0 %collective-permute-start.45 = (bf16[192,768]{1,0:T(8,128)(2,1)S(1)}, bf16[192,768]{1,0:T(8,128)(2,1)S(1)}, u32[]{:S(2)}, u32[]{:S(2)}) collective-permute-start(bf16[192,768]{1,0:T(8,128)(2,1)S(1)} %add_convert_fusion.6), channel_id=1, source_target_pairs={{0,8},{4,12},{8,24},{12,28},{16,0},{20,4},{24,16},{28,20},{1,9},{5... | collective-permute-start | bytes 884744 | tf_op jit(solution)/shard_map/ppermute | solution.py:581
  123.7 10.7 %collective-permute-start.44 = (bf16[192,768]{1,0:T(8,128)(2,1)S(1)}, bf16[192,768]{1,0:T(8,128)(2,1)S(1)}, u32[]{:S(2)}, u32[]{:S(2)}) collective-permute-start(bf16[192,768]{1,0:T(8,128)(2,1)S(1)} %get-tuple-element.295), channel_id=1, source_target_pairs={{0,4},{4,0},{8,12},{12,8},{16,20},{20,16},{24,28},{28,24},{1,5},{5... | collective-permute-start | bytes 884744 | tf_op jit(solution)/shard_map/ppermute | solution.py:566
  141.9 14.0 %collective-permute-start.53 = (bf16[256,768]{1,0:T(8,128)(2,1)S(1)}, bf16[256,768]{1,0:T(8,128)(2,1)S(1)}, u32[]{:S(2)}, u32[]{:S(2)}) collective-permute-start(bf16[256,768]{1,0:T(8,128)(2,1)S(1)} %add_convert_fusion.1), channel_id=1, source_target_pairs={{0,2},{1,3},{2,0},{3,1},{4,6},{5,7},{6,4},{7,5},{8,10},{9,11},{10,... | collective-permute-start | bytes 1179656 | tf_op jit(solution)/shard_map/ppermute | solution.py:551
  145.8 8.8 %collective-permute-start.54 = (f32[1,3,768]{2,1,0:T(4,128)S(1)}, f32[1,3,768]{2,1,0:T(4,128)S(1)}, u32[]{:S(2)}, u32[]{:S(2)}) collective-permute-start(f32[1,3,768]{2,1,0:T(4,128)S(1)} %get-tuple-element.349), channel_id=1, source_target_pairs={{0,4},{4,0},{8,12},{12,8},{16,20},{20,16},{24,28},{28,24},{1,5},{5... | collective-permute-start | bytes 27656 | tf_op jit(solution)/shard_map/ppermute | solution.py:620
  152.3 10.4 %collective-permute-start.55 = (bf16[192,768]{1,0:T(8,128)(2,1)S(1)}, bf16[192,768]{1,0:T(8,128)(2,1)S(1)}, u32[]{:S(2)}, u32[]{:S(2)}) collective-permute-start(bf16[192,768]{1,0:T(8,128)(2,1)S(1)} %add_convert_fusion.5), channel_id=1, source_target_pairs={{0,8},{4,12},{8,24},{12,28},{16,0},{20,4},{24,16},{28,20},{1,9},{5... | collective-permute-start | bytes 884744 | tf_op jit(solution)/shard_map/ppermute | solution.py:581
  155.9 12.7 %collective-permute-start.59 = (bf16[256,768]{1,0:T(8,128)(2,1)S(1)}, bf16[256,768]{1,0:T(8,128)(2,1)S(1)}, u32[]{:S(2)}, u32[]{:S(2)}) collective-permute-start(bf16[256,768]{1,0:T(8,128)(2,1)S(1)} %add_convert_fusion.2), channel_id=1, source_target_pairs={{0,2},{1,3},{2,0},{3,1},{4,6},{5,7},{6,4},{7,5},{8,10},{9,11},{10,... | collective-permute-start | bytes 1179656 | tf_op jit(solution)/shard_map/ppermute | solution.py:551
  158.2 8.7 %collective-permute-start.66 = (f32[2,3,768]{2,1,0:T(4,128)S(1)}, f32[2,3,768]{2,1,0:T(4,128)S(1)}, u32[]{:S(2)}, u32[]{:S(2)}) collective-permute-start(f32[2,3,768]{2,1,0:T(4,128)S(1)} %maximum_select_fusion.4), channel_id=1, source_target_pairs={{0,8},{4,12},{8,0},{12,4},{16,24},{20,28},{24,16},{28,20},{1,9},{5... | collective-permute-start | bytes 55304 | tf_op jit(solution)/shard_map/ppermute | solution.py:620
  (48 other events, 286.3 us)
